TPU v7x, 256 devices: a whole 4x4x8 slice. The times are simulated.
256 devices in a mesh: dp: 16 (over x_hi, y, core), tensor: 16 (over z, x_lo).
Axes of the slice: x: 4 (x_hi: 2, x_lo: 2; x = x_hi * 2 + x_lo), y: 4, z: 8, core: 2. Of those that a mesh axis runs over, the one named last changes fastest.
Arguments:
- out_grad: bfloat16 [8192, 4096], P('dp', 'tensor'), may hold values from -6 to 6
- gate_act: bfloat16 [8192, 14336], P('dp', 'tensor'), may hold values from -8 to 8
- up_act: bfloat16 [8192, 14336], P('dp', 'tensor'), may hold values from -6 to 6
- w_down: bfloat16 [4096, 14336], P('dp', 'tensor'), may hold values from -0.09375 to 0.09375
Outputs:
- gate_grad: bfloat16 [8192, 14336], P('dp', 'tensor')
- up_grad: bfloat16 [8192, 14336], P('dp', 'tensor')
- down_grad: bfloat16 [4096, 14336], P('dp', 'tensor')
All inputs are finite; a program needn't handle non-finite values.
Results may differ from a plain program's by a relative error of at most 0.0049.
Values may be sent and summed in bfloat16 or wider, within the bound.
A program may use at most 128 MiB of HBM per device.

v0:
```python
import math

import jax
import jax.numpy as jnp
from jax import lax
from jax.sharding import PartitionSpec as P


def weight_total(rows_all, hidden):
    return lax.psum_scatter(
        lax.dot_general(
            rows_all, hidden, (((0,), (0,)), ((), ())), preferred_element_type=jnp.float32
        ),
        "dp",
        scatter_dimension=0,
        tiled=True,
    )


def body(out_grad, gate_act, up_act, w_down):
    seq_rows = gate_act.shape[0]
    grad_scale = 1.0 / math.sqrt(seq_rows * lax.axis_size("dp"))
    gate_wide = gate_act.astype(jnp.float32)
    up_wide = up_act.astype(jnp.float32)
    sigmoid_gate = jax.nn.sigmoid(gate_wide)
    activated = gate_wide * sigmoid_gate
    hidden = (activated * up_wide).astype(jnp.bfloat16)
    rows_all = lax.all_gather(out_grad, "tensor", axis=1, tiled=True)
    hidden_grad = jnp.dot(
        rows_all,
        lax.all_gather(w_down, "dp", axis=0, tiled=True),
        preferred_element_type=jnp.float32,
    )
    summed = weight_total(rows_all, hidden)
    gate_grad = (
        hidden_grad * up_wide * sigmoid_gate * (1.0 + gate_wide * (1.0 - sigmoid_gate))
    ).astype(jnp.bfloat16)
    up_grad = (hidden_grad * activated).astype(jnp.bfloat16)
    down_grad = (summed * grad_scale).astype(jnp.bfloat16)
    return (gate_grad, up_grad, down_grad)


def solution(mesh):
    placed = (P("dp", "tensor"), P("dp", "tensor"), P("dp", "tensor"), P("dp", "tensor"))
    return jax.shard_map(
        body,
        mesh=mesh,
        in_specs=placed,
        out_specs=(P("dp", "tensor"), P("dp", "tensor"), P("dp", "tensor")),
        check_vma=False,
    )
```

profile of v0, /device:TPU:26, one launch (start us, length us, event | category | flops | bytes accessed | tf_op | source)
XLA Modules:
  0.0 358.8 jit_solution(15101293496528034004)
XLA Ops:
  7.2 0.0 all-gather.3.cloned.1.call-start
  7.2 0.7 all-gather.3.cloned.1.call-update
  7.9 0.0 all-gather.5.cloned.1.call-start
  7.9 0.7 all-gather.5.cloned.1.call-update
  8.6 0.0 reduce-scatter.2.cloned.1.call-start
  8.7 120.9 %all-gather.3.cloned.1.call-done = bf16[512,4096]{1,0:T(8,128)(2,1)} async-done(((bf16[512,256]{1,0:T(8,128)(2,1)}), bf16[512,4096]{1,0:T(8,128)(2,1)}) %all-gather.3.cloned.1.call-update) | async-done | bytes 4194320 | tf_op jit(solution)/shard_map/all_gather | solution.py:28
  129.6 12.1 %convolution_bitcast_fusion = f32[4096,896]{0,1:T(8,128)} fusion(bf16[512,4096]{1,0:T(8,128)(2,1)} %all-gather.3.cloned.1.call-done, bf16[512,896]{1,0:T(8,128)(2,1)} %param.6, bf16[512,896]{1,0:T(8,128)(2,1)} %param.5), kind=kOutput, calls=%fused_computation | convolution fusion | flops 3761766400 | bytes 20709376 | tf_op jit(solution)/shard_map/dot_general | solution.py:11
  141.6 0.0 copy-start
  141.6 0.0 copy-start.1
  141.6 0.0 reduce-scatter.2.cloned.1.call-update
  141.7 65.0 %all-gather.5.cloned.1.call-done = bf16[4096,896]{1,0:T(8,128)(2,1)} async-done(((bf16[256,896]{1,0:T(8,128)(2,1)}), bf16[4096,896]{1,0:T(8,128)(2,1)}) %all-gather.5.cloned.1.call-update) | async-done | bytes 7340048 | tf_op jit(solution)/shard_map/all_gather | solution.py:31
  206.6 0.0 copy-done
  206.6 0.0 copy-done.1
  206.6 10.5 %multiply_convert_fusion = (bf16[512,896]{1,0:T(8,128)(2,1)}, bf16[512,896]{1,0:T(8,128)(2,1)}) fusion(bf16[512,896]{1,0:T(8,128)(2,1)S(1)} %copy-done, bf16[512,896]{1,0:T(8,128)(2,1)S(1)} %copy-done.1, bf16[512,4096]{1,0:T(8,128)(2,1)} %all-gather.3.cloned.1.call-done, bf16[4096,896]{1,0:T(8,128)(2,1)} %all-gather.5.cloned.1.call-done), kind=kOutput, calls=%fused_computation.14 | convolution fusion | flops 3764977664 | bytes 15204352 | tf_op jit(solution)/shard_map/dot_general | solution.py:29
  217.2 132.8 %reduce-scatter.2.cloned.1.call-done = f32[256,896]{0,1:T(8,128)} async-done(((f32[4096,896]{0,1:T(8,128)}), f32[256,896]{0,1:T(8,128)}) %reduce-scatter.2.cloned.1.call-update) | async-done | bytes 917520 | tf_op jit(solution)/shard_map/reduce_scatter | solution.py:10
  350.0 1.3 multiply_convert_fusion.1
  351.3 1.0 copy.7
Async XLA Ops:
  7.2 122.4 %all-gather.3.cloned.1.call-start = ((), (), s32[]{:S(2)}) async-start(), calls=%async_computation.1 | async-start | bytes 4456448 | tf_op jit(solution)/shard_map/all_gather | solution.py:28
  7.9 198.7 %all-gather.5.cloned.1.call-start = ((), (), s32[]{:S(2)}) async-start(), calls=%async_computation.2 | async-start | bytes 7798784 | tf_op jit(solution)/shard_map/all_gather | solution.py:31
  8.6 341.4 %reduce-scatter.2.cloned.1.call-start = ((), (), s32[]{:S(2)}) async-start(), calls=%async_computation.3 | async-start | bytes 15597568 | tf_op jit(solution)/shard_map/reduce_scatter | solution.py:10
  141.6 65.0 %copy-start = (bf16[512,896]{1,0:T(8,128)(2,1)S(1)}, bf16[512,896]{1,0:T(8,128)(2,1)}, u32[]{:S(2)}) copy-start(bf16[512,896]{1,0:T(8,128)(2,1)} %param.5) | copy-start | bytes 2752516
  141.6 65.0 %copy-start.1 = (bf16[512,896]{1,0:T(8,128)(2,1)S(1)}, bf16[512,896]{1,0:T(8,128)(2,1)}, u32[]{:S(2)}) copy-start(bf16[512,896]{1,0:T(8,128)(2,1)} %param.6) | copy-start | bytes 2752516
Sparse Core Ops, SparseCore 0:
  9.7 119.7 all-gather.2
  132.3 74.2 all-gather.4
  211.2 138.7 reduce-scatter.1
where the time goes:
time: 361 us; the launch traced here: 359 us
  waiting for transfers between devices  320 us (89%)
  matrix products  22.6 us (6%)
  between operations  13.7 us (4%)
    reduce_scatter x1, waiting for transfers between devices, weight_total(): lax.psum_scatter(lax.dot_general(rows_all, hidden, (((0,), (0,)), ((), ()...  133 us
    all_gather x1, waiting for transfers between devices, body(): rows_all = lax.all_gather(out_grad, 'tensor', axis=1, tiled=True)  121 us
    all_gather x1, waiting for transfers between devices, body(): lax.all_gather(w_down, 'dp', axis=0, tiled=True)  65 us
    dot_general x1, matrix products, weight_total(): lax.dot_general(rows_all, hidden, (((0,), (0,)), ((), ())), preferred_ele...  12.1 us
    dot_general x1, matrix products, body(): jnp.dot(rows_all, lax.all_gather(w_down, 'dp', axis=0, tiled=True), prefe...  10.5 us
  transfers between devices with their start and end apart: 3, of which 3 were waited for; matrix products, arithmetic and copies ran while one was open for 6% of the time, Pallas kernels for 0%

commit v1 on v0

v1 whole, which is shorter than its diff:
```python
import math

import jax
import jax.numpy as jnp
import numpy as np
from jax import lax
from jax.sharding import Mesh
from jax.sharding import PartitionSpec as P


def body(out_grad, gate_act, up_act, w_down):
    seq_rows = gate_act.shape[0]
    n_chip = lax.axis_size("chip")
    n_core = lax.axis_size("core")
    width = w_down.shape[0]
    grad_scale = 1.0 / math.sqrt(seq_rows * n_chip * n_core)
    gate_wide = gate_act.astype(jnp.float32)
    up_wide = up_act.astype(jnp.float32)
    sigmoid_gate = jax.nn.sigmoid(gate_wide)
    activated = gate_wide * sigmoid_gate
    hidden = (activated * up_wide).astype(jnp.bfloat16)

    rows_all = lax.all_gather(out_grad, "tensor", axis=1, tiled=True)
    rows4 = rows_all.reshape(seq_rows, n_chip, n_core, width)
    w_chips = lax.all_gather(w_down, "chip", axis=0, tiled=False)
    w_full = lax.all_gather(w_chips, "core", axis=0, tiled=False)
    hidden_grad = jnp.einsum(
        "trck,crkf->tf", rows4, w_full, preferred_element_type=jnp.float32
    )

    rows_pair = lax.all_to_all(rows4, "core", 2, 0, tiled=True)
    hidden_pair = lax.all_gather(hidden, "core", axis=0, tiled=True)
    partial = jnp.einsum(
        "trk,tf->rkf",
        rows_pair.reshape(n_core * seq_rows, n_chip, width),
        hidden_pair,
        preferred_element_type=jnp.float32,
    )
    summed = lax.psum_scatter(partial, "chip", scatter_dimension=0, tiled=False)

    gate_grad = (
        hidden_grad * up_wide * sigmoid_gate * (1.0 + gate_wide * (1.0 - sigmoid_gate))
    ).astype(jnp.bfloat16)
    up_grad = (hidden_grad * activated).astype(jnp.bfloat16)
    down_grad = (summed * grad_scale).astype(jnp.bfloat16)
    return (gate_grad, up_grad, down_grad)


def solution(mesh):
    n_dp = mesh.shape["dp"]
    n_tensor = mesh.shape["tensor"]
    devices = np.asarray(mesh.devices).reshape(n_dp // 2, 2, n_tensor)
    split = Mesh(devices, ("chip", "core", "tensor"))
    placed = P(("chip", "core"), "tensor")
    return jax.shard_map(
        body,
        mesh=split,
        in_specs=(placed, placed, placed, placed),
        out_specs=(placed, placed, placed),
        check_vma=False,
    )
```

time: 361 us -> 371 us (1.028)
  local copies, waits for them, and re-layouts: 0.98 us -> 12 us
  blocking collectives: 0 us -> 8.16 us
  waiting for transfers between devices: 320 us -> 312 us
    all_gather x1 -> x3, waiting for transfers between devices: 65 us -> 98.8 us  [the longest x1 72.8 us: body(): w_chips = lax.all_gather(w_down, 'chip', axis=0, tiled=False)]
    reduce_scatter x1, waiting for transfers between devices: 133 us -> 111 us  [body(): summed = lax.psum_scatter(partial, 'chip', scatter_dimension=0, tiled=False)]
    all_gather x1, waiting for transfers between devices: 121 us -> 102 us  [body(): rows_all = lax.all_gather(out_grad, 'tensor', axis=1, tiled=True)]
    reshape x0 -> x2, local copies, waits for them, and re-layouts: none -> 9.19 us  [the longest x1 6.59 us: body(): rows_pair.reshape(n_core * seq_rows, n_chip, width)]
    all_to_all x0 -> x1, blocking collectives: none -> 8.16 us  [body(): rows_pair = lax.all_to_all(rows4, 'core', 2, 0, tiled=True)]
  transfers between devices with their start and end apart: 3 -> 5, of which waited for: 3 -> 4; matrix products, arithmetic and copies ran while one was open for 6% -> 3% of each run, Pallas kernels for 0% -> 0%
where the time goes in v1:
time: 371 us; the launch traced here: 368 us
  waiting for transfers between devices  312 us (84%)
  matrix products  20.8 us (6%)
  between operations  13.8 us (4%)
  local copies, waits for them, and re-layouts  12 us (3%)
  blocking collectives  8.16 us (2%)
    reduce_scatter x1, waiting for transfers between devices, body(): summed = lax.psum_scatter(partial, 'chip', scatter_dimension=0, tiled=False)  111 us
    all_gather x1, waiting for transfers between devices, body(): rows_all = lax.all_gather(out_grad, 'tensor', axis=1, tiled=True)  102 us
    all_gather x1, waiting for transfers between devices, body(): w_chips = lax.all_gather(w_down, 'chip', axis=0, tiled=False)  72.8 us
    all_gather x1, waiting for transfers between devices, body(): w_full = lax.all_gather(w_chips, 'core', axis=0, tiled=False)  26 us
    dot_general x1, matrix products, body(): jnp.einsum('trck,crkf->tf', rows4, w_full, preferred_element_type=jnp.flo...  11.1 us
    dot_general x1, matrix products, body(): jnp.einsum('trk,tf->rkf', rows_pair.reshape(n_core * seq_rows, n_chip, wi...  9.7 us
    all_to_all x1, blocking collectives, body(): rows_pair = lax.all_to_all(rows4, 'core', 2, 0, tiled=True)  8.16 us
  transfers between devices with their start and end apart: 5, of which 4 were waited for; matrix products, arithmetic and copies ran while one was open for 3% of the time, Pallas kernels for 0%

profile of v1, /device:TPU:26, one launch (start us, length us, event | category | flops | bytes accessed | tf_op | source)
XLA Modules:
  0.0 368.4 jit_solution(12000181678262862470)
XLA Ops:
  7.2 0.0 all-gather.11.cloned.1.call-start
  7.2 0.7 all-gather.11.cloned.1.call-update
  7.9 0.0 all-gather.7.cloned.1.call-start
  7.9 1.8 copy.15
  9.7 0.0 all-gather.7.cloned.1.call-update
  9.8 0.0 all-gather.13.cloned.1.call-start
  9.8 72.8 %all-gather.11.cloned.1.call-done = bf16[2048,896]{1,0:T(8,128)(2,1)} async-done(((bf16[256,896]{1,0:T(8,128)(2,1)}), bf16[2048,896]{1,0:T(8,128)(2,1)}) %all-gather.11.cloned.1.call-update) | async-done | bytes 3670032 | tf_op jit(solution)/shard_map/all_gather | solution.py:25
  82.6 0.0 copy-start
  82.6 0.0 copy-start.1
  82.6 0.0 all-gather.13.cloned.1.call-update
  82.6 0.0 all-gather.9.cloned.1.call-start
  82.6 101.7 %all-gather.7.cloned.1.call-done = bf16[512,4096]{0,1:T(8,128)(2,1)} async-done(((bf16[512,256]{0,1:T(8,128)(2,1)}), bf16[512,4096]{0,1:T(8,128)(2,1)}) %all-gather.7.cloned.1.call-update) | async-done | bytes 4194320 | tf_op jit(solution)/shard_map/all_gather | solution.py:23
  184.4 26.0 %all-gather.13.cloned.1.call-done = bf16[16,256,896]{2,1,0:T(8,128)(2,1)} async-done(((bf16[8,256,896]{2,1,0:T(8,128)(2,1)}), bf16[16,256,896]{2,1,0:T(8,128)(2,1)}) %all-gather.13.cloned.1.call-update) | async-done | bytes 7340048 | tf_op jit(solution)/shard_map/all_gather | solution.py:26
  210.4 0.0 copy-done
  210.4 0.0 copy-done.1
  210.4 11.1 %fusion.9 = (bf16[512,896]{1,0:T(8,128)(2,1)}, bf16[512,896]{1,0:T(8,128)(2,1)}, bf16[512,896]{1,0:T(8,128)(2,1)}) fusion(bf16[512,896]{1,0:T(8,128)(2,1)S(1)} %copy-done, bf16[512,896]{1,0:T(8,128)(2,1)S(1)} %copy-done.1, bf16[2,8,256,896]{3,2,1,0:T(8,128)(2,1)} %bitcast.27, bf16[512,8,2,256]{0,3,2,1:T(8,128)(2,1)} %bitcast.23), kind=kOutput, calls=%fused_computation.16 | convolution fusion | flops 3765895168 | bytes 16121856 | tf_op jit(solution)/shard_map/trck,crkf->tf/dot_general | solution.py:27
  221.5 0.0 all-gather.9.cloned.1.call-update
  221.5 0.0 reduce-scatter.2.cloned.1.call-start
  221.6 2.6 copy.22
  224.2 8.2 %all_to_all.15 = bf16[512,8,2,256]{0,3,1,2:T(8,128)(2,1)} all-to-all(bf16[512,8,2,256]{0,3,1,2:T(8,128)(2,1)S(1)} %copy.22), channel_id=1, replica_groups=mesh['chip'=8,'core'=2,'tensor'=16] {'core'}, dimensions={2} | all-to-all | bytes 8388608 | tf_op jit(solution)/shard_map/all_to_all | solution.py:31
  232.3 6.6 %copy.27 = bf16[512,8,2,256]{3,0,2,1:T(8,128)(2,1)} copy(bf16[512,8,2,256]{0,3,1,2:T(8,128)(2,1)} %all_to_all.15) | data formatting | bytes 8388608 | tf_op jit(solution)/shard_map/reshape | solution.py:35
  238.9 0.0 all-gather.9.cloned.1.call-done
  238.9 9.7 %convolution_bitcast_fusion = f32[8,256,896]{1,2,0:T(8,128)} fusion(bf16[1024,8,256]{2,0,1:T(8,128)(2,1)} %bitcast.25, bf16[1024,896]{1,0:T(8,128)(2,1)} %all-gather.9.cloned.1.call-done), kind=kOutput, calls=%fused_computation | convolution fusion | flops 3758096384 | bytes 13369344 | tf_op jit(solution)/shard_map/trk,tf->rkf/dot_general | solution.py:33
  248.6 0.0 reduce-scatter.2.cloned.1.call-update
  248.7 110.9 %reduce-scatter.2.cloned.1.call-done = f32[1,256,896]{1,2,0:T(8,128)} async-done(((f32[8,256,896]{1,2,0:T(8,128)}), f32[1,256,896]{1,2,0:T(8,128)}) %reduce-scatter.2.cloned.1.call-update) | async-done | bytes 917520 | tf_op jit(solution)/shard_map/reduce_scatter | solution.py:39
  359.6 1.3 fusion.10
  360.9 1.0 copy.21
Async XLA Ops:
  7.2 75.4 %all-gather.11.cloned.1.call-start = ((), (), s32[]{:S(2)}) async-start(), calls=%async_computation.5 | async-start | bytes 4128768 | tf_op jit(solution)/shard_map/all_gather | solution.py:25
  7.9 176.5 %all-gather.7.cloned.1.call-start = ((), (), s32[]{:S(2)}) async-start(), calls=%async_computation.2 | async-start | bytes 4456448 | tf_op jit(solution)/shard_map/all_gather | solution.py:23
  9.8 200.6 %all-gather.13.cloned.1.call-start = ((), (), s32[]{:S(2)}) async-start(), calls=%async_computation.6 | async-start | bytes 11010048 | tf_op jit(solution)/shard_map/all_gather | solution.py:26
  82.6 127.8 %copy-start = (bf16[512,896]{1,0:T(8,128)(2,1)S(1)}, bf16[512,896]{1,0:T(8,128)(2,1)}, u32[]{:S(2)}) copy-start(bf16[512,896]{1,0:T(8,128)(2,1)} %param.5) | copy-start | bytes 2752516
  82.6 127.8 %copy-start.1 = (bf16[512,896]{1,0:T(8,128)(2,1)S(1)}, bf16[512,896]{1,0:T(8,128)(2,1)}, u32[]{:S(2)}) copy-start(bf16[512,896]{1,0:T(8,128)(2,1)} %param.6) | copy-start | bytes 2752516
  82.6 156.3 %all-gather.9.cloned.1.call-start = ((), (), s32[]{:S(2)}) async-start(), calls=%async_computation.3 | async-start | bytes 2752512 | tf_op jit(solution)/shard_map/all_gather | solution.py:32
  221.5 138.1 %reduce-scatter.2.cloned.1.call-start = ((), (), s32[]{:S(2)}) async-start(), calls=%async_computation.4 | async-start | bytes 8257536 | tf_op jit(solution)/shard_map/reduce_scatter | solution.py:39
Sparse Core Ops, SparseCore 0:
  10.6 71.9 all-gather.10
  84.9 99.3 all-gather.6
  186.2 24.1 all-gather.12
  221.6 16.8 all-gather.8
  248.8 110.7 reduce-scatter.1

commit v2 on v1

v2 whole, which is shorter than its diff:
```python
import math

import jax
import jax.numpy as jnp
import numpy as np
from jax import lax
from jax.experimental import pallas as pl
from jax.experimental.pallas import tpu as pltpu
from jax.sharding import Mesh
from jax.sharding import PartitionSpec as P

MESH = pl.DeviceIdType.MESH
ANY = pl.BlockSpec(memory_space=pl.ANY)


def _where():
    return lax.axis_index("chip"), lax.axis_index("core"), lax.axis_index("tensor")


def _gather_kernel(n_chip, n_core, n_ten, og_ref, w_ref, rows_out, w_out,
                   r_send, r_recv, w_send, w_recv, own_sem):
    chip, core, ten = _where()
    barrier = pltpu.get_barrier_semaphore()
    for k in range(1, n_ten):
        pl.semaphore_signal(barrier, inc=1, device_id=(chip, core, (ten + k) % n_ten),
                            device_id_type=MESH)
    for k in range(1, n_chip):
        pl.semaphore_signal(barrier, inc=1, device_id=((chip + k) % n_chip, core, ten),
                            device_id_type=MESH)
    pl.semaphore_wait(barrier, (n_ten - 1) + (n_chip - 1))

    rows_slot = rows_out.at[ten % n_core, ten // n_core]
    own_r = pltpu.make_async_copy(og_ref, rows_slot, own_sem.at[0])
    own_w = pltpu.make_async_copy(w_ref, w_out.at[chip], own_sem.at[1])
    own_r.start()
    own_w.start()
    copies = []
    for k in range(1, n_ten):
        cp = pltpu.make_async_remote_copy(
            og_ref, rows_slot, r_send.at[k], r_recv.at[k],
            device_id=(chip, core, (ten + k) % n_ten), device_id_type=MESH)
        cp.start()
        copies.append(cp)
    for k in range(1, n_chip):
        cp = pltpu.make_async_remote_copy(
            w_ref, w_out.at[chip], w_send.at[k], w_recv.at[k],
            device_id=((chip + k) % n_chip, core, ten), device_id_type=MESH)
        cp.start()
        copies.append(cp)
    own_r.wait()
    own_w.wait()
    for cp in copies:
        cp.wait_send()
        cp.wait_recv()


def _pair_kernel(n_core, w_ref, rows_ref, hid_ref, w_other, rows_other, hid_other,
                 send, recv):
    chip, core, ten = _where()
    other = (chip, 1 - core, ten)
    barrier = pltpu.get_barrier_semaphore()
    pl.semaphore_signal(barrier, inc=1, device_id=other, device_id_type=MESH)
    pl.semaphore_wait(barrier, 1)
    copies = [
        pltpu.make_async_remote_copy(w_ref, w_other, send.at[0], recv.at[0],
                                     device_id=other, device_id_type=MESH),
        pltpu.make_async_remote_copy(rows_ref.at[1 - core], rows_other, send.at[1],
                                     recv.at[1], device_id=other, device_id_type=MESH),
        pltpu.make_async_remote_copy(hid_ref, hid_other, send.at[2], recv.at[2],
                                     device_id=other, device_id_type=MESH),
    ]
    for cp in copies:
        cp.start()
    for cp in copies:
        cp.wait_send()
        cp.wait_recv()


def _scatter_kernel(n_chip, part_ref, recv_out, send, recv, own_sem):
    chip, core, ten = _where()
    barrier = pltpu.get_barrier_semaphore()
    for k in range(1, n_chip):
        pl.semaphore_signal(barrier, inc=1, device_id=((chip + k) % n_chip, core, ten),
                            device_id_type=MESH)
    pl.semaphore_wait(barrier, n_chip - 1)
    own = pltpu.make_async_copy(part_ref.at[chip], recv_out.at[chip], own_sem.at[0])
    own.start()
    copies = []
    for k in range(1, n_chip):
        dest = (chip + k) % n_chip
        cp = pltpu.make_async_remote_copy(
            part_ref.at[dest], recv_out.at[chip], send.at[k], recv.at[k],
            device_id=(dest, core, ten), device_id_type=MESH)
        cp.start()
        copies.append(cp)
    own.wait()
    for cp in copies:
        cp.wait_send()
        cp.wait_recv()


def _params(cid):
    return pltpu.CompilerParams(collective_id=cid, has_side_effects=True)


def body(out_grad, gate_act, up_act, w_down):
    seq_rows, ff = gate_act.shape
    width = w_down.shape[0]
    n_chip = lax.axis_size("chip")
    n_core = lax.axis_size("core")
    n_ten = lax.axis_size("tensor")
    core = lax.axis_index("core")
    grad_scale = 1.0 / math.sqrt(seq_rows * n_chip * n_core)
    gate_wide = gate_act.astype(jnp.float32)
    up_wide = up_act.astype(jnp.float32)
    sigmoid_gate = jax.nn.sigmoid(gate_wide)
    activated = gate_wide * sigmoid_gate
    hidden = (activated * up_wide).astype(jnp.bfloat16)

    rows_g, w_own = pl.pallas_call(
        lambda *refs: _gather_kernel(n_chip, n_core, n_ten, *refs),
        out_shape=(
            jax.ShapeDtypeStruct((n_core, n_chip, seq_rows, out_grad.shape[1]), out_grad.dtype),
            jax.ShapeDtypeStruct((n_chip, width, ff), w_down.dtype),
        ),
        in_specs=[ANY, ANY],
        out_specs=(ANY, ANY),
        scratch_shapes=[pltpu.SemaphoreType.DMA((n_ten,)), pltpu.SemaphoreType.DMA((n_ten,)),
                        pltpu.SemaphoreType.DMA((n_chip,)), pltpu.SemaphoreType.DMA((n_chip,)),
                        pltpu.SemaphoreType.DMA((2,))],
        compiler_params=_params(0),
    )(out_grad, w_down)

    w_other, rows_other, hidden_other = pl.pallas_call(
        lambda *refs: _pair_kernel(n_core, *refs),
        out_shape=(
            jax.ShapeDtypeStruct(w_own.shape, w_own.dtype),
            jax.ShapeDtypeStruct(rows_g.shape[1:], rows_g.dtype),
            jax.ShapeDtypeStruct(hidden.shape, hidden.dtype),
        ),
        in_specs=[ANY, ANY, ANY],
        out_specs=(ANY, ANY, ANY),
        scratch_shapes=[pltpu.SemaphoreType.DMA((3,)), pltpu.SemaphoreType.DMA((3,))],
        compiler_params=_params(1),
    )(w_own, rows_g, hidden)

    rows_mine = lax.dynamic_index_in_dim(rows_g, core, 0, keepdims=False)
    rows_theirs = lax.dynamic_index_in_dim(rows_g, 1 - core, 0, keepdims=False)
    hidden_grad = jnp.einsum(
        "rtk,rkf->tf", rows_mine, w_own, preferred_element_type=jnp.float32
    ) + jnp.einsum("rtk,rkf->tf", rows_theirs, w_other, preferred_element_type=jnp.float32)

    partial = jnp.einsum(
        "rtk,tf->rkf", rows_mine, hidden, preferred_element_type=jnp.float32
    ) + jnp.einsum("rtk,tf->rkf", rows_other, hidden_other, preferred_element_type=jnp.float32)

    received = pl.pallas_call(
        lambda *refs: _scatter_kernel(n_chip, *refs),
        out_shape=jax.ShapeDtypeStruct(partial.shape, partial.dtype),
        in_specs=[ANY],
        out_specs=ANY,
        scratch_shapes=[pltpu.SemaphoreType.DMA((n_chip,)), pltpu.SemaphoreType.DMA((n_chip,)),
                        pltpu.SemaphoreType.DMA((1,))],
        compiler_params=_params(2),
    )(partial)
    summed = jnp.sum(received, axis=0)

    gate_grad = (
        hidden_grad * up_wide * sigmoid_gate * (1.0 + gate_wide * (1.0 - sigmoid_gate))
    ).astype(jnp.bfloat16)
    up_grad = (hidden_grad * activated).astype(jnp.bfloat16)
    down_grad = (summed * grad_scale).astype(jnp.bfloat16)
    return (gate_grad, up_grad, down_grad)


def solution(mesh):
    n_dp = mesh.shape["dp"]
    n_tensor = mesh.shape["tensor"]
    devices = np.asarray(mesh.devices).reshape(n_dp // 2, 2, n_tensor)
    split = Mesh(devices, ("chip", "core", "tensor"))
    placed = P(("chip", "core"), "tensor")
    return jax.shard_map(
        body,
        mesh=split,
        in_specs=(placed, placed, placed, placed),
        out_specs=(placed, placed, placed),
        check_vma=False,
    )
```

time: 371 us -> 261 us (0.70)
  waiting for transfers between devices: 312 us -> 0 us
  Pallas kernels: 0 us -> 234 us
  between operations: 13.8 us -> 0.74 us
  local copies, waits for them, and re-layouts: 12 us -> 0.26 us
  blocking collectives: 8.16 us -> 0 us
  other arithmetic: 1.26 us -> 7.35 us
  matrix products: 20.8 us -> 17 us
    pallas_call x0 -> x3, Pallas kernels: none -> 234 us  [the longest x1 120 us: body(): pl.pallas_call(lambda *refs: _scatter_kernel(n_chip, *refs), out_shape=ja...]
    all_gather x4 -> x0, waiting for transfers between devices: 200 us -> none  [the longest x1 102 us: body(): rows_all = lax.all_gather(out_grad, 'tensor', axis=1, tiled=True)]
    reduce_scatter x1 -> x0, waiting for transfers between devices: 111 us -> none  [body(): summed = lax.psum_scatter(partial, 'chip', scatter_dimension=0, tiled=False)]
    reshape x2 -> x0, local copies, waits for them, and re-layouts: 9.19 us -> none  [the longest x1 6.59 us: body(): rows_pair.reshape(n_core * seq_rows, n_chip, width)]
    all_to_all x1 -> x0, blocking collectives: 8.16 us -> none  [body(): rows_pair = lax.all_to_all(rows4, 'core', 2, 0, tiled=True)]
    dot_general x2 -> x4, matrix products: 20.8 us -> 17 us  [the longest x1 5.33 us: body(): jnp.einsum('rtk,tf->rkf', rows_other, hidden_other, preferred_element_typ...]
  transfers between devices with their start and end apart: 5 -> 0, of which waited for: 4 -> 0; matrix products, arithmetic and copies ran while one was open for 3% -> 0% of each run, Pallas kernels for 0% -> 0%
where the time goes in v2:
time: 261 us; the launch traced here: 260 us
  Pallas kernels  234 us (90%)
  matrix products  17 us (7%)
  other arithmetic  7.35 us (3%)
    pallas_call x1, Pallas kernels, body(): pl.pallas_call(lambda *refs: _scatter_kernel(n_chip, *refs), out_shape=ja...  120 us
    pallas_call x1, Pallas kernels, body(): pl.pallas_call(lambda *refs: _gather_kernel(n_chip, n_core, n_ten, *refs)...  103 us
    pallas_call x1, Pallas kernels, body(): pl.pallas_call(lambda *refs: _pair_kernel(n_core, *refs), out_shape=(jax....  11.3 us
    dot_general x1, matrix products, body(): jnp.einsum('rtk,tf->rkf', rows_other, hidden_other, preferred_element_typ...  5.33 us

profile of v2, /device:TPU:26, one launch (start us, length us, event | category | flops | bytes accessed | tf_op | source)
XLA Modules:
  0.0 259.8 jit_solution(12595487858506399686)
XLA Ops:
  0.6 3.0 %fusion.9.refs_2_ = bf16[512,896]{1,0:T(8,128)(2,1)} fusion(bf16[512,896]{1,0:T(8,128)(2,1)} %param.6, bf16[512,896]{1,0:T(8,128)(2,1)} %param.5), kind=kLoop, calls=%fused_computation.15 | loop fusion | flops 3670016 | bytes 2752512 | tf_op jit(solution)/shard_map/convert_element_type | solution.py:118
  3.6 103.0 %shard_map.67 = (bf16[2,8,512,256]{3,2,1,0:T(8,128)(2,1)}, bf16[8,256,896]{2,1,0:T(8,128)(2,1)}) custom-call(bf16[512,256]{1,0:T(8,128)(2,1)} %refs_0_.1, bf16[256,896]{1,0:T(8,128)(2,1)} %refs_1_.1), custom_call_target="tpu_custom_call" | custom-call | tf_op jit(solution)/shard_map/pallas_call | solution.py:120
  106.6 11.3 %shard_map.68 = (bf16[8,256,896]{2,1,0:T(8,128)(2,1)}, bf16[8,512,256]{2,1,0:T(8,128)(2,1)}, bf16[512,896]{1,0:T(8,128)(2,1)}) custom-call(bf16[8,256,896]{2,1,0:T(8,128)(2,1)} %get-tuple-element.9.refs_0_, bf16[2,8,512,256]{3,2,1,0:T(8,128)(2,1)} %get-tuple-element.8.refs_1_, bf16[512,896]{1,0:T(8,128)(2,1)} %fusion.9.refs_2_), custom_call_target="tpu_custom_call" | custom-call | tf_op jit(solution)/shard_map/pallas_call | solution.py:134
  117.8 0.0 copy-start
  117.9 0.0 copy-start.2
  117.9 0.0 copy-start.4
  117.9 0.0 copy-start.5
  117.9 5.1 %fusion = f32[512,896,1]{1,0,2:T(8,128)S(1)} fusion(bf16[8,256,896]{2,1,0:T(8,128)(2,1)} %get-tuple-element.10, bf16[2,8,512,256]{3,2,1,0:T(8,128)(2,1)} %get-tuple-element.8.refs_1_, s32[]{:T(128)S(6)} %select_n.8), kind=kOutput, calls=%fused_computation.6 | convolution fusion | flops 1879048192 | bytes 7602180 | tf_op jit(solution)/shard_map/rtk,rkf->tf/dot_general | solution.py:151
  123.0 0.0 copy-done
  123.1 0.0 copy-done.2
  123.1 0.0 copy-done.4
  123.1 0.2 copy-done.5
  123.3 0.0 copy-start.1
  123.3 4.1 %multiply_convert_fusion = (bf16[512,896]{1,0:T(8,128)(2,1)}, bf16[512,896]{1,0:T(8,128)(2,1)}) fusion(bf16[512,896]{1,0:T(8,128)(2,1)S(1)} %copy-done.4, bf16[512,896]{1,0:T(8,128)(2,1)S(1)} %copy-done.5, f32[512,896,1]{1,0,2:T(8,128)S(1)} %fusion, bf16[8,256,896]{2,1,0:T(8,128)(2,1)S(1)} %copy-done.2, bf16[2,8,512,256]{3,2,1,0:T(8,128)(2,1)S(1)} %copy-done, ...), kind=kOutput, calls=%fused_computation.24 | convolution fusion | flops 1886388224 | bytes 11272196 | tf_op jit(solution)/shard_map/rtk,rkf->tf/dot_general | solution.py:149
  127.4 0.0 copy-done.1
  127.4 0.0 copy-start.3
  127.4 0.0 copy-start.6
  127.4 2.4 fusion.2
  129.8 0.0 copy-done.3
  129.8 0.0 copy-done.6
  129.8 5.3 %convolution_add_fusion.refs_0_ = f32[8,256,896]{2,1,0:T(8,128)} fusion(f32[8,256,896]{2,1,0:T(8,128)S(1)} %fusion.2, bf16[8,512,256]{2,1,0:T(8,128)(2,1)S(1)} %copy-done.3, bf16[512,896]{1,0:T(8,128)(2,1)S(1)} %copy-done.6), kind=kOutput, calls=%fused_computation.3 | convolution fusion | flops 1880883200 | bytes 17694720 | tf_op jit(solution)/shard_map/rtk,tf->rkf/dot_general | solution.py:155
  135.2 120.2 %shard_map.69 = f32[8,256,896]{2,1,0:T(8,128)} custom-call(f32[8,256,896]{2,1,0:T(8,128)} %convolution_add_fusion.refs_0_), custom_call_target="tpu_custom_call" | custom-call | tf_op jit(solution)/shard_map/pallas_call | solution.py:157
  255.4 3.5 %reduce_sum.9 = f32[256,896]{1,0:T(8,128)S(1)} reduce(f32[8,256,896]{2,1,0:T(8,128)} %shard_map.69, f32[]{:T(128)} %constant.22.clone.1), dimensions={0}, to_apply=%region_0.1 | reduce | flops 1605632 | bytes 8257540 | tf_op jit(solution)/shard_map/reduce_sum | solution.py:166
  258.9 0.8 multiply_convert_fusion.1
Async XLA Ops:
  117.8 5.2 %copy-start = (bf16[2,8,512,256]{3,2,1,0:T(8,128)(2,1)S(1)}, bf16[2,8,512,256]{3,2,1,0:T(8,128)(2,1)}, u32[]{:S(2)}) copy-start(bf16[2,8,512,256]{3,2,1,0:T(8,128)(2,1)} %get-tuple-element.8.refs_1_) | copy-start | bytes 12582916
  117.9 5.2 %copy-start.2 = (bf16[8,256,896]{2,1,0:T(8,128)(2,1)S(1)}, bf16[8,256,896]{2,1,0:T(8,128)(2,1)}, u32[]{:S(2)}) copy-start(bf16[8,256,896]{2,1,0:T(8,128)(2,1)} %get-tuple-element.9.refs_0_) | copy-start | bytes 11010052
  117.9 5.2 %copy-start.4 = (bf16[512,896]{1,0:T(8,128)(2,1)S(1)}, bf16[512,896]{1,0:T(8,128)(2,1)}, u32[]{:S(2)}) copy-start(bf16[512,896]{1,0:T(8,128)(2,1)} %param.5) | copy-start | bytes 2752516
  117.9 5.4 %copy-start.5 = (bf16[512,896]{1,0:T(8,128)(2,1)S(1)}, bf16[512,896]{1,0:T(8,128)(2,1)}, u32[]{:S(2)}) copy-start(bf16[512,896]{1,0:T(8,128)(2,1)} %param.6) | copy-start | bytes 2752516
  123.3 4.1 %copy-start.1 = (bf16[512,896]{1,0:T(8,128)(2,1)S(1)}, bf16[512,896]{1,0:T(8,128)(2,1)}, u32[]{:S(2)}) copy-start(bf16[512,896]{1,0:T(8,128)(2,1)} %fusion.9.refs_2_) | copy-start | bytes 2752516
  127.4 2.4 copy-start.3
  127.4 2.4 copy-start.6

commit v3 on v2

--- a/solution.py
+++ b/solution.py
@@ -17,45 +17,77 @@
     return lax.axis_index("chip"), lax.axis_index("core"), lax.axis_index("tensor")
 
 
-def _gather_kernel(n_chip, n_core, n_ten, og_ref, w_ref, rows_out, w_out,
-                   r_send, r_recv, w_send, w_recv, own_sem):
+def _gather_kernel(n_chip, n_lo, og_ref, w_ref, rows_out, w_out,
+                   x_send, x_recv, r_send, r_recv, l_send, l_recv, w_send, w_recv, own_sem):
     chip, core, ten = _where()
+    n_plane = rows_out.shape[0]
+    plane, lo = ten // n_lo, ten % n_lo
+    right = ((plane + 1) % n_plane) * n_lo + lo
+    left = ((plane + n_plane - 1) % n_plane) * n_lo + lo
+    side = plane * n_lo + (1 - lo)
     barrier = pltpu.get_barrier_semaphore()
-    for k in range(1, n_ten):
-        pl.semaphore_signal(barrier, inc=1, device_id=(chip, core, (ten + k) % n_ten),
-                            device_id_type=MESH)
+    for t in (right, left, side):
+        pl.semaphore_signal(barrier, inc=1, device_id=(chip, core, t), device_id_type=MESH)
     for k in range(1, n_chip):
         pl.semaphore_signal(barrier, inc=1, device_id=((chip + k) % n_chip, core, ten),
                             device_id_type=MESH)
-    pl.semaphore_wait(barrier, (n_ten - 1) + (n_chip - 1))
-
-    rows_slot = rows_out.at[ten % n_core, ten // n_core]
-    own_r = pltpu.make_async_copy(og_ref, rows_slot, own_sem.at[0])
+    pl.semaphore_wait(barrier, 3 + (n_chip - 1))
+
+    own_r = pltpu.make_async_copy(og_ref, rows_out.at[plane, lo], own_sem.at[0])
     own_w = pltpu.make_async_copy(w_ref, w_out.at[chip], own_sem.at[1])
     own_r.start()
     own_w.start()
-    copies = []
-    for k in range(1, n_ten):
-        cp = pltpu.make_async_remote_copy(
-            og_ref, rows_slot, r_send.at[k], r_recv.at[k],
-            device_id=(chip, core, (ten + k) % n_ten), device_id_type=MESH)
-        cp.start()
-        copies.append(cp)
+    w_copies = []
     for k in range(1, n_chip):
         cp = pltpu.make_async_remote_copy(
             w_ref, w_out.at[chip], w_send.at[k], w_recv.at[k],
             device_id=((chip + k) % n_chip, core, ten), device_id_type=MESH)
         cp.start()
-        copies.append(cp)
+        w_copies.append(cp)
+    side_cp = pltpu.make_async_remote_copy(
+        og_ref, rows_out.at[plane, lo], x_send.at[0], x_recv.at[0],
+        device_id=(chip, core, side), device_id_type=MESH)
+    side_cp.start()
     own_r.wait()
+    side_cp.wait_send()
+    side_cp.wait_recv()
+
+    n_right = n_plane // 2
+    n_left = n_plane - 1 - n_right
+    ring = []
+    for s in range(max(n_right, n_left)):
+        if s < n_right:
+            src_plane = (plane + n_plane - s) % n_plane
+            cp = pltpu.make_async_remote_copy(
+                rows_out.at[src_plane], rows_out.at[src_plane], r_send.at[s], r_recv.at[s],
+                device_id=(chip, core, right), device_id_type=MESH)
+            ring.append(("r", s, cp))
+        if s < n_left:
+            src_plane = (plane + s) % n_plane
+            cp = pltpu.make_async_remote_copy(
+                rows_out.at[src_plane], rows_out.at[src_plane], l_send.at[s], l_recv.at[s],
+                device_id=(chip, core, left), device_id_type=MESH)
+            ring.append(("l", s, cp))
+    by = {(d, s): cp for d, s, cp in ring}
+    for s in range(max(n_right, n_left)):
+        for d, n in (("r", n_right), ("l", n_left)):
+            if s < n:
+                if s > 0:
+                    by[(d, s - 1)].wait_recv()
+                by[(d, s)].start()
+    for d, n in (("r", n_right), ("l", n_left)):
+        if n > 0:
+            by[(d, n - 1)].wait_recv()
+        for s in range(n):
+            by[(d, s)].wait_send()
     own_w.wait()
-    for cp in copies:
+    for cp in w_copies:
         cp.wait_send()
         cp.wait_recv()
 
 
-def _pair_kernel(n_core, w_ref, rows_ref, hid_ref, w_other, rows_other, hid_other,
-                 send, recv):
+def _pair_kernel(w_ref, rows_ref, hid_ref, w_other, rows_other, hid_other,
+                 send, recv, r_send, r_recv):
     chip, core, ten = _where()
     other = (chip, 1 - core, ten)
     barrier = pltpu.get_barrier_semaphore()
@@ -64,11 +96,13 @@
     copies = [
         pltpu.make_async_remote_copy(w_ref, w_other, send.at[0], recv.at[0],
                                      device_id=other, device_id_type=MESH),
-        pltpu.make_async_remote_copy(rows_ref.at[1 - core], rows_other, send.at[1],
-                                     recv.at[1], device_id=other, device_id_type=MESH),
-        pltpu.make_async_remote_copy(hid_ref, hid_other, send.at[2], recv.at[2],
+        pltpu.make_async_remote_copy(hid_ref, hid_other, send.at[1], recv.at[1],
                                      device_id=other, device_id_type=MESH),
     ]
+    for r in range(rows_ref.shape[0]):
+        copies.append(pltpu.make_async_remote_copy(
+            rows_ref.at[r, 1 - core], rows_other.at[r], r_send.at[r], r_recv.at[r],
+            device_id=other, device_id_type=MESH))
     for cp in copies:
         cp.start()
     for cp in copies:
@@ -117,35 +151,40 @@
     activated = gate_wide * sigmoid_gate
     hidden = (activated * up_wide).astype(jnp.bfloat16)
 
+    n_lo = n_core
+    n_plane = n_ten // n_lo
     rows_g, w_own = pl.pallas_call(
-        lambda *refs: _gather_kernel(n_chip, n_core, n_ten, *refs),
+        lambda *refs: _gather_kernel(n_chip, n_lo, *refs),
         out_shape=(
-            jax.ShapeDtypeStruct((n_core, n_chip, seq_rows, out_grad.shape[1]), out_grad.dtype),
+            jax.ShapeDtypeStruct((n_plane, n_lo, seq_rows, out_grad.shape[1]), out_grad.dtype),
             jax.ShapeDtypeStruct((n_chip, width, ff), w_down.dtype),
         ),
         in_specs=[ANY, ANY],
         out_specs=(ANY, ANY),
-        scratch_shapes=[pltpu.SemaphoreType.DMA((n_ten,)), pltpu.SemaphoreType.DMA((n_ten,)),
+        scratch_shapes=[pltpu.SemaphoreType.DMA((1,)), pltpu.SemaphoreType.DMA((1,)),
+                        pltpu.SemaphoreType.DMA((n_plane,)), pltpu.SemaphoreType.DMA((n_plane,)),
+                        pltpu.SemaphoreType.DMA((n_plane,)), pltpu.SemaphoreType.DMA((n_plane,)),
                         pltpu.SemaphoreType.DMA((n_chip,)), pltpu.SemaphoreType.DMA((n_chip,)),
                         pltpu.SemaphoreType.DMA((2,))],
         compiler_params=_params(0),
     )(out_grad, w_down)
 
     w_other, rows_other, hidden_other = pl.pallas_call(
-        lambda *refs: _pair_kernel(n_core, *refs),
+        _pair_kernel,
         out_shape=(
             jax.ShapeDtypeStruct(w_own.shape, w_own.dtype),
-            jax.ShapeDtypeStruct(rows_g.shape[1:], rows_g.dtype),
+            jax.ShapeDtypeStruct((n_plane,) + rows_g.shape[2:], rows_g.dtype),
             jax.ShapeDtypeStruct(hidden.shape, hidden.dtype),
         ),
         in_specs=[ANY, ANY, ANY],
         out_specs=(ANY, ANY, ANY),
-        scratch_shapes=[pltpu.SemaphoreType.DMA((3,)), pltpu.SemaphoreType.DMA((3,))],
+        scratch_shapes=[pltpu.SemaphoreType.DMA((2,)), pltpu.SemaphoreType.DMA((2,)),
+                        pltpu.SemaphoreType.DMA((n_plane,)), pltpu.SemaphoreType.DMA((n_plane,))],
         compiler_params=_params(1),
     )(w_own, rows_g, hidden)
 
-    rows_mine = lax.dynamic_index_in_dim(rows_g, core, 0, keepdims=False)
-    rows_theirs = lax.dynamic_index_in_dim(rows_g, 1 - core, 0, keepdims=False)
+    rows_mine = lax.dynamic_index_in_dim(rows_g, core, 1, keepdims=False)
+    rows_theirs = lax.dynamic_index_in_dim(rows_g, 1 - core, 1, keepdims=False)
     hidden_grad = jnp.einsum(
         "rtk,rkf->tf", rows_mine, w_own, preferred_element_type=jnp.float32
     ) + jnp.einsum("rtk,rkf->tf", rows_theirs, w_other, preferred_element_type=jnp.float32)
@@ -156,14 +195,14 @@
 
     received = pl.pallas_call(
         lambda *refs: _scatter_kernel(n_chip, *refs),
-        out_shape=jax.ShapeDtypeStruct(partial.shape, partial.dtype),
+        out_shape=jax.ShapeDtypeStruct(partial.shape, jnp.bfloat16),
         in_specs=[ANY],
         out_specs=ANY,
         scratch_shapes=[pltpu.SemaphoreType.DMA((n_chip,)), pltpu.SemaphoreType.DMA((n_chip,)),
                         pltpu.SemaphoreType.DMA((1,))],
         compiler_params=_params(2),
-    )(partial)
-    summed = jnp.sum(received, axis=0)
+    )(partial.astype(jnp.bfloat16))
+    summed = jnp.sum(received.astype(jnp.float32), axis=0)
 
     gate_grad = (
         hidden_grad * up_wide * sigmoid_gate * (1.0 + gate_wide * (1.0 - sigmoid_gate))

time: 261 us -> 213 us (0.82)
  Pallas kernels: 234 us -> 190 us
    pallas_call x1, Pallas kernels: 120 us -> 61.8 us  [body(): pl.pallas_call(lambda *refs: _scatter_kernel(n_chip, *refs), out_shape=ja...]
    pallas_call x2, Pallas kernels: 114 us -> 128 us  [the longest x1 116 us: body(): pl.pallas_call(lambda *refs: _gather_kernel(n_chip, n_lo, *refs), out_sha...]
where the time goes in v3:
time: 213 us
  Pallas kernels  190 us (89%)
  matrix products  15.8 us (7%)
  other arithmetic  6.43 us (3%)
    pallas_call x1, Pallas kernels, body(): pl.pallas_call(lambda *refs: _gather_kernel(n_chip, n_lo, *refs), out_sha...  116 us
    pallas_call x1, Pallas kernels, body(): pl.pallas_call(lambda *refs: _scatter_kernel(n_chip, *refs), out_shape=ja...  61.8 us
    pallas_call x1, Pallas kernels, body(): pl.pallas_call(_pair_kernel, out_shape=(jax.ShapeDtypeStruct(w_own.shape,...  11.4 us
    dot_general x1, matrix products, body(): jnp.einsum('rtk,rkf->tf', rows_theirs, w_other, preferred_element_type=jn...  5.15 us

profile of v3, /device:TPU:26, one launch (start us, length us, event | category | flops | bytes accessed | tf_op | source)
XLA Modules:
  0.0 212.9 jit_solution(9748437516860591508)
XLA Ops:
  0.6 3.0 %fusion.9.hid_ref = bf16[512,896]{1,0:T(8,128)(2,1)} fusion(bf16[512,896]{1,0:T(8,128)(2,1)} %param.6, bf16[512,896]{1,0:T(8,128)(2,1)} %param.5), kind=kLoop, calls=%fused_computation.16 | loop fusion | flops 3670016 | bytes 2752512 | tf_op jit(solution)/shard_map/convert_element_type | solution.py:152
  3.6 116.4 %shard_map.67 = (bf16[8,2,512,256]{3,2,1,0:T(8,128)(2,1)}, bf16[8,256,896]{2,1,0:T(8,128)(2,1)}) custom-call(bf16[512,256]{1,0:T(8,128)(2,1)} %refs_0_.1, bf16[256,896]{1,0:T(8,128)(2,1)} %refs_1_.1), custom_call_target="tpu_custom_call" | custom-call | tf_op jit(solution)/shard_map/pallas_call | solution.py:156
  120.0 11.4 %shard_map.68 = (bf16[8,256,896]{2,1,0:T(8,128)(2,1)}, bf16[8,512,256]{2,1,0:T(8,128)(2,1)}, bf16[512,896]{1,0:T(8,128)(2,1)}) custom-call(bf16[8,256,896]{2,1,0:T(8,128)(2,1)} %get-tuple-element.9.w_ref, bf16[8,2,512,256]{3,2,1,0:T(8,128)(2,1)} %get-tuple-element.8.rows_ref, bf16[512,896]{1,0:T(8,128)(2,1)} %fusion.9.hid_ref), custom_call_target="tpu_custom_call" | custom-call | tf_op jit(solution)/shard_map/pallas_call | solution.py:172
  131.4 0.0 copy-start
  131.4 0.0 copy-start.2
  131.4 0.0 copy-start.4
  131.5 0.0 copy-start.5
  131.5 5.2 %fusion = f32[512,896,1]{1,0,2:T(8,128)S(1)} fusion(bf16[8,256,896]{2,1,0:T(8,128)(2,1)} %get-tuple-element.10, bf16[8,2,512,256]{3,2,1,0:T(8,128)(2,1)} %get-tuple-element.8.rows_ref, s32[]{:T(128)S(6)} %select_n.8), kind=kOutput, calls=%fused_computation.7 | convolution fusion | flops 1879048192 | bytes 7602180 | tf_op jit(solution)/shard_map/rtk,rkf->tf/dot_general | solution.py:190
  136.6 0.0 copy-done
  136.6 0.0 copy-done.2
  136.6 0.0 copy-done.4
  136.7 0.2 copy-done.5
  136.9 0.0 copy-start.1
  136.9 4.1 %multiply_convert_fusion = (bf16[512,896]{1,0:T(8,128)(2,1)}, bf16[512,896]{1,0:T(8,128)(2,1)}) fusion(bf16[512,896]{1,0:T(8,128)(2,1)S(1)} %copy-done.4, bf16[512,896]{1,0:T(8,128)(2,1)S(1)} %copy-done.5, f32[512,896,1]{1,0,2:T(8,128)S(1)} %fusion, bf16[8,256,896]{2,1,0:T(8,128)(2,1)S(1)} %copy-done.2, bf16[8,2,512,256]{3,2,1,0:T(8,128)(2,1)S(1)} %copy-done, ...), kind=kOutput, calls=%fused_computation.25 | convolution fusion | flops 1886388224 | bytes 11272196 | tf_op jit(solution)/shard_map/rtk,rkf->tf/dot_general | solution.py:188
  141.0 0.0 copy-done.1
  141.0 0.0 copy-start.3
  141.0 0.0 copy-start.6
  141.0 2.4 %fusion.2 = f32[8,256,896]{2,1,0:T(8,128)S(1)} fusion(bf16[8,2,512,256]{3,2,1,0:T(8,128)(2,1)S(1)} %copy-done, s32[]{:T(128)S(6)} %select_n.7, bf16[512,896]{1,0:T(8,128)(2,1)S(1)} %copy-done.1), kind=kOutput, calls=%fused_computation.9 | convolution fusion | flops 1879048192 | bytes 10354692 | tf_op jit(solution)/shard_map/rtk,tf->rkf/dot_general | solution.py:192
  143.4 0.0 copy-done.3
  143.4 0.0 copy-done.6
  143.4 4.2 %add_convert_fusion.refs_0_ = bf16[8,256,896]{2,1,0:T(8,128)(2,1)} fusion(f32[8,256,896]{2,1,0:T(8,128)S(1)} %fusion.2, bf16[8,512,256]{2,1,0:T(8,128)(2,1)S(1)} %copy-done.3, bf16[512,896]{1,0:T(8,128)(2,1)S(1)} %copy-done.6), kind=kOutput, calls=%fused_computation.1 | convolution fusion | flops 1882718208 | bytes 14024704 | tf_op jit(solution)/shard_map/rtk,tf->rkf/dot_general | solution.py:194
  147.6 61.8 %shard_map.69 = bf16[8,256,896]{2,1,0:T(8,128)(2,1)} custom-call(bf16[8,256,896]{2,1,0:T(8,128)(2,1)} %add_convert_fusion.refs_0_), custom_call_target="tpu_custom_call" | custom-call | tf_op jit(solution)/shard_map/pallas_call | solution.py:196
  209.4 2.6 %convert_reduce_fusion = f32[256,896]{1,0:T(8,128)S(1)} fusion(bf16[8,256,896]{2,1,0:T(8,128)(2,1)} %shard_map.69), kind=kLoop, calls=%fused_computation | loop fusion | flops 3440640 | bytes 4587520 | tf_op jit(solution)/shard_map/reduce_sum | solution.py:205
  212.0 0.8 multiply_convert_fusion.1
Async XLA Ops:
  131.4 5.2 %copy-start = (bf16[8,2,512,256]{3,2,1,0:T(8,128)(2,1)S(1)}, bf16[8,2,512,256]{3,2,1,0:T(8,128)(2,1)}, u32[]{:S(2)}) copy-start(bf16[8,2,512,256]{3,2,1,0:T(8,128)(2,1)} %get-tuple-element.8.rows_ref) | copy-start | bytes 12582916
  131.4 5.2 %copy-start.2 = (bf16[8,256,896]{2,1,0:T(8,128)(2,1)S(1)}, bf16[8,256,896]{2,1,0:T(8,128)(2,1)}, u32[]{:S(2)}) copy-start(bf16[8,256,896]{2,1,0:T(8,128)(2,1)} %get-tuple-element.9.w_ref) | copy-start | bytes 11010052
  131.4 5.2 %copy-start.4 = (bf16[512,896]{1,0:T(8,128)(2,1)S(1)}, bf16[512,896]{1,0:T(8,128)(2,1)}, u32[]{:S(2)}) copy-start(bf16[512,896]{1,0:T(8,128)(2,1)} %param.5) | copy-start | bytes 2752516
  131.5 5.4 %copy-start.5 = (bf16[512,896]{1,0:T(8,128)(2,1)S(1)}, bf16[512,896]{1,0:T(8,128)(2,1)}, u32[]{:S(2)}) copy-start(bf16[512,896]{1,0:T(8,128)(2,1)} %param.6) | copy-start | bytes 2752516
  136.9 4.1 %copy-start.1 = (bf16[512,896]{1,0:T(8,128)(2,1)S(1)}, bf16[512,896]{1,0:T(8,128)(2,1)}, u32[]{:S(2)}) copy-start(bf16[512,896]{1,0:T(8,128)(2,1)} %fusion.9.hid_ref) | copy-start | bytes 2752516
  141.0 2.4 %copy-start.3 = (bf16[8,512,256]{2,1,0:T(8,128)(2,1)S(1)}, bf16[8,512,256]{2,1,0:T(8,128)(2,1)}, u32[]{:S(2)}) copy-start(bf16[8,512,256]{2,1,0:T(8,128)(2,1)} %get-tuple-element.11) | copy-start | bytes 6291460
  141.0 2.4 %copy-start.6 = (bf16[512,896]{1,0:T(8,128)(2,1)S(1)}, bf16[512,896]{1,0:T(8,128)(2,1)}, u32[]{:S(2)}) copy-start(bf16[512,896]{1,0:T(8,128)(2,1)} %get-tuple-element.12) | copy-start | bytes 2752516

commit v4 on v3

--- a/solution.py
+++ b/solution.py
@@ -17,8 +17,30 @@
     return lax.axis_index("chip"), lax.axis_index("core"), lax.axis_index("tensor")
 
 
-def _gather_kernel(n_chip, n_lo, og_ref, w_ref, rows_out, w_out,
-                   x_send, x_recv, r_send, r_recv, l_send, l_recv, w_send, w_recv, own_sem):
+def _w_kernel(n_chip, w_ref, w_out, w_send, w_recv, own_sem):
+    chip, core, ten = _where()
+    barrier = pltpu.get_barrier_semaphore()
+    for k in range(1, n_chip):
+        pl.semaphore_signal(barrier, inc=1, device_id=((chip + k) % n_chip, core, ten),
+                            device_id_type=MESH)
+    pl.semaphore_wait(barrier, n_chip - 1)
+    own_w = pltpu.make_async_copy(w_ref, w_out.at[chip], own_sem.at[0])
+    own_w.start()
+    w_copies = []
+    for k in range(1, n_chip):
+        cp = pltpu.make_async_remote_copy(
+            w_ref, w_out.at[chip], w_send.at[k], w_recv.at[k],
+            device_id=((chip + k) % n_chip, core, ten), device_id_type=MESH)
+        cp.start()
+        w_copies.append(cp)
+    own_w.wait()
+    for cp in w_copies:
+        cp.wait_send()
+        cp.wait_recv()
+
+
+def _rows_kernel(n_lo, og_ref, rows_out, x_send, x_recv, r_send, r_recv, l_send, l_recv,
+                 own_sem):
     chip, core, ten = _where()
     n_plane = rows_out.shape[0]
     plane, lo = ten // n_lo, ten % n_lo
@@ -28,22 +50,10 @@
     barrier = pltpu.get_barrier_semaphore()
     for t in (right, left, side):
         pl.semaphore_signal(barrier, inc=1, device_id=(chip, core, t), device_id_type=MESH)
-    for k in range(1, n_chip):
-        pl.semaphore_signal(barrier, inc=1, device_id=((chip + k) % n_chip, core, ten),
-                            device_id_type=MESH)
-    pl.semaphore_wait(barrier, 3 + (n_chip - 1))
+    pl.semaphore_wait(barrier, 3)
 
     own_r = pltpu.make_async_copy(og_ref, rows_out.at[plane, lo], own_sem.at[0])
-    own_w = pltpu.make_async_copy(w_ref, w_out.at[chip], own_sem.at[1])
     own_r.start()
-    own_w.start()
-    w_copies = []
-    for k in range(1, n_chip):
-        cp = pltpu.make_async_remote_copy(
-            w_ref, w_out.at[chip], w_send.at[k], w_recv.at[k],
-            device_id=((chip + k) % n_chip, core, ten), device_id_type=MESH)
-        cp.start()
-        w_copies.append(cp)
     side_cp = pltpu.make_async_remote_copy(
         og_ref, rows_out.at[plane, lo], x_send.at[0], x_recv.at[0],
         device_id=(chip, core, side), device_id_type=MESH)
@@ -80,10 +90,6 @@
             by[(d, n - 1)].wait_recv()
         for s in range(n):
             by[(d, s)].wait_send()
-    own_w.wait()
-    for cp in w_copies:
-        cp.wait_send()
-        cp.wait_recv()
 
 
 def _pair_kernel(w_ref, rows_ref, hid_ref, w_other, rows_other, hid_other,
@@ -153,21 +159,27 @@
 
     n_lo = n_core
     n_plane = n_ten // n_lo
-    rows_g, w_own = pl.pallas_call(
-        lambda *refs: _gather_kernel(n_chip, n_lo, *refs),
-        out_shape=(
-            jax.ShapeDtypeStruct((n_plane, n_lo, seq_rows, out_grad.shape[1]), out_grad.dtype),
-            jax.ShapeDtypeStruct((n_chip, width, ff), w_down.dtype),
-        ),
-        in_specs=[ANY, ANY],
-        out_specs=(ANY, ANY),
+    rows_g = pl.pallas_call(
+        lambda *refs: _rows_kernel(n_lo, *refs),
+        out_shape=jax.ShapeDtypeStruct(
+            (n_plane, n_lo, seq_rows, out_grad.shape[1]), out_grad.dtype),
+        in_specs=[ANY],
+        out_specs=ANY,
         scratch_shapes=[pltpu.SemaphoreType.DMA((1,)), pltpu.SemaphoreType.DMA((1,)),
                         pltpu.SemaphoreType.DMA((n_plane,)), pltpu.SemaphoreType.DMA((n_plane,)),
                         pltpu.SemaphoreType.DMA((n_plane,)), pltpu.SemaphoreType.DMA((n_plane,)),
-                        pltpu.SemaphoreType.DMA((n_chip,)), pltpu.SemaphoreType.DMA((n_chip,)),
-                        pltpu.SemaphoreType.DMA((2,))],
+                        pltpu.SemaphoreType.DMA((1,))],
         compiler_params=_params(0),
-    )(out_grad, w_down)
+    )(out_grad)
+    w_own = pl.pallas_call(
+        lambda *refs: _w_kernel(n_chip, *refs),
+        out_shape=jax.ShapeDtypeStruct((n_chip, width, ff), w_down.dtype),
+        in_specs=[ANY],
+        out_specs=ANY,
+        scratch_shapes=[pltpu.SemaphoreType.DMA((n_chip,)), pltpu.SemaphoreType.DMA((n_chip,)),
+                        pltpu.SemaphoreType.DMA((1,))],
+        compiler_params=_params(3),
+    )(w_down)
 
     w_other, rows_other, hidden_other = pl.pallas_call(
         _pair_kernel,

time: 213 us -> 218 us (1.023)
  Pallas kernels: 190 us -> 195 us
    pallas_call x1 -> x2, Pallas kernels: 116 us -> 121 us  [the longest x1 61 us: body(): pl.pallas_call(lambda *refs: _w_kernel(n_chip, *refs), out_shape=jax.Shap...]
where the time goes in v4:
time: 218 us
  Pallas kernels  195 us (89%)
  matrix products  15.8 us (7%)
  other arithmetic  6.42 us (3%)
    pallas_call x1, Pallas kernels, body(): pl.pallas_call(lambda *refs: _scatter_kernel(n_chip, *refs), out_shape=ja...  61.8 us
    pallas_call x1, Pallas kernels, body(): pl.pallas_call(lambda *refs: _w_kernel(n_chip, *refs), out_shape=jax.Shap...  61 us
    pallas_call x1, Pallas kernels, body(): pl.pallas_call(lambda *refs: _rows_kernel(n_lo, *refs), out_shape=jax.Sha...  60.4 us
    pallas_call x1, Pallas kernels, body(): pl.pallas_call(_pair_kernel, out_shape=(jax.ShapeDtypeStruct(w_own.shape,...  11.4 us
    dot_general x1, matrix products, body(): jnp.einsum('rtk,rkf->tf', rows_theirs, w_other, preferred_element_type=jn...  5.15 us

profile of v4, /device:TPU:26, one launch (start us, length us, event | category | flops | bytes accessed | tf_op | source)
XLA Modules:
  0.0 217.9 jit_solution(17607167422756195269)
XLA Ops:
  0.6 3.0 %fusion.9.hid_ref = bf16[512,896]{1,0:T(8,128)(2,1)} fusion(bf16[512,896]{1,0:T(8,128)(2,1)} %param.6, bf16[512,896]{1,0:T(8,128)(2,1)} %param.5), kind=kLoop, calls=%fused_computation.16 | loop fusion | flops 3670016 | bytes 2752512 | tf_op jit(solution)/shard_map/convert_element_type | solution.py:158
  3.6 61.0 %shard_map.68.w_ref = bf16[8,256,896]{2,1,0:T(8,128)(2,1)} custom-call(bf16[256,896]{1,0:T(8,128)(2,1)} %refs_0_.3), custom_call_target="tpu_custom_call" | custom-call | tf_op jit(solution)/shard_map/pallas_call | solution.py:174
  64.6 60.4 %shard_map.67.rows_ref = bf16[8,2,512,256]{3,2,1,0:T(8,128)(2,1)} custom-call(bf16[512,256]{1,0:T(8,128)(2,1)} %refs_0_.2), custom_call_target="tpu_custom_call" | custom-call | tf_op jit(solution)/shard_map/pallas_call | solution.py:162
  125.0 11.4 %shard_map.69 = (bf16[8,256,896]{2,1,0:T(8,128)(2,1)}, bf16[8,512,256]{2,1,0:T(8,128)(2,1)}, bf16[512,896]{1,0:T(8,128)(2,1)}) custom-call(bf16[8,256,896]{2,1,0:T(8,128)(2,1)} %shard_map.68.w_ref, bf16[8,2,512,256]{3,2,1,0:T(8,128)(2,1)} %shard_map.67.rows_ref, bf16[512,896]{1,0:T(8,128)(2,1)} %fusion.9.hid_ref), custom_call_target="tpu_custom_call" | custom-call | tf_op jit(solution)/shard_map/pallas_call | solution.py:184
  136.4 0.0 copy-start
  136.4 0.0 copy-start.1
  136.5 0.0 copy-start.4
  136.5 0.0 copy-start.5
  136.5 5.2 %fusion = f32[512,896,1]{1,0,2:T(8,128)S(1)} fusion(bf16[8,256,896]{2,1,0:T(8,128)(2,1)} %get-tuple-element.6, bf16[8,2,512,256]{3,2,1,0:T(8,128)(2,1)} %shard_map.67.rows_ref, s32[]{:T(128)S(6)} %select_n.8), kind=kOutput, calls=%fused_computation.7 | convolution fusion | flops 1879048192 | bytes 7602180 | tf_op jit(solution)/shard_map/rtk,rkf->tf/dot_general | solution.py:202
  141.6 0.0 copy-done
  141.6 0.0 copy-done.1
  141.7 0.0 copy-done.4
  141.7 0.2 copy-done.5
  141.9 0.0 copy-start.2
  141.9 4.1 %multiply_convert_fusion = (bf16[512,896]{1,0:T(8,128)(2,1)}, bf16[512,896]{1,0:T(8,128)(2,1)}) fusion(bf16[512,896]{1,0:T(8,128)(2,1)S(1)} %copy-done.4, bf16[512,896]{1,0:T(8,128)(2,1)S(1)} %copy-done.5, f32[512,896,1]{1,0,2:T(8,128)S(1)} %fusion, bf16[8,256,896]{2,1,0:T(8,128)(2,1)S(1)} %copy-done.1, bf16[8,2,512,256]{3,2,1,0:T(8,128)(2,1)S(1)} %copy-done, ...), kind=kOutput, calls=%fused_computation.25 | convolution fusion | flops 1886388224 | bytes 11272196 | tf_op jit(solution)/shard_map/rtk,rkf->tf/dot_general | solution.py:200
  146.0 0.0 copy-done.2
  146.0 0.0 copy-start.3
  146.0 0.0 copy-start.6
  146.0 2.4 %fusion.2 = f32[8,256,896]{2,1,0:T(8,128)S(1)} fusion(bf16[8,2,512,256]{3,2,1,0:T(8,128)(2,1)S(1)} %copy-done, s32[]{:T(128)S(6)} %select_n.7, bf16[512,896]{1,0:T(8,128)(2,1)S(1)} %copy-done.2), kind=kOutput, calls=%fused_computation.9 | convolution fusion | flops 1879048192 | bytes 10354692 | tf_op jit(solution)/shard_map/rtk,tf->rkf/dot_general | solution.py:204
  148.4 0.0 copy-done.3
  148.4 0.0 copy-done.6
  148.4 4.2 %add_convert_fusion.refs_0_ = bf16[8,256,896]{2,1,0:T(8,128)(2,1)} fusion(f32[8,256,896]{2,1,0:T(8,128)S(1)} %fusion.2, bf16[8,512,256]{2,1,0:T(8,128)(2,1)S(1)} %copy-done.3, bf16[512,896]{1,0:T(8,128)(2,1)S(1)} %copy-done.6), kind=kOutput, calls=%fused_computation.1 | convolution fusion | flops 1882718208 | bytes 14024704 | tf_op jit(solution)/shard_map/rtk,tf->rkf/dot_general | solution.py:206
  152.6 61.8 %shard_map.70 = bf16[8,256,896]{2,1,0:T(8,128)(2,1)} custom-call(bf16[8,256,896]{2,1,0:T(8,128)(2,1)} %add_convert_fusion.refs_0_), custom_call_target="tpu_custom_call" | custom-call | tf_op jit(solution)/shard_map/pallas_call | solution.py:208
  214.4 2.6 %convert_reduce_fusion = f32[256,896]{1,0:T(8,128)S(1)} fusion(bf16[8,256,896]{2,1,0:T(8,128)(2,1)} %shard_map.70), kind=kLoop, calls=%fused_computation | loop fusion | flops 3440640 | bytes 4587520 | tf_op jit(solution)/shard_map/reduce_sum | solution.py:217
  217.0 0.8 multiply_convert_fusion.1
Async XLA Ops:
  136.4 5.2 %copy-start = (bf16[8,2,512,256]{3,2,1,0:T(8,128)(2,1)S(1)}, bf16[8,2,512,256]{3,2,1,0:T(8,128)(2,1)}, u32[]{:S(2)}) copy-start(bf16[8,2,512,256]{3,2,1,0:T(8,128)(2,1)} %shard_map.67.rows_ref) | copy-start | bytes 12582916
  136.4 5.2 %copy-start.1 = (bf16[8,256,896]{2,1,0:T(8,128)(2,1)S(1)}, bf16[8,256,896]{2,1,0:T(8,128)(2,1)}, u32[]{:S(2)}) copy-start(bf16[8,256,896]{2,1,0:T(8,128)(2,1)} %shard_map.68.w_ref) | copy-start | bytes 11010052
  136.5 5.2 %copy-start.4 = (bf16[512,896]{1,0:T(8,128)(2,1)S(1)}, bf16[512,896]{1,0:T(8,128)(2,1)}, u32[]{:S(2)}) copy-start(bf16[512,896]{1,0:T(8,128)(2,1)} %param.5) | copy-start | bytes 2752516
  136.5 5.4 %copy-start.5 = (bf16[512,896]{1,0:T(8,128)(2,1)S(1)}, bf16[512,896]{1,0:T(8,128)(2,1)}, u32[]{:S(2)}) copy-start(bf16[512,896]{1,0:T(8,128)(2,1)} %param.6) | copy-start | bytes 2752516
  141.9 4.1 %copy-start.2 = (bf16[512,896]{1,0:T(8,128)(2,1)S(1)}, bf16[512,896]{1,0:T(8,128)(2,1)}, u32[]{:S(2)}) copy-start(bf16[512,896]{1,0:T(8,128)(2,1)} %fusion.9.hid_ref) | copy-start | bytes 2752516
  146.0 2.4 %copy-start.3 = (bf16[8,512,256]{2,1,0:T(8,128)(2,1)S(1)}, bf16[8,512,256]{2,1,0:T(8,128)(2,1)}, u32[]{:S(2)}) copy-start(bf16[8,512,256]{2,1,0:T(8,128)(2,1)} %get-tuple-element.7) | copy-start | bytes 6291460
  146.0 2.4 %copy-start.6 = (bf16[512,896]{1,0:T(8,128)(2,1)S(1)}, bf16[512,896]{1,0:T(8,128)(2,1)}, u32[]{:S(2)}) copy-start(bf16[512,896]{1,0:T(8,128)(2,1)} %get-tuple-element.8) | copy-start | bytes 2752516

commit v5 on v3

--- a/solution.py
+++ b/solution.py
@@ -17,8 +17,8 @@
     return lax.axis_index("chip"), lax.axis_index("core"), lax.axis_index("tensor")
 
 
-def _gather_kernel(n_chip, n_lo, og_ref, w_ref, rows_out, w_out,
-                   x_send, x_recv, r_send, r_recv, l_send, l_recv, w_send, w_recv, own_sem):
+def _gather_kernel(n_chip, n_lo, og_ref, w_ref, rows_out, w_out, x_send, x_recv,
+                   r_send, r_recv, l_send, l_recv, w_send, w_recv, own_sem):
     chip, core, ten = _where()
     n_plane = rows_out.shape[0]
     plane, lo = ten // n_lo, ten % n_lo
@@ -33,10 +33,33 @@
                             device_id_type=MESH)
     pl.semaphore_wait(barrier, 3 + (n_chip - 1))
 
+    side_cp = pltpu.make_async_remote_copy(
+        og_ref, rows_out.at[plane, lo], x_send.at[0], x_recv.at[0],
+        device_id=(chip, core, side), device_id_type=MESH)
+    side_cp.start()
     own_r = pltpu.make_async_copy(og_ref, rows_out.at[plane, lo], own_sem.at[0])
     own_w = pltpu.make_async_copy(w_ref, w_out.at[chip], own_sem.at[1])
     own_r.start()
     own_w.start()
+    own_r.wait()
+    side_cp.wait_send()
+    side_cp.wait_recv()
+
+    n_steps = n_plane // 2
+    ring = {}
+    for s in range(n_steps):
+        for d, sends, recvs, to, src_plane, half in (
+            ("r", r_send, r_recv, right, (plane + n_plane - s) % n_plane, 0),
+            ("l", l_send, l_recv, left, (plane + s) % n_plane, 1),
+        ):
+            block = rows_out.at[src_plane]
+            if s == n_steps - 1:
+                block = rows_out.at[src_plane, half]
+            ring[(d, s)] = pltpu.make_async_remote_copy(
+                block, block, sends.at[s], recvs.at[s],
+                device_id=(chip, core, to), device_id_type=MESH)
+    for d in ("r", "l"):
+        ring[(d, 0)].start()
     w_copies = []
     for k in range(1, n_chip):
         cp = pltpu.make_async_remote_copy(
@@ -44,42 +67,14 @@
             device_id=((chip + k) % n_chip, core, ten), device_id_type=MESH)
         cp.start()
         w_copies.append(cp)
-    side_cp = pltpu.make_async_remote_copy(
-        og_ref, rows_out.at[plane, lo], x_send.at[0], x_recv.at[0],
-        device_id=(chip, core, side), device_id_type=MESH)
-    side_cp.start()
-    own_r.wait()
-    side_cp.wait_send()
-    side_cp.wait_recv()
-
-    n_right = n_plane // 2
-    n_left = n_plane - 1 - n_right
-    ring = []
-    for s in range(max(n_right, n_left)):
-        if s < n_right:
-            src_plane = (plane + n_plane - s) % n_plane
-            cp = pltpu.make_async_remote_copy(
-                rows_out.at[src_plane], rows_out.at[src_plane], r_send.at[s], r_recv.at[s],
-                device_id=(chip, core, right), device_id_type=MESH)
-            ring.append(("r", s, cp))
-        if s < n_left:
-            src_plane = (plane + s) % n_plane
-            cp = pltpu.make_async_remote_copy(
-                rows_out.at[src_plane], rows_out.at[src_plane], l_send.at[s], l_recv.at[s],
-                device_id=(chip, core, left), device_id_type=MESH)
-            ring.append(("l", s, cp))
-    by = {(d, s): cp for d, s, cp in ring}
-    for s in range(max(n_right, n_left)):
-        for d, n in (("r", n_right), ("l", n_left)):
-            if s < n:
-                if s > 0:
-                    by[(d, s - 1)].wait_recv()
-                by[(d, s)].start()
-    for d, n in (("r", n_right), ("l", n_left)):
-        if n > 0:
-            by[(d, n - 1)].wait_recv()
-        for s in range(n):
-            by[(d, s)].wait_send()
+    for s in range(1, n_steps):
+        for d in ("r", "l"):
+            ring[(d, s - 1)].wait_recv()
+            ring[(d, s)].start()
+    for d in ("r", "l"):
+        ring[(d, n_steps - 1)].wait_recv()
+        for s in range(n_steps):
+            ring[(d, s)].wait_send()
     own_w.wait()
     for cp in w_copies:
         cp.wait_send()
@@ -162,8 +157,10 @@
         in_specs=[ANY, ANY],
         out_specs=(ANY, ANY),
         scratch_shapes=[pltpu.SemaphoreType.DMA((1,)), pltpu.SemaphoreType.DMA((1,)),
-                        pltpu.SemaphoreType.DMA((n_plane,)), pltpu.SemaphoreType.DMA((n_plane,)),
-                        pltpu.SemaphoreType.DMA((n_plane,)), pltpu.SemaphoreType.DMA((n_plane,)),
+                        pltpu.SemaphoreType.DMA((n_plane // 2,)),
+                        pltpu.SemaphoreType.DMA((n_plane // 2,)),
+                        pltpu.SemaphoreType.DMA((n_plane // 2,)),
+                        pltpu.SemaphoreType.DMA((n_plane // 2,)),
                         pltpu.SemaphoreType.DMA((n_chip,)), pltpu.SemaphoreType.DMA((n_chip,)),
                         pltpu.SemaphoreType.DMA((2,))],
         compiler_params=_params(0),

time: 213 us -> 169 us (0.79)
  Pallas kernels: 190 us -> 145 us
    pallas_call x1, Pallas kernels: 116 us -> 72.1 us  [body(): pl.pallas_call(lambda *refs: _gather_kernel(n_chip, n_lo, *refs), out_sha...]
where the time goes in v5:
time: 169 us
  Pallas kernels  145 us (86%)
  matrix products  15.8 us (9%)
  other arithmetic  6.43 us (4%)
    pallas_call x1, Pallas kernels, body(): pl.pallas_call(lambda *refs: _gather_kernel(n_chip, n_lo, *refs), out_sha...  72.1 us
    pallas_call x1, Pallas kernels, body(): pl.pallas_call(lambda *refs: _scatter_kernel(n_chip, *refs), out_shape=ja...  61.8 us
    pallas_call x1, Pallas kernels, body(): pl.pallas_call(_pair_kernel, out_shape=(jax.ShapeDtypeStruct(w_own.shape,...  11.4 us
    dot_general x1, matrix products, body(): jnp.einsum('rtk,rkf->tf', rows_theirs, w_other, preferred_element_type=jn...  5.15 us
    dot_general x1, matrix products, body(): jnp.einsum('rtk,tf->rkf', rows_other, hidden_other, preferred_element_typ...  4.17 us
    dot_general x1, matrix products, body(): jnp.einsum('rtk,rkf->tf', rows_mine, w_own, preferred_element_type=jnp.fl...  4.12 us

profile of v5, /device:TPU:26, one launch (start us, length us, event | category | flops | bytes accessed | tf_op | source)
XLA Modules:
  0.0 168.6 jit_solution(2385410526287070075)
XLA Ops:
  0.6 3.0 %fusion.9.hid_ref = bf16[512,896]{1,0:T(8,128)(2,1)} fusion(bf16[512,896]{1,0:T(8,128)(2,1)} %param.6, bf16[512,896]{1,0:T(8,128)(2,1)} %param.5), kind=kLoop, calls=%fused_computation.16 | loop fusion | flops 3670016 | bytes 2752512 | tf_op jit(solution)/shard_map/convert_element_type | solution.py:147
  3.6 72.1 %shard_map.67 = (bf16[8,2,512,256]{3,2,1,0:T(8,128)(2,1)}, bf16[8,256,896]{2,1,0:T(8,128)(2,1)}) custom-call(bf16[512,256]{1,0:T(8,128)(2,1)} %refs_0_.1, bf16[256,896]{1,0:T(8,128)(2,1)} %refs_1_.1), custom_call_target="tpu_custom_call" | custom-call | tf_op jit(solution)/shard_map/pallas_call | solution.py:151
  75.7 11.4 %shard_map.68 = (bf16[8,256,896]{2,1,0:T(8,128)(2,1)}, bf16[8,512,256]{2,1,0:T(8,128)(2,1)}, bf16[512,896]{1,0:T(8,128)(2,1)}) custom-call(bf16[8,256,896]{2,1,0:T(8,128)(2,1)} %get-tuple-element.9.w_ref, bf16[8,2,512,256]{3,2,1,0:T(8,128)(2,1)} %get-tuple-element.8.rows_ref, bf16[512,896]{1,0:T(8,128)(2,1)} %fusion.9.hid_ref), custom_call_target="tpu_custom_call" | custom-call | tf_op jit(solution)/shard_map/pallas_call | solution.py:169
  87.1 0.0 copy-start
  87.1 0.0 copy-start.2
  87.1 0.0 copy-start.4
  87.1 0.0 copy-start.5
  87.2 5.2 %fusion = f32[512,896,1]{1,0,2:T(8,128)S(1)} fusion(bf16[8,256,896]{2,1,0:T(8,128)(2,1)} %get-tuple-element.10, bf16[8,2,512,256]{3,2,1,0:T(8,128)(2,1)} %get-tuple-element.8.rows_ref, s32[]{:T(128)S(6)} %select_n.8), kind=kOutput, calls=%fused_computation.7 | convolution fusion | flops 1879048192 | bytes 7602180 | tf_op jit(solution)/shard_map/rtk,rkf->tf/dot_general | solution.py:187
  92.3 0.0 copy-done
  92.3 0.0 copy-done.2
  92.3 0.0 copy-done.4
  92.3 0.2 copy-done.5
  92.6 0.0 copy-start.1
  92.6 4.1 %multiply_convert_fusion = (bf16[512,896]{1,0:T(8,128)(2,1)}, bf16[512,896]{1,0:T(8,128)(2,1)}) fusion(bf16[512,896]{1,0:T(8,128)(2,1)S(1)} %copy-done.4, bf16[512,896]{1,0:T(8,128)(2,1)S(1)} %copy-done.5, f32[512,896,1]{1,0,2:T(8,128)S(1)} %fusion, bf16[8,256,896]{2,1,0:T(8,128)(2,1)S(1)} %copy-done.2, bf16[8,2,512,256]{3,2,1,0:T(8,128)(2,1)S(1)} %copy-done, ...), kind=kOutput, calls=%fused_computation.25 | convolution fusion | flops 1886388224 | bytes 11272196 | tf_op jit(solution)/shard_map/rtk,rkf->tf/dot_general | solution.py:185
  96.7 0.0 copy-done.1
  96.7 0.0 copy-start.3
  96.7 0.0 copy-start.6
  96.7 2.4 %fusion.2 = f32[8,256,896]{2,1,0:T(8,128)S(1)} fusion(bf16[8,2,512,256]{3,2,1,0:T(8,128)(2,1)S(1)} %copy-done, s32[]{:T(128)S(6)} %select_n.7, bf16[512,896]{1,0:T(8,128)(2,1)S(1)} %copy-done.1), kind=kOutput, calls=%fused_computation.9 | convolution fusion | flops 1879048192 | bytes 10354692 | tf_op jit(solution)/shard_map/rtk,tf->rkf/dot_general | solution.py:189
  99.1 0.0 copy-done.3
  99.1 0.0 copy-done.6
  99.1 4.2 %add_convert_fusion.refs_0_ = bf16[8,256,896]{2,1,0:T(8,128)(2,1)} fusion(f32[8,256,896]{2,1,0:T(8,128)S(1)} %fusion.2, bf16[8,512,256]{2,1,0:T(8,128)(2,1)S(1)} %copy-done.3, bf16[512,896]{1,0:T(8,128)(2,1)S(1)} %copy-done.6), kind=kOutput, calls=%fused_computation.1 | convolution fusion | flops 1882718208 | bytes 14024704 | tf_op jit(solution)/shard_map/rtk,tf->rkf/dot_general | solution.py:191
  103.3 61.8 %shard_map.69 = bf16[8,256,896]{2,1,0:T(8,128)(2,1)} custom-call(bf16[8,256,896]{2,1,0:T(8,128)(2,1)} %add_convert_fusion.refs_0_), custom_call_target="tpu_custom_call" | custom-call | tf_op jit(solution)/shard_map/pallas_call | solution.py:193
  165.1 2.6 %convert_reduce_fusion = f32[256,896]{1,0:T(8,128)S(1)} fusion(bf16[8,256,896]{2,1,0:T(8,128)(2,1)} %shard_map.69), kind=kLoop, calls=%fused_computation | loop fusion | flops 3440640 | bytes 4587520 | tf_op jit(solution)/shard_map/reduce_sum | solution.py:202
  167.7 0.8 multiply_convert_fusion.1
Async XLA Ops:
  87.1 5.2 %copy-start = (bf16[8,2,512,256]{3,2,1,0:T(8,128)(2,1)S(1)}, bf16[8,2,512,256]{3,2,1,0:T(8,128)(2,1)}, u32[]{:S(2)}) copy-start(bf16[8,2,512,256]{3,2,1,0:T(8,128)(2,1)} %get-tuple-element.8.rows_ref) | copy-start | bytes 12582916
  87.1 5.2 %copy-start.2 = (bf16[8,256,896]{2,1,0:T(8,128)(2,1)S(1)}, bf16[8,256,896]{2,1,0:T(8,128)(2,1)}, u32[]{:S(2)}) copy-start(bf16[8,256,896]{2,1,0:T(8,128)(2,1)} %get-tuple-element.9.w_ref) | copy-start | bytes 11010052
  87.1 5.2 %copy-start.4 = (bf16[512,896]{1,0:T(8,128)(2,1)S(1)}, bf16[512,896]{1,0:T(8,128)(2,1)}, u32[]{:S(2)}) copy-start(bf16[512,896]{1,0:T(8,128)(2,1)} %param.5) | copy-start | bytes 2752516
  87.1 5.4 %copy-start.5 = (bf16[512,896]{1,0:T(8,128)(2,1)S(1)}, bf16[512,896]{1,0:T(8,128)(2,1)}, u32[]{:S(2)}) copy-start(bf16[512,896]{1,0:T(8,128)(2,1)} %param.6) | copy-start | bytes 2752516
  92.6 4.1 %copy-start.1 = (bf16[512,896]{1,0:T(8,128)(2,1)S(1)}, bf16[512,896]{1,0:T(8,128)(2,1)}, u32[]{:S(2)}) copy-start(bf16[512,896]{1,0:T(8,128)(2,1)} %fusion.9.hid_ref) | copy-start | bytes 2752516
  96.7 2.4 %copy-start.3 = (bf16[8,512,256]{2,1,0:T(8,128)(2,1)S(1)}, bf16[8,512,256]{2,1,0:T(8,128)(2,1)}, u32[]{:S(2)}) copy-start(bf16[8,512,256]{2,1,0:T(8,128)(2,1)} %get-tuple-element.11) | copy-start | bytes 6291460
  96.7 2.4 %copy-start.6 = (bf16[512,896]{1,0:T(8,128)(2,1)S(1)}, bf16[512,896]{1,0:T(8,128)(2,1)}, u32[]{:S(2)}) copy-start(bf16[512,896]{1,0:T(8,128)(2,1)} %get-tuple-element.12) | copy-start | bytes 2752516

commit v6 on v5

--- a/solution.py
+++ b/solution.py
@@ -17,21 +17,24 @@
     return lax.axis_index("chip"), lax.axis_index("core"), lax.axis_index("tensor")
 
 
-def _gather_kernel(n_chip, n_lo, og_ref, w_ref, rows_out, w_out, x_send, x_recv,
-                   r_send, r_recv, l_send, l_recv, w_send, w_recv, own_sem):
+def _gather_kernel(n_chip, n_lo, og_ref, w_ref, hid_ref, rows_out, w_out, rows_other,
+                   w_other, hid_other, x_send, x_recv, r_send, r_recv, l_send, l_recv,
+                   w_send, w_recv, f_send, f_recv, fw_send, fw_recv, fr_send, fr_recv, own_sem):
     chip, core, ten = _where()
     n_plane = rows_out.shape[0]
     plane, lo = ten // n_lo, ten % n_lo
     right = ((plane + 1) % n_plane) * n_lo + lo
     left = ((plane + n_plane - 1) % n_plane) * n_lo + lo
     side = plane * n_lo + (1 - lo)
+    other = (chip, 1 - core, ten)
     barrier = pltpu.get_barrier_semaphore()
     for t in (right, left, side):
         pl.semaphore_signal(barrier, inc=1, device_id=(chip, core, t), device_id_type=MESH)
     for k in range(1, n_chip):
         pl.semaphore_signal(barrier, inc=1, device_id=((chip + k) % n_chip, core, ten),
                             device_id_type=MESH)
-    pl.semaphore_wait(barrier, 3 + (n_chip - 1))
+    pl.semaphore_signal(barrier, inc=1, device_id=other, device_id_type=MESH)
+    pl.semaphore_wait(barrier, 3 + (n_chip - 1) + 1)
 
     side_cp = pltpu.make_async_remote_copy(
         og_ref, rows_out.at[plane, lo], x_send.at[0], x_recv.at[0],
@@ -41,9 +44,32 @@
     own_w = pltpu.make_async_copy(w_ref, w_out.at[chip], own_sem.at[1])
     own_r.start()
     own_w.start()
+    hid_cp = pltpu.make_async_remote_copy(hid_ref, hid_other, f_send.at[0], f_recv.at[0],
+                                          device_id=other, device_id_type=MESH)
+    hid_cp.start()
+    forwards = [hid_cp]
+
+    def fwd_w(k):
+        r = (chip + n_chip - k) % n_chip
+        src = w_ref if k == 0 else w_out.at[r]
+        cp = pltpu.make_async_remote_copy(src, w_other.at[r], fw_send.at[k], fw_recv.at[k],
+                                          device_id=other, device_id_type=MESH)
+        cp.start()
+        forwards.append(cp)
+
+    def fwd_rows(d):
+        p = (plane + d) % n_plane
+        cp = pltpu.make_async_remote_copy(rows_out.at[p, 1 - core], rows_other.at[p],
+                                          fr_send.at[d], fr_recv.at[d],
+                                          device_id=other, device_id_type=MESH)
+        cp.start()
+        forwards.append(cp)
+
+    fwd_w(0)
     own_r.wait()
     side_cp.wait_send()
     side_cp.wait_recv()
+    fwd_rows(0)
 
     n_steps = n_plane // 2
     ring = {}
@@ -71,36 +97,20 @@
         for d in ("r", "l"):
             ring[(d, s - 1)].wait_recv()
             ring[(d, s)].start()
+        fwd_rows(n_plane - s)
+        fwd_rows(s)
     for d in ("r", "l"):
         ring[(d, n_steps - 1)].wait_recv()
         for s in range(n_steps):
             ring[(d, s)].wait_send()
+    fwd_rows(n_steps)
+    for k in range(1, n_chip):
+        w_copies[k - 1].wait_recv()
+        fwd_w(k)
     own_w.wait()
     for cp in w_copies:
         cp.wait_send()
-        cp.wait_recv()
-
-
-def _pair_kernel(w_ref, rows_ref, hid_ref, w_other, rows_other, hid_other,
-                 send, recv, r_send, r_recv):
-    chip, core, ten = _where()
-    other = (chip, 1 - core, ten)
-    barrier = pltpu.get_barrier_semaphore()
-    pl.semaphore_signal(barrier, inc=1, device_id=other, device_id_type=MESH)
-    pl.semaphore_wait(barrier, 1)
-    copies = [
-        pltpu.make_async_remote_copy(w_ref, w_other, send.at[0], recv.at[0],
-                                     device_id=other, device_id_type=MESH),
-        pltpu.make_async_remote_copy(hid_ref, hid_other, send.at[1], recv.at[1],
-                                     device_id=other, device_id_type=MESH),
-    ]
-    for r in range(rows_ref.shape[0]):
-        copies.append(pltpu.make_async_remote_copy(
-            rows_ref.at[r, 1 - core], rows_other.at[r], r_send.at[r], r_recv.at[r],
-            device_id=other, device_id_type=MESH))
-    for cp in copies:
-        cp.start()
-    for cp in copies:
+    for cp in forwards:
         cp.wait_send()
         cp.wait_recv()
 
@@ -148,37 +158,29 @@
 
     n_lo = n_core
     n_plane = n_ten // n_lo
-    rows_g, w_own = pl.pallas_call(
+    rows_g, w_own, rows_other, w_other, hidden_other = pl.pallas_call(
         lambda *refs: _gather_kernel(n_chip, n_lo, *refs),
         out_shape=(
             jax.ShapeDtypeStruct((n_plane, n_lo, seq_rows, out_grad.shape[1]), out_grad.dtype),
             jax.ShapeDtypeStruct((n_chip, width, ff), w_down.dtype),
-        ),
-        in_specs=[ANY, ANY],
-        out_specs=(ANY, ANY),
-        scratch_shapes=[pltpu.SemaphoreType.DMA((1,)), pltpu.SemaphoreType.DMA((1,)),
-                        pltpu.SemaphoreType.DMA((n_plane // 2,)),
-                        pltpu.SemaphoreType.DMA((n_plane // 2,)),
-                        pltpu.SemaphoreType.DMA((n_plane // 2,)),
-                        pltpu.SemaphoreType.DMA((n_plane // 2,)),
-                        pltpu.SemaphoreType.DMA((n_chip,)), pltpu.SemaphoreType.DMA((n_chip,)),
-                        pltpu.SemaphoreType.DMA((2,))],
-        compiler_params=_params(0),
-    )(out_grad, w_down)
-
-    w_other, rows_other, hidden_other = pl.pallas_call(
-        _pair_kernel,
-        out_shape=(
-            jax.ShapeDtypeStruct(w_own.shape, w_own.dtype),
-            jax.ShapeDtypeStruct((n_plane,) + rows_g.shape[2:], rows_g.dtype),
+            jax.ShapeDtypeStruct((n_plane, seq_rows, out_grad.shape[1]), out_grad.dtype),
+            jax.ShapeDtypeStruct((n_chip, width, ff), w_down.dtype),
             jax.ShapeDtypeStruct(hidden.shape, hidden.dtype),
         ),
         in_specs=[ANY, ANY, ANY],
-        out_specs=(ANY, ANY, ANY),
-        scratch_shapes=[pltpu.SemaphoreType.DMA((2,)), pltpu.SemaphoreType.DMA((2,)),
-                        pltpu.SemaphoreType.DMA((n_plane,)), pltpu.SemaphoreType.DMA((n_plane,))],
-        compiler_params=_params(1),
-    )(w_own, rows_g, hidden)
+        out_specs=(ANY, ANY, ANY, ANY, ANY),
+        scratch_shapes=[pltpu.SemaphoreType.DMA((1,)), pltpu.SemaphoreType.DMA((1,)),
+                        pltpu.SemaphoreType.DMA((n_plane // 2,)),
+                        pltpu.SemaphoreType.DMA((n_plane // 2,)),
+                        pltpu.SemaphoreType.DMA((n_plane // 2,)),
+                        pltpu.SemaphoreType.DMA((n_plane // 2,)),
+                        pltpu.SemaphoreType.DMA((n_chip,)), pltpu.SemaphoreType.DMA((n_chip,)),
+                        pltpu.SemaphoreType.DMA((1,)), pltpu.SemaphoreType.DMA((1,)),
+                        pltpu.SemaphoreType.DMA((n_chip,)), pltpu.SemaphoreType.DMA((n_chip,)),
+                        pltpu.SemaphoreType.DMA((n_plane,)), pltpu.SemaphoreType.DMA((n_plane,)),
+                        pltpu.SemaphoreType.DMA((2,))],
+        compiler_params=_params(0),
+    )(out_grad, w_down, hidden)
 
     rows_mine = lax.dynamic_index_in_dim(rows_g, core, 1, keepdims=False)
     rows_theirs = lax.dynamic_index_in_dim(rows_g, 1 - core, 1, keepdims=False)

time: 169 us -> 162 us (0.959)
  Pallas kernels: 145 us -> 139 us
    pallas_call x1 -> x0, Pallas kernels: 11.4 us -> none  [body(): pl.pallas_call(_pair_kernel, out_shape=(jax.ShapeDtypeStruct(w_own.shape,...]
    pallas_call x1, Pallas kernels: 72.1 us -> 76.2 us  [body(): pl.pallas_call(lambda *refs: _gather_kernel(n_chip, n_lo, *refs), out_sha...]
where the time goes in v6:
time: 162 us
  Pallas kernels  139 us (86%)
  matrix products  15.8 us (10%)
  other arithmetic  6.42 us (4%)
    pallas_call x1, Pallas kernels, body(): pl.pallas_call(lambda *refs: _gather_kernel(n_chip, n_lo, *refs), out_sha...  76.2 us
    pallas_call x1, Pallas kernels, body(): pl.pallas_call(lambda *refs: _scatter_kernel(n_chip, *refs), out_shape=ja...  62.5 us
    dot_general x1, matrix products, body(): jnp.einsum('rtk,rkf->tf', rows_theirs, w_other, preferred_element_type=jn...  5.15 us
    dot_general x1, matrix products, body(): jnp.einsum('rtk,tf->rkf', rows_other, hidden_other, preferred_element_typ...  4.17 us
    dot_general x1, matrix products, body(): jnp.einsum('rtk,rkf->tf', rows_mine, w_own, preferred_element_type=jnp.fl...  4.12 us

profile of v6, /device:TPU:26, one launch (start us, length us, event | category | flops | bytes accessed | tf_op | source)
XLA Modules:
  0.0 161.9 jit_solution(18012819134257640520)
XLA Ops:
  0.6 3.0 %fusion.9.refs_2_ = bf16[512,896]{1,0:T(8,128)(2,1)} fusion(bf16[512,896]{1,0:T(8,128)(2,1)} %param.6, bf16[512,896]{1,0:T(8,128)(2,1)} %param.5), kind=kLoop, calls=%fused_computation.16 | loop fusion | flops 3670016 | bytes 2752512 | tf_op jit(solution)/shard_map/convert_element_type | solution.py:157
  3.6 76.2 %shard_map.67 = (bf16[8,2,512,256]{3,2,1,0:T(8,128)(2,1)}, bf16[8,256,896]{2,1,0:T(8,128)(2,1)}, bf16[8,512,256]{2,1,0:T(8,128)(2,1)}, bf16[8,256,896]{2,1,0:T(8,128)(2,1)}, bf16[512,896]{1,0:T(8,128)(2,1)}) custom-call(bf16[512,256]{1,0:T(8,128)(2,1)} %refs_0_.1, bf16[256,896]{1,0:T(8,128)(2,1)} %refs_1_.1, bf16[512,896]{1,0:T(8,128)(2,1)} %fusion.9.refs_2_), custom_call_target="tpu_custom_call" | custom-call | tf_op jit(solution)/shard_map/pallas_call | solution.py:161
  79.7 0.0 copy-start.2
  79.8 0.0 copy-start.3
  79.8 0.0 copy-start.5
  79.8 0.0 copy-start.6
  79.8 5.2 %fusion = f32[512,896,1]{1,0,2:T(8,128)S(1)} fusion(bf16[8,256,896]{2,1,0:T(8,128)(2,1)} %get-tuple-element.10, bf16[8,2,512,256]{3,2,1,0:T(8,128)(2,1)} %get-tuple-element.8, s32[]{:T(128)S(6)} %select_n.8), kind=kOutput, calls=%fused_computation.7 | convolution fusion | flops 1879048192 | bytes 7602180 | tf_op jit(solution)/shard_map/rtk,rkf->tf/dot_general | solution.py:189
  85.0 0.0 copy-done.2
  85.0 0.0 copy-done.3
  85.0 0.0 copy-done.5
  85.0 0.3 copy-done.6
  85.3 0.0 copy-start
  85.3 4.1 %multiply_convert_fusion = (bf16[512,896]{1,0:T(8,128)(2,1)}, bf16[512,896]{1,0:T(8,128)(2,1)}) fusion(bf16[512,896]{1,0:T(8,128)(2,1)S(1)} %copy-done.2, bf16[512,896]{1,0:T(8,128)(2,1)S(1)} %copy-done.3, f32[512,896,1]{1,0,2:T(8,128)S(1)} %fusion, bf16[8,256,896]{2,1,0:T(8,128)(2,1)S(1)} %copy-done.6, bf16[8,2,512,256]{3,2,1,0:T(8,128)(2,1)S(1)} %copy-done.5, ...), kind=kOutput, calls=%fused_computation.25 | convolution fusion | flops 1886388224 | bytes 11272196 | tf_op jit(solution)/shard_map/rtk,rkf->tf/dot_general | solution.py:187
  89.4 0.0 copy-done
  89.4 0.0 copy-start.1
  89.4 0.0 copy-start.4
  89.4 2.4 %fusion.2 = f32[8,256,896]{2,1,0:T(8,128)S(1)} fusion(bf16[8,2,512,256]{3,2,1,0:T(8,128)(2,1)S(1)} %copy-done.5, s32[]{:T(128)S(6)} %select_n.7, bf16[512,896]{1,0:T(8,128)(2,1)S(1)} %copy-done), kind=kOutput, calls=%fused_computation.9 | convolution fusion | flops 1879048192 | bytes 10354692 | tf_op jit(solution)/shard_map/rtk,tf->rkf/dot_general | solution.py:191
  91.8 0.0 copy-done.1
  91.8 0.0 copy-done.4
  91.8 4.2 %add_convert_fusion.refs_0_ = bf16[8,256,896]{2,1,0:T(8,128)(2,1)} fusion(f32[8,256,896]{2,1,0:T(8,128)S(1)} %fusion.2, bf16[8,512,256]{2,1,0:T(8,128)(2,1)S(1)} %copy-done.1, bf16[512,896]{1,0:T(8,128)(2,1)S(1)} %copy-done.4), kind=kOutput, calls=%fused_computation.1 | convolution fusion | flops 1882718208 | bytes 14024704 | tf_op jit(solution)/shard_map/rtk,tf->rkf/dot_general | solution.py:193
  96.0 62.5 %shard_map.68 = bf16[8,256,896]{2,1,0:T(8,128)(2,1)} custom-call(bf16[8,256,896]{2,1,0:T(8,128)(2,1)} %add_convert_fusion.refs_0_), custom_call_target="tpu_custom_call" | custom-call | tf_op jit(solution)/shard_map/pallas_call | solution.py:195
  158.5 2.6 %convert_reduce_fusion = f32[256,896]{1,0:T(8,128)S(1)} fusion(bf16[8,256,896]{2,1,0:T(8,128)(2,1)} %shard_map.68), kind=kLoop, calls=%fused_computation | loop fusion | flops 3440640 | bytes 4587520 | tf_op jit(solution)/shard_map/reduce_sum | solution.py:204
  161.1 0.8 multiply_convert_fusion.1
Async XLA Ops:
  79.7 5.2 %copy-start.2 = (bf16[512,896]{1,0:T(8,128)(2,1)S(1)}, bf16[512,896]{1,0:T(8,128)(2,1)}, u32[]{:S(2)}) copy-start(bf16[512,896]{1,0:T(8,128)(2,1)} %param.5) | copy-start | bytes 2752516
  79.8 5.2 %copy-start.3 = (bf16[512,896]{1,0:T(8,128)(2,1)S(1)}, bf16[512,896]{1,0:T(8,128)(2,1)}, u32[]{:S(2)}) copy-start(bf16[512,896]{1,0:T(8,128)(2,1)} %param.6) | copy-start | bytes 2752516
  79.8 5.2 %copy-start.5 = (bf16[8,2,512,256]{3,2,1,0:T(8,128)(2,1)S(1)}, bf16[8,2,512,256]{3,2,1,0:T(8,128)(2,1)}, u32[]{:S(2)}) copy-start(bf16[8,2,512,256]{3,2,1,0:T(8,128)(2,1)} %get-tuple-element.8) | copy-start | bytes 12582916
  79.8 5.5 %copy-start.6 = (bf16[8,256,896]{2,1,0:T(8,128)(2,1)S(1)}, bf16[8,256,896]{2,1,0:T(8,128)(2,1)}, u32[]{:S(2)}) copy-start(bf16[8,256,896]{2,1,0:T(8,128)(2,1)} %get-tuple-element.9) | copy-start | bytes 11010052
  85.3 4.1 %copy-start = (bf16[512,896]{1,0:T(8,128)(2,1)S(1)}, bf16[512,896]{1,0:T(8,128)(2,1)}, u32[]{:S(2)}) copy-start(bf16[512,896]{1,0:T(8,128)(2,1)} %fusion.9.refs_2_) | copy-start | bytes 2752516
  89.4 2.4 %copy-start.1 = (bf16[8,512,256]{2,1,0:T(8,128)(2,1)S(1)}, bf16[8,512,256]{2,1,0:T(8,128)(2,1)}, u32[]{:S(2)}) copy-start(bf16[8,512,256]{2,1,0:T(8,128)(2,1)} %get-tuple-element.11) | copy-start | bytes 6291460
  89.4 2.4 %copy-start.4 = (bf16[512,896]{1,0:T(8,128)(2,1)S(1)}, bf16[512,896]{1,0:T(8,128)(2,1)}, u32[]{:S(2)}) copy-start(bf16[512,896]{1,0:T(8,128)(2,1)} %get-tuple-element.12) | copy-start | bytes 2752516

commit v7 on v6

--- a/solution.py
+++ b/solution.py
@@ -115,7 +115,8 @@
         cp.wait_recv()
 
 
-def _scatter_kernel(n_chip, part_ref, recv_out, send, recv, own_sem):
+def _scatter_kernel(n_chip, tile, part_ref, rows_ref, w_ref, wo_ref, gate_ref, up_ref,
+                    recv_out, gate_out, up_out, send, recv, own_sem):
     chip, core, ten = _where()
     barrier = pltpu.get_barrier_semaphore()
     for k in range(1, n_chip):
@@ -132,6 +133,27 @@
             device_id=(dest, core, ten), device_id_type=MESH)
         cp.start()
         copies.append(cp)
+
+    def one_tile(i, carry):
+        rows = pl.ds(pl.multiple_of(i * tile, tile), tile)
+        acc = jnp.zeros((tile, gate_ref.shape[1]), jnp.float32)
+        for r in range(w_ref.shape[0]):
+            acc += jnp.dot(rows_ref[r, core, rows, :], w_ref[r],
+                           preferred_element_type=jnp.float32)
+            acc += jnp.dot(rows_ref[r, 1 - core, rows, :], wo_ref[r],
+                           preferred_element_type=jnp.float32)
+        gate_wide = gate_ref[rows, :].astype(jnp.float32)
+        up_wide = up_ref[rows, :].astype(jnp.float32)
+        sigmoid_gate = jax.nn.sigmoid(gate_wide)
+        activated = gate_wide * sigmoid_gate
+        gate_out[rows, :] = (
+            acc * up_wide * sigmoid_gate * (1.0 + gate_wide * (1.0 - sigmoid_gate))
+        ).astype(gate_out.dtype)
+        up_out[rows, :] = (acc * activated).astype(up_out.dtype)
+        return carry
+
+    lax.fori_loop(0, gate_ref.shape[0] // tile, one_tile, 0)
+
     own.wait()
     for cp in copies:
         cp.wait_send()
@@ -183,30 +205,25 @@
     )(out_grad, w_down, hidden)
 
     rows_mine = lax.dynamic_index_in_dim(rows_g, core, 1, keepdims=False)
-    rows_theirs = lax.dynamic_index_in_dim(rows_g, 1 - core, 1, keepdims=False)
-    hidden_grad = jnp.einsum(
-        "rtk,rkf->tf", rows_mine, w_own, preferred_element_type=jnp.float32
-    ) + jnp.einsum("rtk,rkf->tf", rows_theirs, w_other, preferred_element_type=jnp.float32)
-
     partial = jnp.einsum(
         "rtk,tf->rkf", rows_mine, hidden, preferred_element_type=jnp.float32
     ) + jnp.einsum("rtk,tf->rkf", rows_other, hidden_other, preferred_element_type=jnp.float32)
 
-    received = pl.pallas_call(
-        lambda *refs: _scatter_kernel(n_chip, *refs),
-        out_shape=jax.ShapeDtypeStruct(partial.shape, jnp.bfloat16),
-        in_specs=[ANY],
-        out_specs=ANY,
+    vmem = pl.BlockSpec(memory_space=pltpu.VMEM)
+    received, gate_grad, up_grad = pl.pallas_call(
+        lambda *refs: _scatter_kernel(n_chip, min(128, seq_rows), *refs),
+        out_shape=(
+            jax.ShapeDtypeStruct(partial.shape, jnp.bfloat16),
+            jax.ShapeDtypeStruct(gate_act.shape, jnp.bfloat16),
+            jax.ShapeDtypeStruct(up_act.shape, jnp.bfloat16),
+        ),
+        in_specs=[ANY, vmem, vmem, vmem, vmem, vmem],
+        out_specs=(ANY, vmem, vmem),
         scratch_shapes=[pltpu.SemaphoreType.DMA((n_chip,)), pltpu.SemaphoreType.DMA((n_chip,)),
                         pltpu.SemaphoreType.DMA((1,))],
         compiler_params=_params(2),
-    )(partial.astype(jnp.bfloat16))
+    )(partial.astype(jnp.bfloat16), rows_g, w_own, w_other, gate_act, up_act)
     summed = jnp.sum(received.astype(jnp.float32), axis=0)
-
-    gate_grad = (
-        hidden_grad * up_wide * sigmoid_gate * (1.0 + gate_wide * (1.0 - sigmoid_gate))
-    ).astype(jnp.bfloat16)
-    up_grad = (hidden_grad * activated).astype(jnp.bfloat16)
     down_grad = (summed * grad_scale).astype(jnp.bfloat16)
     return (gate_grad, up_grad, down_grad)
 

time: 162 us -> 163 us (level)
  matrix products: 15.8 us -> 8.79 us
  Pallas kernels: 139 us -> 145 us
    dot_general x2 -> x0, matrix products: 9.27 us -> none  [the longest x1 5.15 us: body(): jnp.einsum('rtk,rkf->tf', rows_theirs, w_other, preferred_element_type=jn...]
    pallas_call x1, Pallas kernels: 62.5 us -> 68.5 us  [body(): pl.pallas_call(lambda *refs: _scatter_kernel(n_chip, min(128, seq_rows),...]
    dot_general x1, matrix products: 2.38 us -> 4.35 us  [body(): jnp.einsum('rtk,tf->rkf', rows_mine, hidden, preferred_element_type=jnp.f...]
where the time goes in v7:
time: 163 us
  Pallas kernels  145 us (89%)
  matrix products  8.79 us (5%)
  other arithmetic  6.53 us (4%)
  local copies, waits for them, and re-layouts  1.86 us (1%)
    pallas_call x1, Pallas kernels, body(): pl.pallas_call(lambda *refs: _gather_kernel(n_chip, n_lo, *refs), out_sha...  76.2 us
    pallas_call x1, Pallas kernels, body(): pl.pallas_call(lambda *refs: _scatter_kernel(n_chip, min(128, seq_rows),...  68.5 us
    dot_general x1, matrix products, body(): jnp.einsum('rtk,tf->rkf', rows_other, hidden_other, preferred_element_typ...  4.44 us
    dot_general x1, matrix products, body(): jnp.einsum('rtk,tf->rkf', rows_mine, hidden, preferred_element_type=jnp.f...  4.35 us

profile of v7, /device:TPU:26, one launch (start us, length us, event | category | flops | bytes accessed | tf_op | source)
XLA Modules:
  0.0 162.5 jit_solution(9502303399283215932)
XLA Ops:
  0.6 2.9 %fusion.7.refs_2_ = bf16[512,896]{1,0:T(8,128)(2,1)} fusion(bf16[512,896]{1,0:T(8,128)(2,1)} %refs_5_.1, bf16[512,896]{1,0:T(8,128)(2,1)} %refs_4_.1), kind=kLoop, calls=%fused_computation.11 | loop fusion | flops 3670016 | bytes 2752512 | tf_op jit(solution)/shard_map/convert_element_type | solution.py:179
  3.6 76.2 %shard_map.67 = (bf16[8,2,512,256]{3,2,1,0:T(8,128)(2,1)}, bf16[8,256,896]{2,1,0:T(8,128)(2,1)}, bf16[8,512,256]{2,1,0:T(8,128)(2,1)}, bf16[8,256,896]{2,1,0:T(8,128)(2,1)}, bf16[512,896]{1,0:T(8,128)(2,1)}) custom-call(bf16[512,256]{1,0:T(8,128)(2,1)} %refs_0_.1, bf16[256,896]{1,0:T(8,128)(2,1)} %refs_1_.1, bf16[512,896]{1,0:T(8,128)(2,1)} %fusion.7.refs_2_), custom_call_target="tpu_custom_call" | custom-call | tf_op jit(solution)/shard_map/pallas_call | solution.py:183
  79.7 0.0 copy-start
  79.8 0.0 copy-start.3
  79.8 4.4 %fusion = f32[8,256,896]{2,1,0:T(8,128)S(1)} fusion(bf16[8,2,512,256]{3,2,1,0:T(8,128)(2,1)} %get-tuple-element.11.refs_1_, s32[]{:T(128)S(6)} %select_n.4, bf16[512,896]{1,0:T(8,128)(2,1)} %fusion.7.refs_2_), kind=kOutput, calls=%fused_computation.4 | convolution fusion | flops 1879048192 | bytes 10354692 | tf_op jit(solution)/shard_map/rtk,tf->rkf/dot_general | solution.py:208
  84.1 0.0 copy-done
  84.1 0.0 copy-done.3
  84.1 4.4 %add_convert_fusion.refs_0_ = bf16[8,256,896]{2,1,0:T(8,128)(2,1)} fusion(f32[8,256,896]{2,1,0:T(8,128)S(1)} %fusion, bf16[8,512,256]{2,1,0:T(8,128)(2,1)S(1)} %copy-done, bf16[512,896]{1,0:T(8,128)(2,1)S(1)} %copy-done.3), kind=kOutput, calls=%fused_computation.1 | convolution fusion | flops 1882718208 | bytes 14024704 | tf_op jit(solution)/shard_map/rtk,tf->rkf/dot_general | solution.py:210
  88.6 68.5 %shard_map.68 = (bf16[8,256,896]{2,1,0:T(8,128)(2,1)}, bf16[512,896]{1,0:T(8,128)(2,1)}, bf16[512,896]{1,0:T(8,128)(2,1)}) custom-call(bf16[8,256,896]{2,1,0:T(8,128)(2,1)} %add_convert_fusion.refs_0_, bf16[8,2,512,256]{3,2,1,0:T(8,128)(2,1)} %get-tuple-element.11.refs_1_, bf16[8,256,896]{2,1,0:T(8,128)(2,1)} %get-tuple-element.14.refs_2_, ...), custom_call_target="tpu_custom_call" | custom-call | tf_op jit(solution)/shard_map/pallas_call | solution.py:213
  157.1 0.0 copy-start.2
  157.1 0.0 copy-start.1
  157.1 2.7 %convert_reduce_fusion = f32[256,896]{1,0:T(8,128)S(1)} fusion(bf16[8,256,896]{2,1,0:T(8,128)(2,1)} %get-tuple-element.18), kind=kLoop, calls=%fused_computation | loop fusion | flops 3440640 | bytes 4587520 | tf_op jit(solution)/shard_map/reduce_sum | solution.py:226
  159.8 0.8 multiply_convert_fusion
  160.7 0.0 copy-done.2
  160.7 0.9 copy.14
  161.6 0.0 copy-done.1
  161.6 0.9 copy.15
Async XLA Ops:
  79.7 4.4 %copy-start = (bf16[8,512,256]{2,1,0:T(8,128)(2,1)S(1)}, bf16[8,512,256]{2,1,0:T(8,128)(2,1)}, u32[]{:S(2)}) copy-start(bf16[8,512,256]{2,1,0:T(8,128)(2,1)} %get-tuple-element.12) | copy-start | bytes 6291460
  79.8 4.4 %copy-start.3 = (bf16[512,896]{1,0:T(8,128)(2,1)S(1)}, bf16[512,896]{1,0:T(8,128)(2,1)}, u32[]{:S(2)}) copy-start(bf16[512,896]{1,0:T(8,128)(2,1)} %get-tuple-element.13) | copy-start | bytes 2752516
  157.1 3.6 %copy-start.2 = (bf16[512,896]{1,0:T(8,128)(2,1)S(1)}, bf16[512,896]{1,0:T(8,128)(2,1)}, u32[]{:S(2)}) copy-start(bf16[512,896]{1,0:T(8,128)(2,1)} %get-tuple-element.22) | copy-start | bytes 2752516
  157.1 4.5 %copy-start.1 = (bf16[512,896]{1,0:T(8,128)(2,1)S(1)}, bf16[512,896]{1,0:T(8,128)(2,1)}, u32[]{:S(2)}) copy-start(bf16[512,896]{1,0:T(8,128)(2,1)} %get-tuple-element.23) | copy-start | bytes 2752516

commit v8 on v7

--- a/solution.py
+++ b/solution.py
@@ -115,8 +115,9 @@
         cp.wait_recv()
 
 
-def _scatter_kernel(n_chip, tile, part_ref, rows_ref, w_ref, wo_ref, gate_ref, up_ref,
-                    recv_out, gate_out, up_out, send, recv, own_sem):
+def _scatter_kernel(n_chip, tile, part_ref, rows_hbm, w_hbm, wo_hbm, gate_hbm, up_hbm,
+                    recv_out, gate_out, up_out, send, recv, own_sem,
+                    rows_ref, w_ref, wo_ref, gate_ref, up_ref, load_sem):
     chip, core, ten = _where()
     barrier = pltpu.get_barrier_semaphore()
     for k in range(1, n_chip):
@@ -133,6 +134,13 @@
             device_id=(dest, core, ten), device_id_type=MESH)
         cp.start()
         copies.append(cp)
+    loads = [pltpu.make_async_copy(src, dst, load_sem.at[i]) for i, (src, dst) in enumerate(
+        ((rows_hbm, rows_ref), (w_hbm, w_ref), (wo_hbm, wo_ref), (gate_hbm, gate_ref),
+         (up_hbm, up_ref)))]
+    for ld in loads:
+        ld.start()
+    for ld in loads:
+        ld.wait()
 
     def one_tile(i, carry):
         rows = pl.ds(pl.multiple_of(i * tile, tile), tile)
@@ -217,10 +225,16 @@
             jax.ShapeDtypeStruct(gate_act.shape, jnp.bfloat16),
             jax.ShapeDtypeStruct(up_act.shape, jnp.bfloat16),
         ),
-        in_specs=[ANY, vmem, vmem, vmem, vmem, vmem],
+        in_specs=[ANY, ANY, ANY, ANY, ANY, ANY],
         out_specs=(ANY, vmem, vmem),
         scratch_shapes=[pltpu.SemaphoreType.DMA((n_chip,)), pltpu.SemaphoreType.DMA((n_chip,)),
-                        pltpu.SemaphoreType.DMA((1,))],
+                        pltpu.SemaphoreType.DMA((1,)),
+                        pltpu.VMEM(rows_g.shape, rows_g.dtype),
+                        pltpu.VMEM(w_own.shape, w_own.dtype),
+                        pltpu.VMEM(w_other.shape, w_other.dtype),
+                        pltpu.VMEM(gate_act.shape, gate_act.dtype),
+                        pltpu.VMEM(up_act.shape, up_act.dtype),
+                        pltpu.SemaphoreType.DMA((5,))],
         compiler_params=_params(2),
     )(partial.astype(jnp.bfloat16), rows_g, w_own, w_other, gate_act, up_act)
     summed = jnp.sum(received.astype(jnp.float32), axis=0)

time: 163 us -> 158 us (0.969)
  Pallas kernels: 145 us -> 140 us
    pallas_call x1, Pallas kernels: 68.5 us -> 63.7 us  [body(): pl.pallas_call(lambda *refs: _scatter_kernel(n_chip, min(128, seq_rows),...]
where the time goes in v8:
time: 158 us
  Pallas kernels  140 us (89%)
  matrix products  8.79 us (6%)
  other arithmetic  6.53 us (4%)
  local copies, waits for them, and re-layouts  1.86 us (1%)
    pallas_call x1, Pallas kernels, body(): pl.pallas_call(lambda *refs: _gather_kernel(n_chip, n_lo, *refs), out_sha...  76.2 us
    pallas_call x1, Pallas kernels, body(): pl.pallas_call(lambda *refs: _scatter_kernel(n_chip, min(128, seq_rows),...  63.7 us
    dot_general x1, matrix products, body(): jnp.einsum('rtk,tf->rkf', rows_other, hidden_other, preferred_element_typ...  4.44 us
    dot_general x1, matrix products, body(): jnp.einsum('rtk,tf->rkf', rows_mine, hidden, preferred_element_type=jnp.f...  4.35 us

profile of v8, /device:TPU:26, one launch (start us, length us, event | category | flops | bytes accessed | tf_op | source)
XLA Modules:
  0.0 157.8 jit_solution(3123524464560909871)
XLA Ops:
  0.6 2.9 %fusion.7.refs_2_ = bf16[512,896]{1,0:T(8,128)(2,1)} fusion(bf16[512,896]{1,0:T(8,128)(2,1)} %refs_5_.1, bf16[512,896]{1,0:T(8,128)(2,1)} %refs_4_.1), kind=kLoop, calls=%fused_computation.11 | loop fusion | flops 3670016 | bytes 2752512 | tf_op jit(solution)/shard_map/convert_element_type | solution.py:187
  3.6 76.2 %shard_map.67 = (bf16[8,2,512,256]{3,2,1,0:T(8,128)(2,1)}, bf16[8,256,896]{2,1,0:T(8,128)(2,1)}, bf16[8,512,256]{2,1,0:T(8,128)(2,1)}, bf16[8,256,896]{2,1,0:T(8,128)(2,1)}, bf16[512,896]{1,0:T(8,128)(2,1)}) custom-call(bf16[512,256]{1,0:T(8,128)(2,1)} %refs_0_.1, bf16[256,896]{1,0:T(8,128)(2,1)} %refs_1_.1, bf16[512,896]{1,0:T(8,128)(2,1)} %fusion.7.refs_2_), custom_call_target="tpu_custom_call" | custom-call | tf_op jit(solution)/shard_map/pallas_call | solution.py:191
  79.7 0.0 copy-start
  79.8 0.0 copy-start.3
  79.8 4.4 %fusion = f32[8,256,896]{2,1,0:T(8,128)S(1)} fusion(bf16[8,2,512,256]{3,2,1,0:T(8,128)(2,1)} %get-tuple-element.11.refs_1_, s32[]{:T(128)S(6)} %select_n.4, bf16[512,896]{1,0:T(8,128)(2,1)} %fusion.7.refs_2_), kind=kOutput, calls=%fused_computation.4 | convolution fusion | flops 1879048192 | bytes 10354692 | tf_op jit(solution)/shard_map/rtk,tf->rkf/dot_general | solution.py:216
  84.1 0.0 copy-done
  84.1 0.0 copy-done.3
  84.1 4.4 %add_convert_fusion.refs_0_ = bf16[8,256,896]{2,1,0:T(8,128)(2,1)} fusion(f32[8,256,896]{2,1,0:T(8,128)S(1)} %fusion, bf16[8,512,256]{2,1,0:T(8,128)(2,1)S(1)} %copy-done, bf16[512,896]{1,0:T(8,128)(2,1)S(1)} %copy-done.3), kind=kOutput, calls=%fused_computation.1 | convolution fusion | flops 1882718208 | bytes 14024704 | tf_op jit(solution)/shard_map/rtk,tf->rkf/dot_general | solution.py:218
  88.6 63.7 %shard_map.68 = (bf16[8,256,896]{2,1,0:T(8,128)(2,1)}, bf16[512,896]{1,0:T(8,128)(2,1)}, bf16[512,896]{1,0:T(8,128)(2,1)}) custom-call(bf16[8,256,896]{2,1,0:T(8,128)(2,1)} %add_convert_fusion.refs_0_, bf16[8,2,512,256]{3,2,1,0:T(8,128)(2,1)} %get-tuple-element.11.refs_1_, bf16[8,256,896]{2,1,0:T(8,128)(2,1)} %get-tuple-element.14.refs_2_, ...), custom_call_target="tpu_custom_call" | custom-call | tf_op jit(solution)/shard_map/pallas_call | solution.py:221
  152.3 0.0 copy-start.2
  152.3 0.0 copy-start.1
  152.4 2.7 %convert_reduce_fusion = f32[256,896]{1,0:T(8,128)S(1)} fusion(bf16[8,256,896]{2,1,0:T(8,128)(2,1)} %get-tuple-element.18), kind=kLoop, calls=%fused_computation | loop fusion | flops 3440640 | bytes 4587520 | tf_op jit(solution)/shard_map/reduce_sum | solution.py:240
  155.1 0.8 multiply_convert_fusion
  155.9 0.0 copy-done.2
  155.9 0.9 copy.14
  156.9 0.0 copy-done.1
  156.9 0.9 copy.15
Async XLA Ops:
  79.7 4.4 %copy-start = (bf16[8,512,256]{2,1,0:T(8,128)(2,1)S(1)}, bf16[8,512,256]{2,1,0:T(8,128)(2,1)}, u32[]{:S(2)}) copy-start(bf16[8,512,256]{2,1,0:T(8,128)(2,1)} %get-tuple-element.12) | copy-start | bytes 6291460
  79.8 4.4 %copy-start.3 = (bf16[512,896]{1,0:T(8,128)(2,1)S(1)}, bf16[512,896]{1,0:T(8,128)(2,1)}, u32[]{:S(2)}) copy-start(bf16[512,896]{1,0:T(8,128)(2,1)} %get-tuple-element.13) | copy-start | bytes 2752516
  152.3 3.6 %copy-start.2 = (bf16[512,896]{1,0:T(8,128)(2,1)S(1)}, bf16[512,896]{1,0:T(8,128)(2,1)}, u32[]{:S(2)}) copy-start(bf16[512,896]{1,0:T(8,128)(2,1)} %get-tuple-element.22) | copy-start | bytes 2752516
  152.3 4.5 %copy-start.1 = (bf16[512,896]{1,0:T(8,128)(2,1)S(1)}, bf16[512,896]{1,0:T(8,128)(2,1)}, u32[]{:S(2)}) copy-start(bf16[512,896]{1,0:T(8,128)(2,1)} %get-tuple-element.23) | copy-start | bytes 2752516

commit v9 on v8

--- a/solution.py
+++ b/solution.py
@@ -18,8 +18,9 @@
 
 
 def _gather_kernel(n_chip, n_lo, og_ref, w_ref, hid_ref, rows_out, w_out, rows_other,
-                   w_other, hid_other, x_send, x_recv, r_send, r_recv, l_send, l_recv,
-                   w_send, w_recv, f_send, f_recv, fw_send, fw_recv, fr_send, fr_recv, own_sem):
+                   w_other, hid_other, part_out, x_send, x_recv, r_send, r_recv, l_send, l_recv,
+                   w_send, w_recv, f_send, f_recv, fw_send, fw_recv, fr_send, fr_recv,
+                   own_sem, rows_v, ro_v, hid_v, ho_v, load_sem):
     chip, core, ten = _where()
     n_plane = rows_out.shape[0]
     plane, lo = ten // n_lo, ten % n_lo
@@ -104,15 +105,38 @@
         for s in range(n_steps):
             ring[(d, s)].wait_send()
     fwd_rows(n_steps)
+
+    loads = [pltpu.make_async_copy(rows_out.at[r, core], rows_v.at[r], load_sem.at[r])
+             for r in range(n_plane)]
+    loads.append(pltpu.make_async_copy(hid_ref, hid_v, load_sem.at[n_plane]))
+    for ld in loads:
+        ld.start()
+    for cp in forwards:
+        cp.wait_recv()
+    later = [pltpu.make_async_copy(rows_other, ro_v, load_sem.at[n_plane + 1]),
+             pltpu.make_async_copy(hid_other, ho_v, load_sem.at[n_plane + 2])]
+    for ld in later:
+        ld.start()
+    for ld in loads + later:
+        ld.wait()
+    for r in range(n_plane):
+        part = lax.dot_general(rows_v[r], hid_v[...], (((0,), (0,)), ((), ())),
+                               preferred_element_type=jnp.float32)
+        part += lax.dot_general(ro_v[r], ho_v[...], (((0,), (0,)), ((), ())),
+                                preferred_element_type=jnp.float32)
+        part_out[r] = part.astype(part_out.dtype)
+
+    n_before = len(forwards)
     for k in range(1, n_chip):
         w_copies[k - 1].wait_recv()
         fwd_w(k)
     own_w.wait()
     for cp in w_copies:
         cp.wait_send()
-    for cp in forwards:
+    for i, cp in enumerate(forwards):
         cp.wait_send()
-        cp.wait_recv()
+        if i >= n_before:
+            cp.wait_recv()
 
 
 def _scatter_kernel(n_chip, tile, part_ref, rows_hbm, w_hbm, wo_hbm, gate_hbm, up_hbm,
@@ -188,7 +212,8 @@
 
     n_lo = n_core
     n_plane = n_ten // n_lo
-    rows_g, w_own, rows_other, w_other, hidden_other = pl.pallas_call(
+    vmem = pl.BlockSpec(memory_space=pltpu.VMEM)
+    rows_g, w_own, rows_other, w_other, hidden_other, partial = pl.pallas_call(
         lambda *refs: _gather_kernel(n_chip, n_lo, *refs),
         out_shape=(
             jax.ShapeDtypeStruct((n_plane, n_lo, seq_rows, out_grad.shape[1]), out_grad.dtype),
@@ -196,9 +221,10 @@
             jax.ShapeDtypeStruct((n_plane, seq_rows, out_grad.shape[1]), out_grad.dtype),
             jax.ShapeDtypeStruct((n_chip, width, ff), w_down.dtype),
             jax.ShapeDtypeStruct(hidden.shape, hidden.dtype),
+            jax.ShapeDtypeStruct((n_chip, width, ff), jnp.bfloat16),
         ),
         in_specs=[ANY, ANY, ANY],
-        out_specs=(ANY, ANY, ANY, ANY, ANY),
+        out_specs=(ANY, ANY, ANY, ANY, ANY, vmem),
         scratch_shapes=[pltpu.SemaphoreType.DMA((1,)), pltpu.SemaphoreType.DMA((1,)),
                         pltpu.SemaphoreType.DMA((n_plane // 2,)),
                         pltpu.SemaphoreType.DMA((n_plane // 2,)),
@@ -208,16 +234,15 @@
                         pltpu.SemaphoreType.DMA((1,)), pltpu.SemaphoreType.DMA((1,)),
                         pltpu.SemaphoreType.DMA((n_chip,)), pltpu.SemaphoreType.DMA((n_chip,)),
                         pltpu.SemaphoreType.DMA((n_plane,)), pltpu.SemaphoreType.DMA((n_plane,)),
-                        pltpu.SemaphoreType.DMA((2,))],
+                        pltpu.SemaphoreType.DMA((2,)),
+                        pltpu.VMEM((n_plane, seq_rows, out_grad.shape[1]), out_grad.dtype),
+                        pltpu.VMEM((n_plane, seq_rows, out_grad.shape[1]), out_grad.dtype),
+                        pltpu.VMEM(hidden.shape, hidden.dtype),
+                        pltpu.VMEM(hidden.shape, hidden.dtype),
+                        pltpu.SemaphoreType.DMA((n_plane + 3,))],
         compiler_params=_params(0),
     )(out_grad, w_down, hidden)
 
-    rows_mine = lax.dynamic_index_in_dim(rows_g, core, 1, keepdims=False)
-    partial = jnp.einsum(
-        "rtk,tf->rkf", rows_mine, hidden, preferred_element_type=jnp.float32
-    ) + jnp.einsum("rtk,tf->rkf", rows_other, hidden_other, preferred_element_type=jnp.float32)
-
-    vmem = pl.BlockSpec(memory_space=pltpu.VMEM)
     received, gate_grad, up_grad = pl.pallas_call(
         lambda *refs: _scatter_kernel(n_chip, min(128, seq_rows), *refs),
         out_shape=(
@@ -225,7 +250,7 @@
             jax.ShapeDtypeStruct(gate_act.shape, jnp.bfloat16),
             jax.ShapeDtypeStruct(up_act.shape, jnp.bfloat16),
         ),
-        in_specs=[ANY, ANY, ANY, ANY, ANY, ANY],
+        in_specs=[vmem, ANY, ANY, ANY, ANY, ANY],
         out_specs=(ANY, vmem, vmem),
         scratch_shapes=[pltpu.SemaphoreType.DMA((n_chip,)), pltpu.SemaphoreType.DMA((n_chip,)),
                         pltpu.SemaphoreType.DMA((1,)),
@@ -236,7 +261,7 @@
                         pltpu.VMEM(up_act.shape, up_act.dtype),
                         pltpu.SemaphoreType.DMA((5,))],
         compiler_params=_params(2),
-    )(partial.astype(jnp.bfloat16), rows_g, w_own, w_other, gate_act, up_act)
+    )(partial, rows_g, w_own, w_other, gate_act, up_act)
     summed = jnp.sum(received.astype(jnp.float32), axis=0)
     down_grad = (summed * grad_scale).astype(jnp.bfloat16)
     return (gate_grad, up_grad, down_grad)

time: 158 us -> 153 us (0.968)
  matrix products: 8.79 us -> 0 us
  Pallas kernels: 140 us -> 144 us
    dot_general x2 -> x0, matrix products: 8.79 us -> none  [the longest x1 4.44 us: body(): jnp.einsum('rtk,tf->rkf', rows_other, hidden_other, preferred_element_typ...]
    pallas_call x1, Pallas kernels: 63.7 us -> 65.7 us  [body(): pl.pallas_call(lambda *refs: _scatter_kernel(n_chip, min(128, seq_rows),...]
    pallas_call x1, Pallas kernels: 76.2 us -> 78.1 us  [body(): pl.pallas_call(lambda *refs: _gather_kernel(n_chip, n_lo, *refs), out_sha...]
where the time goes in v9:
time: 153 us
  Pallas kernels  144 us (94%)
  other arithmetic  6.48 us (4%)
  local copies, waits for them, and re-layouts  1.85 us (1%)
    pallas_call x1, Pallas kernels, body(): pl.pallas_call(lambda *refs: _gather_kernel(n_chip, n_lo, *refs), out_sha...  78.1 us
    pallas_call x1, Pallas kernels, body(): pl.pallas_call(lambda *refs: _scatter_kernel(n_chip, min(128, seq_rows),...  65.7 us

profile of v9, /device:TPU:26, one launch (start us, length us, event | category | flops | bytes accessed | tf_op | source)
XLA Modules:
  0.0 152.8 jit_solution(17301199120654660294)
XLA Ops:
  0.6 2.9 %fusion.4.refs_2_ = bf16[512,896]{1,0:T(8,128)(2,1)} fusion(bf16[512,896]{1,0:T(8,128)(2,1)} %refs_5_.1, bf16[512,896]{1,0:T(8,128)(2,1)} %refs_4_.1), kind=kLoop, calls=%fused_computation.7 | loop fusion | flops 3670016 | bytes 2752512 | tf_op jit(solution)/shard_map/convert_element_type | solution.py:211
  3.6 78.1 %shard_map.67 = (bf16[8,2,512,256]{3,2,1,0:T(8,128)(2,1)}, bf16[8,256,896]{2,1,0:T(8,128)(2,1)}, bf16[8,512,256]{2,1,0:T(8,128)(2,1)}, bf16[8,256,896]{2,1,0:T(8...) custom-call(bf16[512,256]{1,0:T(8,128)(2,1)} %refs_0_.1, bf16[256,896]{1,0:T(8,128)(2,1)} %refs_1_.1, ...), custom_call_target="tpu_custom_call" | custom-call | tf_op jit(solution)/shard_map/pallas_call | solution.py:216
  81.7 65.7 %shard_map.68 = (bf16[8,256,896]{2,1,0:T(8,128)(2,1)}, bf16[512,896]{1,0:T(8,128)(2,1)}, bf16[512,896]{1,0:T(8,128)(2,1)}) custom-call(bf16[8,256,896]{2,1,0:T(8,128)(2,1)} %get-tuple-element.10.refs_0_, bf16[8,2,512,256]{3,2,1,0:T(8,128)(2,1)} %get-tuple-element.11.refs_1_, bf16[8,256,896]{2,1,0:T(8,128)(2,1)} %get-tuple-element.12.refs_2_, ...), custom_call_target="tpu_custom_call" | custom-call | tf_op jit(solution)/shard_map/pallas_call | solution.py:246
  147.4 0.0 copy-start.1
  147.4 2.7 %convert_reduce_fusion = f32[256,896]{1,0:T(8,128)S(1)} fusion(bf16[8,256,896]{2,1,0:T(8,128)(2,1)} %get-tuple-element.16), kind=kLoop, calls=%fused_computation | loop fusion | flops 3440640 | bytes 4587520 | tf_op jit(solution)/shard_map/reduce_sum | solution.py:265
  150.1 0.0 copy-start
  150.1 0.8 multiply_convert_fusion
  151.0 0.0 copy-done.1
  151.0 0.9 copy.9
  151.9 0.0 copy-done
  151.9 0.9 copy.10
Async XLA Ops:
  147.4 3.6 %copy-start.1 = (bf16[512,896]{1,0:T(8,128)(2,1)S(1)}, bf16[512,896]{1,0:T(8,128)(2,1)}, u32[]{:S(2)}) copy-start(bf16[512,896]{1,0:T(8,128)(2,1)} %get-tuple-element.20) | copy-start | bytes 2752516
  150.1 1.8 %copy-start = (bf16[512,896]{1,0:T(8,128)(2,1)S(1)}, bf16[512,896]{1,0:T(8,128)(2,1)}, u32[]{:S(2)}) copy-start(bf16[512,896]{1,0:T(8,128)(2,1)} %get-tuple-element.21) | copy-start | bytes 2752516

commit v10 on v8

--- a/solution.py
+++ b/solution.py
@@ -17,9 +17,10 @@
     return lax.axis_index("chip"), lax.axis_index("core"), lax.axis_index("tensor")
 
 
-def _gather_kernel(n_chip, n_lo, og_ref, w_ref, hid_ref, rows_out, w_out, rows_other,
-                   w_other, hid_other, x_send, x_recv, r_send, r_recv, l_send, l_recv,
-                   w_send, w_recv, f_send, f_recv, fw_send, fw_recv, fr_send, fr_recv, own_sem):
+def _gather_kernel(n_chip, n_lo, og_ref, w_ref, hid_ref, rows_out, w_out, w_other, part_out,
+                   x_send, x_recv, r_send, r_recv, l_send, l_recv, w_send, w_recv,
+                   f_send, f_recv, fw_send, fw_recv, fr_send, fr_recv, own_sem,
+                   rows_v, ro_v, hid_v, ho_v, load_sem):
     chip, core, ten = _where()
     n_plane = rows_out.shape[0]
     plane, lo = ten // n_lo, ten % n_lo
@@ -44,10 +45,15 @@
     own_w = pltpu.make_async_copy(w_ref, w_out.at[chip], own_sem.at[1])
     own_r.start()
     own_w.start()
-    hid_cp = pltpu.make_async_remote_copy(hid_ref, hid_other, f_send.at[0], f_recv.at[0],
+    hid_cp = pltpu.make_async_remote_copy(hid_ref, ho_v, f_send.at[0], f_recv.at[0],
                                           device_id=other, device_id_type=MESH)
     hid_cp.start()
+    hid_ld = pltpu.make_async_copy(hid_ref, hid_v, load_sem.at[n_plane])
+    hid_ld.start()
     forwards = [hid_cp]
+    w_fwds = []
+    rows_fwd = {}
+    rows_ld = {}
 
     def fwd_w(k):
         r = (chip + n_chip - k) % n_chip
@@ -56,20 +62,35 @@
                                           device_id=other, device_id_type=MESH)
         cp.start()
         forwards.append(cp)
-
-    def fwd_rows(d):
+        w_fwds.append(cp)
+
+    def arrived(d):
         p = (plane + d) % n_plane
-        cp = pltpu.make_async_remote_copy(rows_out.at[p, 1 - core], rows_other.at[p],
+        cp = pltpu.make_async_remote_copy(rows_out.at[p, 1 - core], ro_v.at[p],
                                           fr_send.at[d], fr_recv.at[d],
                                           device_id=other, device_id_type=MESH)
         cp.start()
         forwards.append(cp)
+        rows_fwd[d] = cp
+        ld = pltpu.make_async_copy(rows_out.at[p, core], rows_v.at[p], load_sem.at[d])
+        ld.start()
+        rows_ld[d] = ld
+
+    def partial(d):
+        p = (plane + d) % n_plane
+        rows_ld[d].wait()
+        rows_fwd[d].wait_recv()
+        part = lax.dot_general(rows_v[p], hid_v[...], (((0,), (0,)), ((), ())),
+                               preferred_element_type=jnp.float32)
+        part += lax.dot_general(ro_v[p], ho_v[...], (((0,), (0,)), ((), ())),
+                                preferred_element_type=jnp.float32)
+        part_out[p] = part.astype(part_out.dtype)
 
     fwd_w(0)
     own_r.wait()
     side_cp.wait_send()
     side_cp.wait_recv()
-    fwd_rows(0)
+    arrived(0)
 
     n_steps = n_plane // 2
     ring = {}
@@ -93,17 +114,26 @@
             device_id=((chip + k) % n_chip, core, ten), device_id_type=MESH)
         cp.start()
         w_copies.append(cp)
+    hid_ld.wait()
+    hid_cp.wait_recv()
+    pending = [0]
     for s in range(1, n_steps):
         for d in ("r", "l"):
             ring[(d, s - 1)].wait_recv()
             ring[(d, s)].start()
-        fwd_rows(n_plane - s)
-        fwd_rows(s)
+        arrived(n_plane - s)
+        arrived(s)
+        for d in pending:
+            partial(d)
+        pending = [n_plane - s, s]
     for d in ("r", "l"):
         ring[(d, n_steps - 1)].wait_recv()
         for s in range(n_steps):
             ring[(d, s)].wait_send()
-    fwd_rows(n_steps)
+    arrived(n_steps)
+    for d in pending + [n_steps]:
+        partial(d)
+
     for k in range(1, n_chip):
         w_copies[k - 1].wait_recv()
         fwd_w(k)
@@ -112,6 +142,7 @@
         cp.wait_send()
     for cp in forwards:
         cp.wait_send()
+    for cp in w_fwds:
         cp.wait_recv()
 
 
@@ -188,17 +219,17 @@
 
     n_lo = n_core
     n_plane = n_ten // n_lo
-    rows_g, w_own, rows_other, w_other, hidden_other = pl.pallas_call(
+    vmem = pl.BlockSpec(memory_space=pltpu.VMEM)
+    rows_g, w_own, w_other, partial = pl.pallas_call(
         lambda *refs: _gather_kernel(n_chip, n_lo, *refs),
         out_shape=(
             jax.ShapeDtypeStruct((n_plane, n_lo, seq_rows, out_grad.shape[1]), out_grad.dtype),
             jax.ShapeDtypeStruct((n_chip, width, ff), w_down.dtype),
-            jax.ShapeDtypeStruct((n_plane, seq_rows, out_grad.shape[1]), out_grad.dtype),
             jax.ShapeDtypeStruct((n_chip, width, ff), w_down.dtype),
-            jax.ShapeDtypeStruct(hidden.shape, hidden.dtype),
+            jax.ShapeDtypeStruct((n_chip, width, ff), jnp.bfloat16),
         ),
         in_specs=[ANY, ANY, ANY],
-        out_specs=(ANY, ANY, ANY, ANY, ANY),
+        out_specs=(ANY, ANY, ANY, vmem),
         scratch_shapes=[pltpu.SemaphoreType.DMA((1,)), pltpu.SemaphoreType.DMA((1,)),
                         pltpu.SemaphoreType.DMA((n_plane // 2,)),
                         pltpu.SemaphoreType.DMA((n_plane // 2,)),
@@ -208,16 +239,15 @@
                         pltpu.SemaphoreType.DMA((1,)), pltpu.SemaphoreType.DMA((1,)),
                         pltpu.SemaphoreType.DMA((n_chip,)), pltpu.SemaphoreType.DMA((n_chip,)),
                         pltpu.SemaphoreType.DMA((n_plane,)), pltpu.SemaphoreType.DMA((n_plane,)),
-                        pltpu.SemaphoreType.DMA((2,))],
+                        pltpu.SemaphoreType.DMA((2,)),
+                        pltpu.VMEM((n_plane, seq_rows, out_grad.shape[1]), out_grad.dtype),
+                        pltpu.VMEM((n_plane, seq_rows, out_grad.shape[1]), out_grad.dtype),
+                        pltpu.VMEM(hidden.shape, hidden.dtype),
+                        pltpu.VMEM(hidden.shape, hidden.dtype),
+                        pltpu.SemaphoreType.DMA((n_plane + 1,))],
         compiler_params=_params(0),
     )(out_grad, w_down, hidden)
 
-    rows_mine = lax.dynamic_index_in_dim(rows_g, core, 1, keepdims=False)
-    partial = jnp.einsum(
-        "rtk,tf->rkf", rows_mine, hidden, preferred_element_type=jnp.float32
-    ) + jnp.einsum("rtk,tf->rkf", rows_other, hidden_other, preferred_element_type=jnp.float32)
-
-    vmem = pl.BlockSpec(memory_space=pltpu.VMEM)
     received, gate_grad, up_grad = pl.pallas_call(
         lambda *refs: _scatter_kernel(n_chip, min(128, seq_rows), *refs),
         out_shape=(
@@ -225,7 +255,7 @@
             jax.ShapeDtypeStruct(gate_act.shape, jnp.bfloat16),
             jax.ShapeDtypeStruct(up_act.shape, jnp.bfloat16),
         ),
-        in_specs=[ANY, ANY, ANY, ANY, ANY, ANY],
+        in_specs=[vmem, ANY, ANY, ANY, ANY, ANY],
         out_specs=(ANY, vmem, vmem),
         scratch_shapes=[pltpu.SemaphoreType.DMA((n_chip,)), pltpu.SemaphoreType.DMA((n_chip,)),
                         pltpu.SemaphoreType.DMA((1,)),
@@ -236,7 +266,7 @@
                         pltpu.VMEM(up_act.shape, up_act.dtype),
                         pltpu.SemaphoreType.DMA((5,))],
         compiler_params=_params(2),
-    )(partial.astype(jnp.bfloat16), rows_g, w_own, w_other, gate_act, up_act)
+    )(partial, rows_g, w_own, w_other, gate_act, up_act)
     summed = jnp.sum(received.astype(jnp.float32), axis=0)
     down_grad = (summed * grad_scale).astype(jnp.bfloat16)
     return (gate_grad, up_grad, down_grad)

time: 158 us -> 153 us (0.968)
  matrix products: 8.79 us -> 0 us
  Pallas kernels: 140 us -> 144 us
    dot_general x2 -> x0, matrix products: 8.79 us -> none  [the longest x1 4.44 us: body(): jnp.einsum('rtk,tf->rkf', rows_other, hidden_other, preferred_element_typ...]
    pallas_call x1, Pallas kernels: 76.2 us -> 78.1 us  [body(): pl.pallas_call(lambda *refs: _gather_kernel(n_chip, n_lo, *refs), out_sha...]
    pallas_call x1, Pallas kernels: 63.7 us -> 65.7 us  [body(): pl.pallas_call(lambda *refs: _scatter_kernel(n_chip, min(128, seq_rows),...]
where the time goes in v10:
time: 153 us
  Pallas kernels  144 us (94%)
  other arithmetic  6.48 us (4%)
  local copies, waits for them, and re-layouts  1.85 us (1%)
    pallas_call x1, Pallas kernels, body(): pl.pallas_call(lambda *refs: _gather_kernel(n_chip, n_lo, *refs), out_sha...  78.1 us
    pallas_call x1, Pallas kernels, body(): pl.pallas_call(lambda *refs: _scatter_kernel(n_chip, min(128, seq_rows),...  65.7 us

profile of v10, /device:TPU:26, one launch (start us, length us, event | category | flops | bytes accessed | tf_op | source)
XLA Modules:
  0.0 152.8 jit_solution(9155483635477150295)
XLA Ops:
  0.6 2.9 %fusion.4.refs_2_ = bf16[512,896]{1,0:T(8,128)(2,1)} fusion(bf16[512,896]{1,0:T(8,128)(2,1)} %refs_5_.1, bf16[512,896]{1,0:T(8,128)(2,1)} %refs_4_.1), kind=kLoop, calls=%fused_computation.7 | loop fusion | flops 3670016 | bytes 2752512 | tf_op jit(solution)/shard_map/convert_element_type | solution.py:218
  3.6 78.1 %shard_map.67 = (bf16[8,2,512,256]{3,2,1,0:T(8,128)(2,1)}, bf16[8,256,896]{2,1,0:T(8,128)(2,1)}, bf16[8,256,896]{2,1,0:T(8,128)(2,1)}, bf16[8,256,896]{2,1,0:T(8,128)(2,1)}) custom-call(bf16[512,256]{1,0:T(8,128)(2,1)} %refs_0_.1, bf16[256,896]{1,0:T(8,128)(2,1)} %refs_1_.1, bf16[512,896]{1,0:T(8,128)(2,1)} %fusion.4.refs_2_), custom_call_target="tpu_custom_call" | custom-call | tf_op jit(solution)/shard_map/pallas_call | solution.py:223
  81.7 65.7 %shard_map.68 = (bf16[8,256,896]{2,1,0:T(8,128)(2,1)}, bf16[512,896]{1,0:T(8,128)(2,1)}, bf16[512,896]{1,0:T(8,128)(2,1)}) custom-call(bf16[8,256,896]{2,1,0:T(8,128)(2,1)} %get-tuple-element.10.refs_0_, bf16[8,2,512,256]{3,2,1,0:T(8,128)(2,1)} %get-tuple-element.11.refs_1_, bf16[8,256,896]{2,1,0:T(8,128)(2,1)} %get-tuple-element.12.refs_2_, ...), custom_call_target="tpu_custom_call" | custom-call | tf_op jit(solution)/shard_map/pallas_call | solution.py:251
  147.4 0.0 copy-start.1
  147.4 2.7 %convert_reduce_fusion = f32[256,896]{1,0:T(8,128)S(1)} fusion(bf16[8,256,896]{2,1,0:T(8,128)(2,1)} %get-tuple-element.16), kind=kLoop, calls=%fused_computation | loop fusion | flops 3440640 | bytes 4587520 | tf_op jit(solution)/shard_map/reduce_sum | solution.py:270
  150.1 0.0 copy-start
  150.1 0.8 multiply_convert_fusion
  150.9 0.0 copy-done.1
  151.0 0.9 copy.9
  151.9 0.0 copy-done
  151.9 0.9 copy.10
Async XLA Ops:
  147.4 3.6 %copy-start.1 = (bf16[512,896]{1,0:T(8,128)(2,1)S(1)}, bf16[512,896]{1,0:T(8,128)(2,1)}, u32[]{:S(2)}) copy-start(bf16[512,896]{1,0:T(8,128)(2,1)} %get-tuple-element.20) | copy-start | bytes 2752516
  150.1 1.8 %copy-start = (bf16[512,896]{1,0:T(8,128)(2,1)S(1)}, bf16[512,896]{1,0:T(8,128)(2,1)}, u32[]{:S(2)}) copy-start(bf16[512,896]{1,0:T(8,128)(2,1)} %get-tuple-element.21) | copy-start | bytes 2752516

commit v11 on v10

--- a/solution.py
+++ b/solution.py
@@ -17,10 +17,12 @@
     return lax.axis_index("chip"), lax.axis_index("core"), lax.axis_index("tensor")
 
 
-def _gather_kernel(n_chip, n_lo, og_ref, w_ref, hid_ref, rows_out, w_out, w_other, part_out,
-                   x_send, x_recv, r_send, r_recv, l_send, l_recv, w_send, w_recv,
-                   f_send, f_recv, fw_send, fw_recv, fr_send, fr_recv, own_sem,
-                   rows_v, ro_v, hid_v, ho_v, load_sem):
+def _fused_kernel(n_chip, n_lo, tile, grad_scale, og_ref, w_ref, hid_ref, gate_hbm, up_hbm,
+                  gate_out, up_out, down_out, rows_out, w_out, w_other,
+                  x_send, x_recv, r_send, r_recv, l_send, l_recv, w_send, w_recv,
+                  f_send, f_recv, fw_send, fw_recv, fr_send, fr_recv, own_sem,
+                  rows_v, ro_v, hid_v, ho_v, load_sem, part_v, recv_v, s_send, s_recv,
+                  wv, wov, rows2_v, gate_v, up_v, late_sem):
     chip, core, ten = _where()
     n_plane = rows_out.shape[0]
     plane, lo = ten // n_lo, ten % n_lo
@@ -51,6 +53,7 @@
     hid_ld = pltpu.make_async_copy(hid_ref, hid_v, load_sem.at[n_plane])
     hid_ld.start()
     forwards = [hid_cp]
+    outgoing = {}
     w_fwds = []
     rows_fwd = {}
     rows_ld = {}
@@ -84,7 +87,16 @@
                                preferred_element_type=jnp.float32)
         part += lax.dot_general(ro_v[p], ho_v[...], (((0,), (0,)), ((), ())),
                                 preferred_element_type=jnp.float32)
-        part_out[p] = part.astype(part_out.dtype)
+        part_v[p] = part.astype(part_v.dtype)
+        k = (p - chip + n_chip) % n_chip
+        send = pltpu.make_async_remote_copy(
+            part_v.at[p], recv_v.at[chip], s_send.at[d], s_recv.at[k],
+            device_id=(p, core, ten), device_id_type=MESH)
+        outgoing[d] = (p, send)
+
+        @pl.when(p != chip)
+        def _():
+            send.start()
 
     fwd_w(0)
     own_r.wait()
@@ -145,29 +157,10 @@
     for cp in w_fwds:
         cp.wait_recv()
 
-
-def _scatter_kernel(n_chip, tile, part_ref, rows_hbm, w_hbm, wo_hbm, gate_hbm, up_hbm,
-                    recv_out, gate_out, up_out, send, recv, own_sem,
-                    rows_ref, w_ref, wo_ref, gate_ref, up_ref, load_sem):
-    chip, core, ten = _where()
-    barrier = pltpu.get_barrier_semaphore()
-    for k in range(1, n_chip):
-        pl.semaphore_signal(barrier, inc=1, device_id=((chip + k) % n_chip, core, ten),
-                            device_id_type=MESH)
-    pl.semaphore_wait(barrier, n_chip - 1)
-    own = pltpu.make_async_copy(part_ref.at[chip], recv_out.at[chip], own_sem.at[0])
-    own.start()
-    copies = []
-    for k in range(1, n_chip):
-        dest = (chip + k) % n_chip
-        cp = pltpu.make_async_remote_copy(
-            part_ref.at[dest], recv_out.at[chip], send.at[k], recv.at[k],
-            device_id=(dest, core, ten), device_id_type=MESH)
-        cp.start()
-        copies.append(cp)
-    loads = [pltpu.make_async_copy(src, dst, load_sem.at[i]) for i, (src, dst) in enumerate(
-        ((rows_hbm, rows_ref), (w_hbm, w_ref), (wo_hbm, wo_ref), (gate_hbm, gate_ref),
-         (up_hbm, up_ref)))]
+    loads = [pltpu.make_async_copy(src, dst, late_sem.at[i]) for i, (src, dst) in enumerate(
+        ((w_out, wv), (w_other, wov), (gate_hbm, gate_v), (up_hbm, up_v)))]
+    loads += [pltpu.make_async_copy(rows_out.at[r, 1 - core], rows2_v.at[r],
+                                    late_sem.at[4 + r]) for r in range(n_plane)]
     for ld in loads:
         ld.start()
     for ld in loads:
@@ -175,14 +168,12 @@
 
     def one_tile(i, carry):
         rows = pl.ds(pl.multiple_of(i * tile, tile), tile)
-        acc = jnp.zeros((tile, gate_ref.shape[1]), jnp.float32)
-        for r in range(w_ref.shape[0]):
-            acc += jnp.dot(rows_ref[r, core, rows, :], w_ref[r],
-                           preferred_element_type=jnp.float32)
-            acc += jnp.dot(rows_ref[r, 1 - core, rows, :], wo_ref[r],
-                           preferred_element_type=jnp.float32)
-        gate_wide = gate_ref[rows, :].astype(jnp.float32)
-        up_wide = up_ref[rows, :].astype(jnp.float32)
+        acc = jnp.zeros((tile, gate_v.shape[1]), jnp.float32)
+        for r in range(n_plane):
+            acc += jnp.dot(rows_v[r, rows, :], wv[r], preferred_element_type=jnp.float32)
+            acc += jnp.dot(rows2_v[r, rows, :], wov[r], preferred_element_type=jnp.float32)
+        gate_wide = gate_v[rows, :].astype(jnp.float32)
+        up_wide = up_v[rows, :].astype(jnp.float32)
         sigmoid_gate = jax.nn.sigmoid(gate_wide)
         activated = gate_wide * sigmoid_gate
         gate_out[rows, :] = (
@@ -191,16 +182,20 @@
         up_out[rows, :] = (acc * activated).astype(up_out.dtype)
         return carry
 
-    lax.fori_loop(0, gate_ref.shape[0] // tile, one_tile, 0)
-
-    own.wait()
-    for cp in copies:
-        cp.wait_send()
-        cp.wait_recv()
-
-
-def _params(cid):
-    return pltpu.CompilerParams(collective_id=cid, has_side_effects=True)
+    lax.fori_loop(0, gate_v.shape[0] // tile, one_tile, 0)
+
+    for d in range(n_plane):
+        p, send = outgoing[d]
+
+        @pl.when(p != chip)
+        def _():
+            send.wait_send()
+            send.wait_recv()
+
+    total = part_v[chip].astype(jnp.float32)
+    for k in range(1, n_chip):
+        total += recv_v[(chip + k) % n_chip].astype(jnp.float32)
+    down_out[...] = (total * grad_scale).astype(down_out.dtype)
 
 
 def body(out_grad, gate_act, up_act, w_down):
@@ -220,16 +215,19 @@
     n_lo = n_core
     n_plane = n_ten // n_lo
     vmem = pl.BlockSpec(memory_space=pltpu.VMEM)
-    rows_g, w_own, w_other, partial = pl.pallas_call(
-        lambda *refs: _gather_kernel(n_chip, n_lo, *refs),
+    rows_shape = (n_plane, seq_rows, out_grad.shape[1])
+    gate_grad, up_grad, down_grad, _, _, _ = pl.pallas_call(
+        lambda *refs: _fused_kernel(n_chip, n_lo, min(128, seq_rows), grad_scale, *refs),
         out_shape=(
+            jax.ShapeDtypeStruct(gate_act.shape, jnp.bfloat16),
+            jax.ShapeDtypeStruct(up_act.shape, jnp.bfloat16),
+            jax.ShapeDtypeStruct(w_down.shape, jnp.bfloat16),
             jax.ShapeDtypeStruct((n_plane, n_lo, seq_rows, out_grad.shape[1]), out_grad.dtype),
             jax.ShapeDtypeStruct((n_chip, width, ff), w_down.dtype),
             jax.ShapeDtypeStruct((n_chip, width, ff), w_down.dtype),
-            jax.ShapeDtypeStruct((n_chip, width, ff), jnp.bfloat16),
         ),
-        in_specs=[ANY, ANY, ANY],
-        out_specs=(ANY, ANY, ANY, vmem),
+        in_specs=[ANY, ANY, ANY, ANY, ANY],
+        out_specs=(vmem, vmem, vmem, ANY, ANY, ANY),
         scratch_shapes=[pltpu.SemaphoreType.DMA((1,)), pltpu.SemaphoreType.DMA((1,)),
                         pltpu.SemaphoreType.DMA((n_plane // 2,)),
                         pltpu.SemaphoreType.DMA((n_plane // 2,)),
@@ -240,35 +238,23 @@
                         pltpu.SemaphoreType.DMA((n_chip,)), pltpu.SemaphoreType.DMA((n_chip,)),
                         pltpu.SemaphoreType.DMA((n_plane,)), pltpu.SemaphoreType.DMA((n_plane,)),
                         pltpu.SemaphoreType.DMA((2,)),
-                        pltpu.VMEM((n_plane, seq_rows, out_grad.shape[1]), out_grad.dtype),
-                        pltpu.VMEM((n_plane, seq_rows, out_grad.shape[1]), out_grad.dtype),
+                        pltpu.VMEM(rows_shape, out_grad.dtype),
+                        pltpu.VMEM(rows_shape, out_grad.dtype),
                         pltpu.VMEM(hidden.shape, hidden.dtype),
                         pltpu.VMEM(hidden.shape, hidden.dtype),
-                        pltpu.SemaphoreType.DMA((n_plane + 1,))],
-        compiler_params=_params(0),
-    )(out_grad, w_down, hidden)
-
-    received, gate_grad, up_grad = pl.pallas_call(
-        lambda *refs: _scatter_kernel(n_chip, min(128, seq_rows), *refs),
-        out_shape=(
-            jax.ShapeDtypeStruct(partial.shape, jnp.bfloat16),
-            jax.ShapeDtypeStruct(gate_act.shape, jnp.bfloat16),
-            jax.ShapeDtypeStruct(up_act.shape, jnp.bfloat16),
-        ),
-        in_specs=[vmem, ANY, ANY, ANY, ANY, ANY],
-        out_specs=(ANY, vmem, vmem),
-        scratch_shapes=[pltpu.SemaphoreType.DMA((n_chip,)), pltpu.SemaphoreType.DMA((n_chip,)),
-                        pltpu.SemaphoreType.DMA((1,)),
-                        pltpu.VMEM(rows_g.shape, rows_g.dtype),
-                        pltpu.VMEM(w_own.shape, w_own.dtype),
-                        pltpu.VMEM(w_other.shape, w_other.dtype),
+                        pltpu.SemaphoreType.DMA((n_plane + 1,)),
+                        pltpu.VMEM((n_chip, width, ff), jnp.bfloat16),
+                        pltpu.VMEM((n_chip, width, ff), jnp.bfloat16),
+                        pltpu.SemaphoreType.DMA((n_plane,)), pltpu.SemaphoreType.DMA((n_chip,)),
+                        pltpu.VMEM((n_chip, width, ff), w_down.dtype),
+                        pltpu.VMEM((n_chip, width, ff), w_down.dtype),
+                        pltpu.VMEM(rows_shape, out_grad.dtype),
                         pltpu.VMEM(gate_act.shape, gate_act.dtype),
                         pltpu.VMEM(up_act.shape, up_act.dtype),
-                        pltpu.SemaphoreType.DMA((5,))],
-        compiler_params=_params(2),
-    )(partial, rows_g, w_own, w_other, gate_act, up_act)
-    summed = jnp.sum(received.astype(jnp.float32), axis=0)
-    down_grad = (summed * grad_scale).astype(jnp.bfloat16)
+                        pltpu.SemaphoreType.DMA((4 + n_plane,))],
+        compiler_params=pltpu.CompilerParams(collective_id=0, has_side_effects=True,
+                                             vmem_limit_bytes=56 * 1024 * 1024),
+    )(out_grad, w_down, hidden, gate_act, up_act)
     return (gate_grad, up_grad, down_grad)
 
 

time: 153 us -> 136 us (0.89)
  the two profiles are of different devices: /device:TPU:26 before, /device:TPU:4 now
where the time goes in v11:
time: 136 us; the launch traced here: 135 us
  Pallas kernels  128 us (94%)
  local copies, waits for them, and re-layouts  3.98 us (3%)
  other arithmetic  2.95 us (2%)
    pallas_call x1, Pallas kernels, body(): pl.pallas_call(lambda *refs: _fused_kernel(n_chip, n_lo, min(128, seq_row...  128 us
    unnamed x7, local copies, waits for them, and re-layouts  3.98 us
    convert_element_type x1, other arithmetic, body(): hidden = (activated * up_wide).astype(jnp.bfloat16)  2.95 us

profile of v11, /device:TPU:4, one launch (start us, length us, event | category | flops | bytes accessed | tf_op | source)
XLA Modules:
  0.0 135.4 jit_solution(17399839415493395747)
XLA Ops:
  0.6 2.9 %fusion.4.refs_2_ = bf16[512,896]{1,0:T(8,128)(2,1)} fusion(bf16[512,896]{1,0:T(8,128)(2,1)} %refs_4_.1, bf16[512,896]{1,0:T(8,128)(2,1)} %refs_3_.1), kind=kLoop, calls=%fused_computation.6 | loop fusion | flops 3670016 | bytes 2752512 | tf_op jit(solution)/shard_map/convert_element_type | solution.py:213
  3.6 127.8 %shard_map.67 = (bf16[512,896]{1,0:T(8,128)(2,1)}, bf16[512,896]{1,0:T(8,128)(2,1)}, bf16[256,896]{1,0:T(8,128)(2,1)}, bf16[8,2,512,256]{3,2,1,0:T(8,128)(2,1)},...) custom-call(bf16[512,256]{1,0:T(8,128)(2,1)} %refs_0_.1, bf16[256,896]{1,0:T(8,128)(2,1)} %refs_1_.1, ...), custom_call_target="tpu_custom_call" | custom-call | tf_op jit(solution)/shard_map/pallas_call | solution.py:219
  131.4 0.0 copy-start
  131.4 0.0 copy-start.1
  131.4 2.3 %copy.10 = bf16[512,896]{1,0:T(8,128)(2,1)} copy(bf16[512,896]{1,0:T(8,128)(2,1)} %get-tuple-element.12) | data formatting | bytes 1835008
  133.7 0.0 copy-done
  133.7 0.9 copy.11
  134.6 0.0 copy-done.1
  134.6 0.8 copy.12
Async XLA Ops:
  131.4 2.3 %copy-start = (bf16[512,896]{1,0:T(8,128)(2,1)S(1)}, bf16[512,896]{1,0:T(8,128)(2,1)}, u32[]{:S(2)}) copy-start(bf16[512,896]{1,0:T(8,128)(2,1)} %get-tuple-element.13) | copy-start | bytes 2752516
  131.4 3.2 %copy-start.1 = (bf16[256,896]{1,0:T(8,128)(2,1)S(1)}, bf16[256,896]{1,0:T(8,128)(2,1)}, u32[]{:S(2)}) copy-start(bf16[256,896]{1,0:T(8,128)(2,1)} %get-tuple-element.14) | copy-start | bytes 1376260

commit v12 on v11

--- a/solution.py
+++ b/solution.py
@@ -93,10 +93,6 @@
             part_v.at[p], recv_v.at[chip], s_send.at[d], s_recv.at[k],
             device_id=(p, core, ten), device_id_type=MESH)
         outgoing[d] = (p, send)
-
-        @pl.when(p != chip)
-        def _():
-            send.start()
 
     fwd_w(0)
     own_r.wait()
@@ -149,6 +145,13 @@
     for k in range(1, n_chip):
         w_copies[k - 1].wait_recv()
         fwd_w(k)
+    for d in range(n_plane):
+        p, send = outgoing[d]
+
+        @pl.when(p != chip)
+        def _():
+            send.start()
+
     own_w.wait()
     for cp in w_copies:
         cp.wait_send()

time: 136 us -> 136 us (level)
  the two profiles are of different devices: /device:TPU:4 before, /device:TPU:244 now
where the time goes in v12:
time: 136 us; the launch traced here: 135 us
  Pallas kernels  128 us (94%)
  local copies, waits for them, and re-layouts  3.98 us (3%)
  other arithmetic  2.95 us (2%)
    pallas_call x1, Pallas kernels, body(): pl.pallas_call(lambda *refs: _fused_kernel(n_chip, n_lo, min(128, seq_row...  128 us
    unnamed x7, local copies, waits for them, and re-layouts  3.98 us
    convert_element_type x1, other arithmetic, body(): hidden = (activated * up_wide).astype(jnp.bfloat16)  2.95 us

profile of v12, /device:TPU:244, one launch (start us, length us, event | category | flops | bytes accessed | tf_op | source)
XLA Modules:
  0.0 135.5 jit_solution(4873244973861155835)
XLA Ops:
  0.6 2.9 %fusion.4.refs_2_ = bf16[512,896]{1,0:T(8,128)(2,1)} fusion(bf16[512,896]{1,0:T(8,128)(2,1)} %refs_4_.1, bf16[512,896]{1,0:T(8,128)(2,1)} %refs_3_.1), kind=kLoop, calls=%fused_computation.6 | loop fusion | flops 3670016 | bytes 2752512 | tf_op jit(solution)/shard_map/convert_element_type | solution.py:216
  3.6 127.9 %shard_map.67 = (bf16[512,896]{1,0:T(8,128)(2,1)}, bf16[512,896]{1,0:T(8,128)(2,1)}, bf16[256,896]{1,0:T(8,128)(2,1)}, bf16[8,2,512,256]{3,2,1,0:T(8,128)(2,1)},...) custom-call(bf16[512,256]{1,0:T(8,128)(2,1)} %refs_0_.1, bf16[256,896]{1,0:T(8,128)(2,1)} %refs_1_.1, ...), custom_call_target="tpu_custom_call" | custom-call | tf_op jit(solution)/shard_map/pallas_call | solution.py:222
  131.5 0.0 copy-start
  131.5 0.0 copy-start.1
  131.5 2.3 %copy.10 = bf16[512,896]{1,0:T(8,128)(2,1)} copy(bf16[512,896]{1,0:T(8,128)(2,1)} %get-tuple-element.12) | data formatting | bytes 1835008
  133.8 0.0 copy-done
  133.8 0.9 copy.11
  134.7 0.0 copy-done.1
  134.7 0.8 copy.12
Async XLA Ops:
  131.5 2.3 %copy-start = (bf16[512,896]{1,0:T(8,128)(2,1)S(1)}, bf16[512,896]{1,0:T(8,128)(2,1)}, u32[]{:S(2)}) copy-start(bf16[512,896]{1,0:T(8,128)(2,1)} %get-tuple-element.13) | copy-start | bytes 2752516
  131.5 3.2 %copy-start.1 = (bf16[256,896]{1,0:T(8,128)(2,1)S(1)}, bf16[256,896]{1,0:T(8,128)(2,1)}, u32[]{:S(2)}) copy-start(bf16[256,896]{1,0:T(8,128)(2,1)} %get-tuple-element.14) | copy-start | bytes 1376260

commit v13 on v11

--- a/solution.py
+++ b/solution.py
@@ -21,7 +21,8 @@
                   gate_out, up_out, down_out, rows_out, w_out, w_other,
                   x_send, x_recv, r_send, r_recv, l_send, l_recv, w_send, w_recv,
                   f_send, f_recv, fw_send, fw_recv, fr_send, fr_recv, own_sem,
-                  rows_v, ro_v, hid_v, ho_v, load_sem, part_v, recv_v, s_send, s_recv,
+                  rows_v, ro_v, hid_v, ho_v, load_sem, part_v, recv_own, recv_agg, recv_x,
+                  agg_v, s_send, s_recv, x2_send, x2_recv,
                   wv, wov, rows2_v, gate_v, up_v, late_sem):
     chip, core, ten = _where()
     n_plane = rows_out.shape[0]
@@ -53,7 +54,6 @@
     hid_ld = pltpu.make_async_copy(hid_ref, hid_v, load_sem.at[n_plane])
     hid_ld.start()
     forwards = [hid_cp]
-    outgoing = {}
     w_fwds = []
     rows_fwd = {}
     rows_ld = {}
@@ -88,15 +88,6 @@
         part += lax.dot_general(ro_v[p], ho_v[...], (((0,), (0,)), ((), ())),
                                 preferred_element_type=jnp.float32)
         part_v[p] = part.astype(part_v.dtype)
-        k = (p - chip + n_chip) % n_chip
-        send = pltpu.make_async_remote_copy(
-            part_v.at[p], recv_v.at[chip], s_send.at[d], s_recv.at[k],
-            device_id=(p, core, ten), device_id_type=MESH)
-        outgoing[d] = (p, send)
-
-        @pl.when(p != chip)
-        def _():
-            send.start()
 
     fwd_w(0)
     own_r.wait()
@@ -149,6 +140,31 @@
     for k in range(1, n_chip):
         w_copies[k - 1].wait_recv()
         fwd_w(k)
+    n_y = n_chip // 2
+    half, y = chip // n_y, chip % n_y
+    across = (1 - half) * n_y + y
+    stage = []
+    for ky in range(1, n_y):
+        to_y = (y + ky) % n_y
+        for kind, (block, slot) in enumerate(((half * n_y + to_y, recv_own),
+                                              ((1 - half) * n_y + to_y, recv_agg))):
+            cp = pltpu.make_async_remote_copy(
+                part_v.at[block], slot.at[y], s_send.at[2 * ky + kind],
+                s_recv.at[2 * ky + kind],
+                device_id=(half * n_y + to_y, core, ten), device_id_type=MESH)
+            cp.start()
+            stage.append((kind, cp))
+    agg = part_v[across].astype(jnp.float32)
+    for kind, cp in stage:
+        if kind == 1:
+            cp.wait_recv()
+    for ky in range(1, n_y):
+        agg += recv_agg[(y + n_y - ky) % n_y].astype(jnp.float32)
+    agg_v[...] = agg
+    cross = pltpu.make_async_remote_copy(agg_v, recv_x, x2_send.at[0], x2_recv.at[0],
+                                         device_id=(across, core, ten), device_id_type=MESH)
+    cross.start()
+
     own_w.wait()
     for cp in w_copies:
         cp.wait_send()
@@ -184,17 +200,15 @@
 
     lax.fori_loop(0, gate_v.shape[0] // tile, one_tile, 0)
 
-    for d in range(n_plane):
-        p, send = outgoing[d]
-
-        @pl.when(p != chip)
-        def _():
-            send.wait_send()
-            send.wait_recv()
-
-    total = part_v[chip].astype(jnp.float32)
-    for k in range(1, n_chip):
-        total += recv_v[(chip + k) % n_chip].astype(jnp.float32)
+    for kind, cp in stage:
+        cp.wait_send()
+        if kind == 0:
+            cp.wait_recv()
+    cross.wait_send()
+    cross.wait_recv()
+    total = part_v[chip].astype(jnp.float32) + recv_x[...]
+    for ky in range(1, n_y):
+        total += recv_own[(y + n_y - ky) % n_y].astype(jnp.float32)
     down_out[...] = (total * grad_scale).astype(down_out.dtype)
 
 
@@ -244,8 +258,12 @@
                         pltpu.VMEM(hidden.shape, hidden.dtype),
                         pltpu.SemaphoreType.DMA((n_plane + 1,)),
                         pltpu.VMEM((n_chip, width, ff), jnp.bfloat16),
-                        pltpu.VMEM((n_chip, width, ff), jnp.bfloat16),
-                        pltpu.SemaphoreType.DMA((n_plane,)), pltpu.SemaphoreType.DMA((n_chip,)),
+                        pltpu.VMEM((n_chip // 2, width, ff), jnp.bfloat16),
+                        pltpu.VMEM((n_chip // 2, width, ff), jnp.bfloat16),
+                        pltpu.VMEM((width, ff), jnp.float32),
+                        pltpu.VMEM((width, ff), jnp.float32),
+                        pltpu.SemaphoreType.DMA((n_chip,)), pltpu.SemaphoreType.DMA((n_chip,)),
+                        pltpu.SemaphoreType.DMA((1,)), pltpu.SemaphoreType.DMA((1,)),
                         pltpu.VMEM((n_chip, width, ff), w_down.dtype),
                         pltpu.VMEM((n_chip, width, ff), w_down.dtype),
                         pltpu.VMEM(rows_shape, out_grad.dtype),

time: 136 us -> 144 us (1.059)
  the two profiles are of different devices: /device:TPU:4 before, /device:TPU:26 now
where the time goes in v13:
time: 144 us; the launch traced here: 142 us
  Pallas kernels  135 us (94%)
  local copies, waits for them, and re-layouts  3.98 us (3%)
  other arithmetic  2.95 us (2%)
    pallas_call x1, Pallas kernels, body(): pl.pallas_call(lambda *refs: _fused_kernel(n_chip, n_lo, min(128, seq_row...  135 us
    unnamed x7, local copies, waits for them, and re-layouts  3.98 us
    convert_element_type x1, other arithmetic, body(): hidden = (activated * up_wide).astype(jnp.bfloat16)  2.95 us

profile of v13, /device:TPU:26, one launch (start us, length us, event | category | flops | bytes accessed | tf_op | source)
XLA Modules:
  0.0 142.4 jit_solution(9053435069616423434)
XLA Ops:
  0.6 2.9 %fusion.4.refs_2_ = bf16[512,896]{1,0:T(8,128)(2,1)} fusion(bf16[512,896]{1,0:T(8,128)(2,1)} %refs_4_.1, bf16[512,896]{1,0:T(8,128)(2,1)} %refs_3_.1), kind=kLoop, calls=%fused_computation.6 | loop fusion | flops 3670016 | bytes 2752512 | tf_op jit(solution)/shard_map/convert_element_type | solution.py:227
  3.6 134.8 %shard_map.67 = (bf16[512,896]{1,0:T(8,128)(2,1)}, bf16[512,896]{1,0:T(8,128)(2,1)}, bf16[256,896]{1,0:T(8,128)(2,1)}, bf16[8,2,512,256]{3,2,1,0:T(8,128)(2,1)},...) custom-call(bf16[512,256]{1,0:T(8,128)(2,1)} %refs_0_.1, bf16[256,896]{1,0:T(8,128)(2,1)} %refs_1_.1, ...), custom_call_target="tpu_custom_call" | custom-call | tf_op jit(solution)/shard_map/pallas_call | solution.py:233
  138.4 0.0 copy-start
  138.4 0.0 copy-start.1
  138.4 2.3 %copy.10 = bf16[512,896]{1,0:T(8,128)(2,1)} copy(bf16[512,896]{1,0:T(8,128)(2,1)} %get-tuple-element.12) | data formatting | bytes 1835008
  140.7 0.0 copy-done
  140.7 0.9 copy.11
  141.6 0.0 copy-done.1
  141.6 0.8 copy.12
Async XLA Ops:
  138.4 2.3 %copy-start = (bf16[512,896]{1,0:T(8,128)(2,1)S(1)}, bf16[512,896]{1,0:T(8,128)(2,1)}, u32[]{:S(2)}) copy-start(bf16[512,896]{1,0:T(8,128)(2,1)} %get-tuple-element.13) | copy-start | bytes 2752516
  138.4 3.2 %copy-start.1 = (bf16[256,896]{1,0:T(8,128)(2,1)S(1)}, bf16[256,896]{1,0:T(8,128)(2,1)}, u32[]{:S(2)}) copy-start(bf16[256,896]{1,0:T(8,128)(2,1)} %get-tuple-element.14) | copy-start | bytes 1376260

commit v14 on v12

--- a/solution.py
+++ b/solution.py
@@ -17,7 +17,7 @@
     return lax.axis_index("chip"), lax.axis_index("core"), lax.axis_index("tensor")
 
 
-def _fused_kernel(n_chip, n_lo, tile, grad_scale, og_ref, w_ref, hid_ref, gate_hbm, up_hbm,
+def _fused_kernel(n_chip, n_lo, tile, grad_scale, og_ref, w_ref, gate_hbm, up_hbm,
                   gate_out, up_out, down_out, rows_out, w_out, w_other,
                   x_send, x_recv, r_send, r_recv, l_send, l_recv, w_send, w_recv,
                   f_send, f_recv, fw_send, fw_recv, fr_send, fr_recv, own_sem,
@@ -47,11 +47,12 @@
     own_w = pltpu.make_async_copy(w_ref, w_out.at[chip], own_sem.at[1])
     own_r.start()
     own_w.start()
-    hid_cp = pltpu.make_async_remote_copy(hid_ref, ho_v, f_send.at[0], f_recv.at[0],
+    act_ld = [pltpu.make_async_copy(gate_hbm, gate_v, late_sem.at[2]),
+              pltpu.make_async_copy(up_hbm, up_v, late_sem.at[3])]
+    for ld in act_ld:
+        ld.start()
+    hid_cp = pltpu.make_async_remote_copy(hid_v, ho_v, f_send.at[0], f_recv.at[0],
                                           device_id=other, device_id_type=MESH)
-    hid_cp.start()
-    hid_ld = pltpu.make_async_copy(hid_ref, hid_v, load_sem.at[n_plane])
-    hid_ld.start()
     forwards = [hid_cp]
     outgoing = {}
     w_fwds = []
@@ -122,7 +123,12 @@
             device_id=((chip + k) % n_chip, core, ten), device_id_type=MESH)
         cp.start()
         w_copies.append(cp)
-    hid_ld.wait()
+    for ld in act_ld:
+        ld.wait()
+    gate_wide = gate_v[...].astype(jnp.float32)
+    sigmoid_gate = jax.nn.sigmoid(gate_wide)
+    hid_v[...] = (gate_wide * sigmoid_gate * up_v[...].astype(jnp.float32)).astype(hid_v.dtype)
+    hid_cp.start()
     hid_cp.wait_recv()
     pending = [0]
     for s in range(1, n_steps):
@@ -161,7 +167,7 @@
         cp.wait_recv()
 
     loads = [pltpu.make_async_copy(src, dst, late_sem.at[i]) for i, (src, dst) in enumerate(
-        ((w_out, wv), (w_other, wov), (gate_hbm, gate_v), (up_hbm, up_v)))]
+        ((w_out, wv), (w_other, wov)))]
     loads += [pltpu.make_async_copy(rows_out.at[r, 1 - core], rows2_v.at[r],
                                     late_sem.at[4 + r]) for r in range(n_plane)]
     for ld in loads:
@@ -209,11 +215,7 @@
     n_ten = lax.axis_size("tensor")
     core = lax.axis_index("core")
     grad_scale = 1.0 / math.sqrt(seq_rows * n_chip * n_core)
-    gate_wide = gate_act.astype(jnp.float32)
-    up_wide = up_act.astype(jnp.float32)
-    sigmoid_gate = jax.nn.sigmoid(gate_wide)
-    activated = gate_wide * sigmoid_gate
-    hidden = (activated * up_wide).astype(jnp.bfloat16)
+    hidden = jax.ShapeDtypeStruct(gate_act.shape, jnp.bfloat16)
 
     n_lo = n_core
     n_plane = n_ten // n_lo
@@ -229,7 +231,7 @@
             jax.ShapeDtypeStruct((n_chip, width, ff), w_down.dtype),
             jax.ShapeDtypeStruct((n_chip, width, ff), w_down.dtype),
         ),
-        in_specs=[ANY, ANY, ANY, ANY, ANY],
+        in_specs=[ANY, ANY, ANY, ANY],
         out_specs=(vmem, vmem, vmem, ANY, ANY, ANY),
         scratch_shapes=[pltpu.SemaphoreType.DMA((1,)), pltpu.SemaphoreType.DMA((1,)),
                         pltpu.SemaphoreType.DMA((n_plane // 2,)),
@@ -257,7 +259,7 @@
                         pltpu.SemaphoreType.DMA((4 + n_plane,))],
         compiler_params=pltpu.CompilerParams(collective_id=0, has_side_effects=True,
                                              vmem_limit_bytes=56 * 1024 * 1024),
-    )(out_grad, w_down, hidden, gate_act, up_act)
+    )(out_grad, w_down, gate_act, up_act)
     return (gate_grad, up_grad, down_grad)
 
 

time: 136 us -> 134 us (0.985)
  other arithmetic: 2.95 us -> 0 us
    convert_element_type x1 -> x0, other arithmetic: 2.95 us -> none  [body(): hidden = (activated * up_wide).astype(jnp.bfloat16)]
    unnamed x7 -> x5, local copies, waits for them, and re-layouts: 3.98 us -> 5.17 us
where the time goes in v14:
time: 134 us
  Pallas kernels  128 us (96%)
  local copies, waits for them, and re-layouts  5.17 us (4%)
    pallas_call x1, Pallas kernels, body(): pl.pallas_call(lambda *refs: _fused_kernel(n_chip, n_lo, min(128, seq_row...  128 us
    unnamed x5, local copies, waits for them, and re-layouts  5.17 us

profile of v14, /device:TPU:244, one launch (start us, length us, event | category | flops | bytes accessed | tf_op | source)
XLA Modules:
  0.0 133.9 jit_solution(7178093108620930185)
XLA Ops:
  0.6 128.1 %shard_map.67 = (bf16[512,896]{1,0:T(8,128)(2,1)}, bf16[512,896]{1,0:T(8,128)(2,1)}, bf16[256,896]{1,0:T(8,128)(2,1)}, bf16[8,2,512,256]{3,2,1,0:T(8,128)(2,1)},...) custom-call(bf16[512,256]{1,0:T(8,128)(2,1)} %refs_0_.1, bf16[256,896]{1,0:T(8,128)(2,1)} %refs_1_.1, ...), custom_call_target="tpu_custom_call" | custom-call | tf_op jit(solution)/shard_map/pallas_call | solution.py:224
  128.7 0.0 copy-start
  128.7 2.2 %copy.10 = bf16[512,896]{1,0:T(8,128)(2,1)} copy(bf16[512,896]{1,0:T(8,128)(2,1)} %get-tuple-element.12) | data formatting | bytes 1835008
  131.0 2.2 %copy.11 = bf16[512,896]{1,0:T(8,128)(2,1)} copy(bf16[512,896]{1,0:T(8,128)(2,1)} %get-tuple-element.13) | data formatting | bytes 1835008
  133.1 0.0 copy-done
  133.1 0.8 copy.12
Async XLA Ops:
  128.7 4.4 %copy-start = (bf16[256,896]{1,0:T(8,128)(2,1)S(1)}, bf16[256,896]{1,0:T(8,128)(2,1)}, u32[]{:S(2)}) copy-start(bf16[256,896]{1,0:T(8,128)(2,1)} %get-tuple-element.14) | copy-start | bytes 1376260

commit v15 on v14

--- a/solution.py
+++ b/solution.py
@@ -54,7 +54,6 @@
     hid_cp = pltpu.make_async_remote_copy(hid_v, ho_v, f_send.at[0], f_recv.at[0],
                                           device_id=other, device_id_type=MESH)
     forwards = [hid_cp]
-    outgoing = {}
     w_fwds = []
     rows_fwd = {}
     rows_ld = {}
@@ -89,11 +88,6 @@
         part += lax.dot_general(ro_v[p], ho_v[...], (((0,), (0,)), ((), ())),
                                 preferred_element_type=jnp.float32)
         part_v[p] = part.astype(part_v.dtype)
-        k = (p - chip + n_chip) % n_chip
-        send = pltpu.make_async_remote_copy(
-            part_v.at[p], recv_v.at[chip], s_send.at[d], s_recv.at[k],
-            device_id=(p, core, ten), device_id_type=MESH)
-        outgoing[d] = (p, send)
 
     fwd_w(0)
     own_r.wait()
@@ -151,12 +145,15 @@
     for k in range(1, n_chip):
         w_copies[k - 1].wait_recv()
         fwd_w(k)
-    for d in range(n_plane):
-        p, send = outgoing[d]
-
-        @pl.when(p != chip)
-        def _():
-            send.start()
+    order = sorted(range(1, n_chip), key=lambda k: abs(k - n_chip // 2))
+    outgoing = []
+    for k in order:
+        p = (chip + k) % n_chip
+        send = pltpu.make_async_remote_copy(
+            part_v.at[p], recv_v.at[chip], s_send.at[k], s_recv.at[k],
+            device_id=(p, core, ten), device_id_type=MESH)
+        send.start()
+        outgoing.append(send)
 
     own_w.wait()
     for cp in w_copies:
@@ -193,13 +190,9 @@
 
     lax.fori_loop(0, gate_v.shape[0] // tile, one_tile, 0)
 
-    for d in range(n_plane):
-        p, send = outgoing[d]
-
-        @pl.when(p != chip)
-        def _():
-            send.wait_send()
-            send.wait_recv()
+    for send in outgoing:
+        send.wait_send()
+        send.wait_recv()
 
     total = part_v[chip].astype(jnp.float32)
     for k in range(1, n_chip):

time: 134 us -> 132 us (0.985)
  the two profiles are of different devices: /device:TPU:244 before, /device:TPU:26 now
where the time goes in v15:
time: 132 us; the launch traced here: 130 us
  Pallas kernels  125 us (95%)
  local copies, waits for them, and re-layouts  5.17 us (4%)
    pallas_call x1, Pallas kernels, body(): pl.pallas_call(lambda *refs: _fused_kernel(n_chip, n_lo, min(128, seq_row...  125 us
    unnamed x5, local copies, waits for them, and re-layouts  5.17 us

profile of v15, /device:TPU:26, one launch (start us, length us, event | category | flops | bytes accessed | tf_op | source)
XLA Modules:
  0.0 130.4 jit_solution(14454669468222604382)
XLA Ops:
  0.6 124.6 %shard_map.67 = (bf16[512,896]{1,0:T(8,128)(2,1)}, bf16[512,896]{1,0:T(8,128)(2,1)}, bf16[256,896]{1,0:T(8,128)(2,1)}, bf16[8,2,512,256]{3,2,1,0:T(8,128)(2,1)},...) custom-call(bf16[512,256]{1,0:T(8,128)(2,1)} %refs_0_.1, bf16[256,896]{1,0:T(8,128)(2,1)} %refs_1_.1, ...), custom_call_target="tpu_custom_call" | custom-call | tf_op jit(solution)/shard_map/pallas_call | solution.py:217
  125.3 0.0 copy-start
  125.3 2.2 %copy.10 = bf16[512,896]{1,0:T(8,128)(2,1)} copy(bf16[512,896]{1,0:T(8,128)(2,1)} %get-tuple-element.12) | data formatting | bytes 1835008
  127.5 2.2 %copy.11 = bf16[512,896]{1,0:T(8,128)(2,1)} copy(bf16[512,896]{1,0:T(8,128)(2,1)} %get-tuple-element.13) | data formatting | bytes 1835008
  129.7 0.0 copy-done
  129.7 0.8 copy.12
Async XLA Ops:
  125.3 4.4 %copy-start = (bf16[256,896]{1,0:T(8,128)(2,1)S(1)}, bf16[256,896]{1,0:T(8,128)(2,1)}, u32[]{:S(2)}) copy-start(bf16[256,896]{1,0:T(8,128)(2,1)} %get-tuple-element.14) | copy-start | bytes 1376260

commit v16 on v15

--- a/solution.py
+++ b/solution.py
@@ -110,13 +110,14 @@
                 device_id=(chip, core, to), device_id_type=MESH)
     for d in ("r", "l"):
         ring[(d, 0)].start()
-    w_copies = []
-    for k in range(1, n_chip):
+    order = sorted(range(1, n_chip), key=lambda k: abs(k - n_chip // 2))
+    w_copies = {}
+    for k in order:
         cp = pltpu.make_async_remote_copy(
             w_ref, w_out.at[chip], w_send.at[k], w_recv.at[k],
             device_id=((chip + k) % n_chip, core, ten), device_id_type=MESH)
         cp.start()
-        w_copies.append(cp)
+        w_copies[k] = cp
     for ld in act_ld:
         ld.wait()
     gate_wide = gate_v[...].astype(jnp.float32)
@@ -142,10 +143,9 @@
     for d in pending + [n_steps]:
         partial(d)
 
-    for k in range(1, n_chip):
-        w_copies[k - 1].wait_recv()
+    for k in order:
+        w_copies[k].wait_recv()
         fwd_w(k)
-    order = sorted(range(1, n_chip), key=lambda k: abs(k - n_chip // 2))
     outgoing = []
     for k in order:
         p = (chip + k) % n_chip
@@ -156,8 +156,8 @@
         outgoing.append(send)
 
     own_w.wait()
-    for cp in w_copies:
-        cp.wait_send()
+    for k in order:
+        w_copies[k].wait_send()
     for cp in forwards:
         cp.wait_send()
     for cp in w_fwds:

time: 132 us -> 131 us (level)
  Pallas kernels: 125 us -> 123 us
    pallas_call x1, Pallas kernels: 125 us -> 123 us  [body(): pl.pallas_call(lambda *refs: _fused_kernel(n_chip, n_lo, min(128, seq_row...]
where the time goes in v16:
time: 131 us; the launch traced here: 129 us
  Pallas kernels  123 us (94%)
  local copies, waits for them, and re-layouts  5.17 us (4%)
    pallas_call x1, Pallas kernels, body(): pl.pallas_call(lambda *refs: _fused_kernel(n_chip, n_lo, min(128, seq_row...  123 us
    unnamed x5, local copies, waits for them, and re-layouts  5.17 us

profile of v16, /device:TPU:26, one launch (start us, length us, event | category | flops | bytes accessed | tf_op | source)
XLA Modules:
  0.0 128.7 jit_solution(4409969774822048178)
XLA Ops:
  0.6 122.9 %shard_map.67 = (bf16[512,896]{1,0:T(8,128)(2,1)}, bf16[512,896]{1,0:T(8,128)(2,1)}, bf16[256,896]{1,0:T(8,128)(2,1)}, bf16[8,2,512,256]{3,2,1,0:T(8,128)(2,1)},...) custom-call(bf16[512,256]{1,0:T(8,128)(2,1)} %refs_0_.1, bf16[256,896]{1,0:T(8,128)(2,1)} %refs_1_.1, ...), custom_call_target="tpu_custom_call" | custom-call | tf_op jit(solution)/shard_map/pallas_call | solution.py:217
  123.5 0.0 copy-start
  123.5 2.2 %copy.10 = bf16[512,896]{1,0:T(8,128)(2,1)} copy(bf16[512,896]{1,0:T(8,128)(2,1)} %get-tuple-element.12) | data formatting | bytes 1835008
  125.7 2.2 %copy.11 = bf16[512,896]{1,0:T(8,128)(2,1)} copy(bf16[512,896]{1,0:T(8,128)(2,1)} %get-tuple-element.13) | data formatting | bytes 1835008
  127.9 0.0 copy-done
  127.9 0.8 copy.12
Async XLA Ops:
  123.5 4.4 %copy-start = (bf16[256,896]{1,0:T(8,128)(2,1)S(1)}, bf16[256,896]{1,0:T(8,128)(2,1)}, u32[]{:S(2)}) copy-start(bf16[256,896]{1,0:T(8,128)(2,1)} %get-tuple-element.14) | copy-start | bytes 1376260

commit v17 on v16

--- a/solution.py
+++ b/solution.py
@@ -18,7 +18,7 @@
 
 
 def _fused_kernel(n_chip, n_lo, tile, grad_scale, og_ref, w_ref, gate_hbm, up_hbm,
-                  gate_out, up_out, down_out, rows_out, w_out, w_other,
+                  gate_out, up_out, down_out, rows_out,
                   x_send, x_recv, r_send, r_recv, l_send, l_recv, w_send, w_recv,
                   f_send, f_recv, fw_send, fw_recv, fr_send, fr_recv, own_sem,
                   rows_v, ro_v, hid_v, ho_v, load_sem, part_v, recv_v, s_send, s_recv,
@@ -44,7 +44,7 @@
         device_id=(chip, core, side), device_id_type=MESH)
     side_cp.start()
     own_r = pltpu.make_async_copy(og_ref, rows_out.at[plane, lo], own_sem.at[0])
-    own_w = pltpu.make_async_copy(w_ref, w_out.at[chip], own_sem.at[1])
+    own_w = pltpu.make_async_copy(w_ref, wv.at[chip], own_sem.at[1])
     own_r.start()
     own_w.start()
     act_ld = [pltpu.make_async_copy(gate_hbm, gate_v, late_sem.at[2]),
@@ -60,8 +60,8 @@
 
     def fwd_w(k):
         r = (chip + n_chip - k) % n_chip
-        src = w_ref if k == 0 else w_out.at[r]
-        cp = pltpu.make_async_remote_copy(src, w_other.at[r], fw_send.at[k], fw_recv.at[k],
+        src = w_ref if k == 0 else wv.at[r]
+        cp = pltpu.make_async_remote_copy(src, wov.at[r], fw_send.at[k], fw_recv.at[k],
                                           device_id=other, device_id_type=MESH)
         cp.start()
         forwards.append(cp)
@@ -114,7 +114,7 @@
     w_copies = {}
     for k in order:
         cp = pltpu.make_async_remote_copy(
-            w_ref, w_out.at[chip], w_send.at[k], w_recv.at[k],
+            w_ref, wv.at[chip], w_send.at[k], w_recv.at[k],
             device_id=((chip + k) % n_chip, core, ten), device_id_type=MESH)
         cp.start()
         w_copies[k] = cp
@@ -140,6 +140,10 @@
         for s in range(n_steps):
             ring[(d, s)].wait_send()
     arrived(n_steps)
+    loads = [pltpu.make_async_copy(rows_out.at[r, 1 - core], rows2_v.at[r],
+                                   late_sem.at[4 + r]) for r in range(n_plane)]
+    for ld in loads:
+        ld.start()
     for d in pending + [n_steps]:
         partial(d)
 
@@ -163,12 +167,6 @@
     for cp in w_fwds:
         cp.wait_recv()
 
-    loads = [pltpu.make_async_copy(src, dst, late_sem.at[i]) for i, (src, dst) in enumerate(
-        ((w_out, wv), (w_other, wov)))]
-    loads += [pltpu.make_async_copy(rows_out.at[r, 1 - core], rows2_v.at[r],
-                                    late_sem.at[4 + r]) for r in range(n_plane)]
-    for ld in loads:
-        ld.start()
     for ld in loads:
         ld.wait()
 
@@ -214,18 +212,16 @@
     n_plane = n_ten // n_lo
     vmem = pl.BlockSpec(memory_space=pltpu.VMEM)
     rows_shape = (n_plane, seq_rows, out_grad.shape[1])
-    gate_grad, up_grad, down_grad, _, _, _ = pl.pallas_call(
+    gate_grad, up_grad, down_grad, _ = pl.pallas_call(
         lambda *refs: _fused_kernel(n_chip, n_lo, min(128, seq_rows), grad_scale, *refs),
         out_shape=(
             jax.ShapeDtypeStruct(gate_act.shape, jnp.bfloat16),
             jax.ShapeDtypeStruct(up_act.shape, jnp.bfloat16),
             jax.ShapeDtypeStruct(w_down.shape, jnp.bfloat16),
             jax.ShapeDtypeStruct((n_plane, n_lo, seq_rows, out_grad.shape[1]), out_grad.dtype),
-            jax.ShapeDtypeStruct((n_chip, width, ff), w_down.dtype),
-            jax.ShapeDtypeStruct((n_chip, width, ff), w_down.dtype),
         ),
         in_specs=[ANY, ANY, ANY, ANY],
-        out_specs=(vmem, vmem, vmem, ANY, ANY, ANY),
+        out_specs=(vmem, vmem, vmem, ANY),
         scratch_shapes=[pltpu.SemaphoreType.DMA((1,)), pltpu.SemaphoreType.DMA((1,)),
                         pltpu.SemaphoreType.DMA((n_plane // 2,)),
                         pltpu.SemaphoreType.DMA((n_plane // 2,)),

time: 131 us -> 132 us (level)
  the two profiles are of different devices: /device:TPU:26 before, /device:TPU:154 now
where the time goes in v17:
time: 132 us
  Pallas kernels  125 us (95%)
  local copies, waits for them, and re-layouts  6.17 us (5%)
    pallas_call x1, Pallas kernels, body(): pl.pallas_call(lambda *refs: _fused_kernel(n_chip, n_lo, min(128, seq_row...  125 us
    unnamed x3, local copies, waits for them, and re-layouts  6.17 us

profile of v17, /device:TPU:154, one launch (start us, length us, event | category | flops | bytes accessed | tf_op | source)
XLA Modules:
  0.0 131.9 jit_solution(8287177774010680170)
XLA Ops:
  0.6 125.1 %shard_map.67 = (bf16[512,896]{1,0:T(8,128)(2,1)}, bf16[512,896]{1,0:T(8,128)(2,1)}, bf16[256,896]{1,0:T(8,128)(2,1)}, bf16[8,2,512,256]{3,2,1,0:T(8,128)(2,1)}) custom-call(bf16[512,256]{1,0:T(8,128)(2,1)} %refs_0_.1, bf16[256,896]{1,0:T(8,128)(2,1)} %refs_1_.1, bf16[512,896]{1,0:T(8,128)(2,1)} %refs_2_.1, bf16[512,896]{1,0:T(8,128)(2,1)} %refs_3_.1), custom_call_target="tpu_custom_call" | custom-call | tf_op jit(solution)/shard_map/pallas_call | solution.py:215
  125.7 2.2 %copy.10 = bf16[512,896]{1,0:T(8,128)(2,1)} copy(bf16[512,896]{1,0:T(8,128)(2,1)} %get-tuple-element.12) | data formatting | bytes 1835008
  127.9 2.2 %copy.11 = bf16[512,896]{1,0:T(8,128)(2,1)} copy(bf16[512,896]{1,0:T(8,128)(2,1)} %get-tuple-element.13) | data formatting | bytes 1835008
  130.1 1.8 %copy.12 = bf16[256,896]{1,0:T(8,128)(2,1)} copy(bf16[256,896]{1,0:T(8,128)(2,1)} %get-tuple-element.14) | data formatting | bytes 917504

commit v18 on v17

--- a/solution.py
+++ b/solution.py
@@ -22,7 +22,8 @@
                   x_send, x_recv, r_send, r_recv, l_send, l_recv, w_send, w_recv,
                   f_send, f_recv, fw_send, fw_recv, fr_send, fr_recv, own_sem,
                   rows_v, ro_v, hid_v, ho_v, load_sem, part_v, recv_v, s_send, s_recv,
-                  wv, wov, rows2_v, gate_v, up_v, late_sem):
+                  wv, wov, rows2_v, gate_v, up_v, late_sem, gate_res, up_res, down_res,
+                  out_sem):
     chip, core, ten = _where()
     n_plane = rows_out.shape[0]
     plane, lo = ten // n_lo, ten % n_lo
@@ -180,13 +181,17 @@
         up_wide = up_v[rows, :].astype(jnp.float32)
         sigmoid_gate = jax.nn.sigmoid(gate_wide)
         activated = gate_wide * sigmoid_gate
-        gate_out[rows, :] = (
+        gate_res[rows, :] = (
             acc * up_wide * sigmoid_gate * (1.0 + gate_wide * (1.0 - sigmoid_gate))
-        ).astype(gate_out.dtype)
-        up_out[rows, :] = (acc * activated).astype(up_out.dtype)
+        ).astype(gate_res.dtype)
+        up_res[rows, :] = (acc * activated).astype(up_res.dtype)
         return carry
 
     lax.fori_loop(0, gate_v.shape[0] // tile, one_tile, 0)
+    results = [pltpu.make_async_copy(gate_res, gate_out, out_sem.at[0]),
+               pltpu.make_async_copy(up_res, up_out, out_sem.at[1])]
+    for cp in results:
+        cp.start()
 
     for send in outgoing:
         send.wait_send()
@@ -195,7 +200,11 @@
     total = part_v[chip].astype(jnp.float32)
     for k in range(1, n_chip):
         total += recv_v[(chip + k) % n_chip].astype(jnp.float32)
-    down_out[...] = (total * grad_scale).astype(down_out.dtype)
+    down_res[...] = (total * grad_scale).astype(down_res.dtype)
+    results.append(pltpu.make_async_copy(down_res, down_out, out_sem.at[2]))
+    results[-1].start()
+    for cp in results:
+        cp.wait()
 
 
 def body(out_grad, gate_act, up_act, w_down):
@@ -221,7 +230,7 @@
             jax.ShapeDtypeStruct((n_plane, n_lo, seq_rows, out_grad.shape[1]), out_grad.dtype),
         ),
         in_specs=[ANY, ANY, ANY, ANY],
-        out_specs=(vmem, vmem, vmem, ANY),
+        out_specs=(ANY, ANY, ANY, ANY),
         scratch_shapes=[pltpu.SemaphoreType.DMA((1,)), pltpu.SemaphoreType.DMA((1,)),
                         pltpu.SemaphoreType.DMA((n_plane // 2,)),
                         pltpu.SemaphoreType.DMA((n_plane // 2,)),
@@ -245,7 +254,11 @@
                         pltpu.VMEM(rows_shape, out_grad.dtype),
                         pltpu.VMEM(gate_act.shape, gate_act.dtype),
                         pltpu.VMEM(up_act.shape, up_act.dtype),
-                        pltpu.SemaphoreType.DMA((4 + n_plane,))],
+                        pltpu.SemaphoreType.DMA((4 + n_plane,)),
+                        pltpu.VMEM(gate_act.shape, jnp.bfloat16),
+                        pltpu.VMEM(up_act.shape, jnp.bfloat16),
+                        pltpu.VMEM(w_down.shape, jnp.bfloat16),
+                        pltpu.SemaphoreType.DMA((3,))],
         compiler_params=pltpu.CompilerParams(collective_id=0, has_side_effects=True,
                                              vmem_limit_bytes=56 * 1024 * 1024),
     )(out_grad, w_down, gate_act, up_act)

time: 132 us -> 132 us (level)
  no operation moved by 1% of the time
where the time goes in v18:
time: 132 us
  Pallas kernels  125 us (95%)
  local copies, waits for them, and re-layouts  6.17 us (5%)
    pallas_call x1, Pallas kernels, body(): pl.pallas_call(lambda *refs: _fused_kernel(n_chip, n_lo, min(128, seq_row...  125 us
    unnamed x3, local copies, waits for them, and re-layouts  6.17 us

profile of v18, /device:TPU:154, one launch (start us, length us, event | category | flops | bytes accessed | tf_op | source)
XLA Modules:
  0.0 131.8 jit_solution(4369628999137995147)
XLA Ops:
  0.6 125.0 %shard_map.67 = (bf16[512,896]{1,0:T(8,128)(2,1)}, bf16[512,896]{1,0:T(8,128)(2,1)}, bf16[256,896]{1,0:T(8,128)(2,1)}, bf16[8,2,512,256]{3,2,1,0:T(8,128)(2,1)}) custom-call(bf16[512,256]{1,0:T(8,128)(2,1)} %refs_0_.1, bf16[256,896]{1,0:T(8,128)(2,1)} %refs_1_.1, bf16[512,896]{1,0:T(8,128)(2,1)} %refs_2_.1, bf16[512,896]{1,0:T(8,128)(2,1)} %refs_3_.1), custom_call_target="tpu_custom_call" | custom-call | tf_op jit(solution)/shard_map/pallas_call | solution.py:224
  125.7 2.2 %copy.10 = bf16[512,896]{1,0:T(8,128)(2,1)} copy(bf16[512,896]{1,0:T(8,128)(2,1)} %get-tuple-element.12) | data formatting | bytes 1835008
  127.8 2.2 %copy.11 = bf16[512,896]{1,0:T(8,128)(2,1)} copy(bf16[512,896]{1,0:T(8,128)(2,1)} %get-tuple-element.13) | data formatting | bytes 1835008
  130.0 1.8 %copy.12 = bf16[256,896]{1,0:T(8,128)(2,1)} copy(bf16[256,896]{1,0:T(8,128)(2,1)} %get-tuple-element.14) | data formatting | bytes 917504

commit v19 on v16

--- a/solution.py
+++ b/solution.py
@@ -143,17 +143,22 @@
     for d in pending + [n_steps]:
         partial(d)
 
-    for k in order:
-        w_copies[k].wait_recv()
-        fwd_w(k)
     outgoing = []
-    for k in order:
+
+    def send_partial(k):
         p = (chip + k) % n_chip
         send = pltpu.make_async_remote_copy(
             part_v.at[p], recv_v.at[chip], s_send.at[k], s_recv.at[k],
             device_id=(p, core, ten), device_id_type=MESH)
         send.start()
         outgoing.append(send)
+
+    send_partial(order[0])
+    for k in order:
+        w_copies[k].wait_recv()
+        fwd_w(k)
+    for k in order[1:]:
+        send_partial(k)
 
     own_w.wait()
     for k in order:

time: 131 us -> 132 us (level)
    pallas_call x1, Pallas kernels: 123 us -> 124 us  [body(): pl.pallas_call(lambda *refs: _fused_kernel(n_chip, n_lo, min(128, seq_row...]
where the time goes in v19:
time: 132 us; the launch traced here: 130 us
  Pallas kernels  124 us (94%)
  local copies, waits for them, and re-layouts  5.17 us (4%)
    pallas_call x1, Pallas kernels, body(): pl.pallas_call(lambda *refs: _fused_kernel(n_chip, n_lo, min(128, seq_row...  124 us
    unnamed x5, local copies, waits for them, and re-layouts  5.17 us

profile of v19, /device:TPU:26, one launch (start us, length us, event | category | flops | bytes accessed | tf_op | source)
XLA Modules:
  0.0 130.2 jit_solution(11554462753643355534)
XLA Ops:
  0.6 124.4 %shard_map.67 = (bf16[512,896]{1,0:T(8,128)(2,1)}, bf16[512,896]{1,0:T(8,128)(2,1)}, bf16[256,896]{1,0:T(8,128)(2,1)}, bf16[8,2,512,256]{3,2,1,0:T(8,128)(2,1)},...) custom-call(bf16[512,256]{1,0:T(8,128)(2,1)} %refs_0_.1, bf16[256,896]{1,0:T(8,128)(2,1)} %refs_1_.1, ...), custom_call_target="tpu_custom_call" | custom-call | tf_op jit(solution)/shard_map/pallas_call | solution.py:222
  125.1 0.0 copy-start
  125.1 2.2 %copy.10 = bf16[512,896]{1,0:T(8,128)(2,1)} copy(bf16[512,896]{1,0:T(8,128)(2,1)} %get-tuple-element.12) | data formatting | bytes 1835008
  127.3 2.2 %copy.11 = bf16[512,896]{1,0:T(8,128)(2,1)} copy(bf16[512,896]{1,0:T(8,128)(2,1)} %get-tuple-element.13) | data formatting | bytes 1835008
  129.5 0.0 copy-done
  129.5 0.8 copy.12
Async XLA Ops:
  125.1 4.4 %copy-start = (bf16[256,896]{1,0:T(8,128)(2,1)S(1)}, bf16[256,896]{1,0:T(8,128)(2,1)}, u32[]{:S(2)}) copy-start(bf16[256,896]{1,0:T(8,128)(2,1)} %get-tuple-element.14) | copy-start | bytes 1376260

commit v20 on v16

--- a/solution.py
+++ b/solution.py
@@ -18,7 +18,7 @@
 
 
 def _fused_kernel(n_chip, n_lo, tile, grad_scale, og_ref, w_ref, gate_hbm, up_hbm,
-                  gate_out, up_out, down_out, rows_out, w_out, w_other,
+                  hg_out, down_out, rows_out, w_out, w_other,
                   x_send, x_recv, r_send, r_recv, l_send, l_recv, w_send, w_recv,
                   f_send, f_recv, fw_send, fw_recv, fr_send, fr_recv, own_sem,
                   rows_v, ro_v, hid_v, ho_v, load_sem, part_v, recv_v, s_send, s_recv,
@@ -178,14 +178,7 @@
         for r in range(n_plane):
             acc += jnp.dot(rows_v[r, rows, :], wv[r], preferred_element_type=jnp.float32)
             acc += jnp.dot(rows2_v[r, rows, :], wov[r], preferred_element_type=jnp.float32)
-        gate_wide = gate_v[rows, :].astype(jnp.float32)
-        up_wide = up_v[rows, :].astype(jnp.float32)
-        sigmoid_gate = jax.nn.sigmoid(gate_wide)
-        activated = gate_wide * sigmoid_gate
-        gate_out[rows, :] = (
-            acc * up_wide * sigmoid_gate * (1.0 + gate_wide * (1.0 - sigmoid_gate))
-        ).astype(gate_out.dtype)
-        up_out[rows, :] = (acc * activated).astype(up_out.dtype)
+        hg_out[rows, :] = acc
         return carry
 
     lax.fori_loop(0, gate_v.shape[0] // tile, one_tile, 0)
@@ -214,18 +207,17 @@
     n_plane = n_ten // n_lo
     vmem = pl.BlockSpec(memory_space=pltpu.VMEM)
     rows_shape = (n_plane, seq_rows, out_grad.shape[1])
-    gate_grad, up_grad, down_grad, _, _, _ = pl.pallas_call(
+    hidden_grad, down_grad, _, _, _ = pl.pallas_call(
         lambda *refs: _fused_kernel(n_chip, n_lo, min(128, seq_rows), grad_scale, *refs),
         out_shape=(
-            jax.ShapeDtypeStruct(gate_act.shape, jnp.bfloat16),
-            jax.ShapeDtypeStruct(up_act.shape, jnp.bfloat16),
+            jax.ShapeDtypeStruct(gate_act.shape, jnp.float32),
             jax.ShapeDtypeStruct(w_down.shape, jnp.bfloat16),
             jax.ShapeDtypeStruct((n_plane, n_lo, seq_rows, out_grad.shape[1]), out_grad.dtype),
             jax.ShapeDtypeStruct((n_chip, width, ff), w_down.dtype),
             jax.ShapeDtypeStruct((n_chip, width, ff), w_down.dtype),
         ),
         in_specs=[ANY, ANY, ANY, ANY],
-        out_specs=(vmem, vmem, vmem, ANY, ANY, ANY),
+        out_specs=(vmem, vmem, ANY, ANY, ANY),
         scratch_shapes=[pltpu.SemaphoreType.DMA((1,)), pltpu.SemaphoreType.DMA((1,)),
                         pltpu.SemaphoreType.DMA((n_plane // 2,)),
                         pltpu.SemaphoreType.DMA((n_plane // 2,)),
@@ -253,6 +245,14 @@
         compiler_params=pltpu.CompilerParams(collective_id=0, has_side_effects=True,
                                              vmem_limit_bytes=56 * 1024 * 1024),
     )(out_grad, w_down, gate_act, up_act)
+    gate_wide = gate_act.astype(jnp.float32)
+    up_wide = up_act.astype(jnp.float32)
+    sigmoid_gate = jax.nn.sigmoid(gate_wide)
+    activated = gate_wide * sigmoid_gate
+    gate_grad = (
+        hidden_grad * up_wide * sigmoid_gate * (1.0 + gate_wide * (1.0 - sigmoid_gate))
+    ).astype(jnp.bfloat16)
+    up_grad = (hidden_grad * activated).astype(jnp.bfloat16)
     return (gate_grad, up_grad, down_grad)
 
 

time: 131 us -> 131 us (level)
  local copies, waits for them, and re-layouts: 5.17 us -> 0.78 us
  other arithmetic: 0 us -> 3.69 us
    unnamed x5 -> x7, local copies, waits for them, and re-layouts: 5.17 us -> 0.78 us
    convert_element_type x0 -> x1, other arithmetic: none -> 3.69 us  [body(): up_grad = (hidden_grad * activated).astype(jnp.bfloat16)]
where the time goes in v20:
time: 131 us; the launch traced here: 128 us
  Pallas kernels  123 us (94%)
  other arithmetic  3.69 us (3%)
    pallas_call x1, Pallas kernels, body(): pl.pallas_call(lambda *refs: _fused_kernel(n_chip, n_lo, min(128, seq_row...  123 us
    convert_element_type x1, other arithmetic, body(): up_grad = (hidden_grad * activated).astype(jnp.bfloat16)  3.69 us

profile of v20, /device:TPU:26, one launch (start us, length us, event | category | flops | bytes accessed | tf_op | source)
XLA Modules:
  0.0 128.0 jit_solution(294636366775688091)
XLA Ops:
  0.6 0.0 copy-start.1
  0.6 0.0 copy-start
  0.7 122.9 %shard_map.67 = (f32[512,896]{1,0:T(8,128)}, bf16[256,896]{1,0:T(8,128)(2,1)}, bf16[8,2,512,256]{3,2,1,0:T(8,128)(2,1)}, bf16[8,256,896]{2,1,0:T(8,128)(2,1)}, bf16[8,256,896]{2,1,0:T(8,128)(2,1)}) custom-call(bf16[512,256]{1,0:T(8,128)(2,1)} %refs_0_.1, bf16[256,896]{1,0:T(8,128)(2,1)} %refs_1_.1, bf16[512,896]{1,0:T(8,128)(2,1)} %refs_2_.1, ...), custom_call_target="tpu_custom_call" | custom-call | tf_op jit(solution)/shard_map/pallas_call | solution.py:210
  123.5 0.0 copy-done.1
  123.5 0.0 copy-done
  123.5 0.0 copy-start.2
  123.5 3.7 %fusion.7 = (bf16[512,896]{1,0:T(8,128)(2,1)}, bf16[512,896]{1,0:T(8,128)(2,1)}) fusion(f32[512,896]{1,0:T(8,128)} %get-tuple-element.5, bf16[512,896]{1,0:T(8,128)(2,1)S(1)} %copy-done, bf16[512,896]{1,0:T(8,128)(2,1)S(1)} %copy-done.1), kind=kLoop, calls=%fused_computation.10 | loop fusion | flops 6881280 | bytes 5505024 | tf_op jit(solution)/shard_map/convert_element_type | solution.py:255
  127.2 0.0 copy-done.2
  127.2 0.8 copy.8
Async XLA Ops:
  0.6 122.9 %copy-start.1 = (bf16[512,896]{1,0:T(8,128)(2,1)S(1)}, bf16[512,896]{1,0:T(8,128)(2,1)}, u32[]{:S(2)}) copy-start(bf16[512,896]{1,0:T(8,128)(2,1)} %refs_3_.1) | copy-start | bytes 2752516
  0.6 122.9 %copy-start = (bf16[512,896]{1,0:T(8,128)(2,1)S(1)}, bf16[512,896]{1,0:T(8,128)(2,1)}, u32[]{:S(2)}) copy-start(bf16[512,896]{1,0:T(8,128)(2,1)} %refs_2_.1) | copy-start | bytes 2752516
  123.5 3.7 %copy-start.2 = (bf16[256,896]{1,0:T(8,128)(2,1)S(1)}, bf16[256,896]{1,0:T(8,128)(2,1)}, u32[]{:S(2)}) copy-start(bf16[256,896]{1,0:T(8,128)(2,1)} %get-tuple-element.14) | copy-start | bytes 1376260

commit v21 on v20

--- a/solution.py
+++ b/solution.py
@@ -190,7 +190,7 @@
     total = part_v[chip].astype(jnp.float32)
     for k in range(1, n_chip):
         total += recv_v[(chip + k) % n_chip].astype(jnp.float32)
-    down_out[...] = (total * grad_scale).astype(down_out.dtype)
+    down_out[...] = total
 
 
 def body(out_grad, gate_act, up_act, w_down):
@@ -207,11 +207,11 @@
     n_plane = n_ten // n_lo
     vmem = pl.BlockSpec(memory_space=pltpu.VMEM)
     rows_shape = (n_plane, seq_rows, out_grad.shape[1])
-    hidden_grad, down_grad, _, _, _ = pl.pallas_call(
+    hidden_grad, summed, _, _, _ = pl.pallas_call(
         lambda *refs: _fused_kernel(n_chip, n_lo, min(128, seq_rows), grad_scale, *refs),
         out_shape=(
             jax.ShapeDtypeStruct(gate_act.shape, jnp.float32),
-            jax.ShapeDtypeStruct(w_down.shape, jnp.bfloat16),
+            jax.ShapeDtypeStruct(w_down.shape, jnp.float32),
             jax.ShapeDtypeStruct((n_plane, n_lo, seq_rows, out_grad.shape[1]), out_grad.dtype),
             jax.ShapeDtypeStruct((n_chip, width, ff), w_down.dtype),
             jax.ShapeDtypeStruct((n_chip, width, ff), w_down.dtype),
@@ -253,6 +253,7 @@
         hidden_grad * up_wide * sigmoid_gate * (1.0 + gate_wide * (1.0 - sigmoid_gate))
     ).astype(jnp.bfloat16)
     up_grad = (hidden_grad * activated).astype(jnp.bfloat16)
+    down_grad = (summed * grad_scale).astype(jnp.bfloat16)
     return (gate_grad, up_grad, down_grad)
 
 

time: 131 us -> 131 us (level)
  no operation moved by 1% of the time
where the time goes in v21:
time: 131 us; the launch traced here: 128 us
  Pallas kernels  123 us (94%)
  other arithmetic  4.56 us (3%)
    pallas_call x1, Pallas kernels, body(): pl.pallas_call(lambda *refs: _fused_kernel(n_chip, n_lo, min(128, seq_row...  123 us
    convert_element_type x1, other arithmetic, body(): up_grad = (hidden_grad * activated).astype(jnp.bfloat16)  3.72 us

profile of v21, /device:TPU:26, one launch (start us, length us, event | category | flops | bytes accessed | tf_op | source)
XLA Modules:
  0.0 128.2 jit_solution(738466929327148056)
XLA Ops:
  0.6 0.0 copy-start.1
  0.6 0.0 copy-start
  0.7 123.0 %shard_map.67 = (f32[512,896]{1,0:T(8,128)}, f32[256,896]{1,0:T(8,128)}, bf16[8,2,512,256]{3,2,1,0:T(8,128)(2,1)}, bf16[8,256,896]{2,1,0:T(8,128)(2,1)}, bf16[8,256,896]{2,1,0:T(8,128)(2,1)}) custom-call(bf16[512,256]{1,0:T(8,128)(2,1)} %refs_0_.1, bf16[256,896]{1,0:T(8,128)(2,1)} %refs_1_.1, bf16[512,896]{1,0:T(8,128)(2,1)} %refs_2_.1, bf16[512,896]{1,0:T(8,128)(2,1)} %refs_3_.1), custom_call_target="tpu_custom_call" | custom-call | tf_op jit(solution)/shard_map/pallas_call | solution.py:210
  123.6 0.0 copy-done.1
  123.6 0.0 copy-done
  123.6 0.0 copy-start.2
  123.7 3.7 %fusion.7 = (bf16[512,896]{1,0:T(8,128)(2,1)}, bf16[512,896]{1,0:T(8,128)(2,1)}) fusion(f32[512,896]{1,0:T(8,128)} %get-tuple-element.5, bf16[512,896]{1,0:T(8,128)(2,1)S(1)} %copy-done, bf16[512,896]{1,0:T(8,128)(2,1)S(1)} %copy-done.1), kind=kLoop, calls=%fused_computation.10 | loop fusion | flops 6881280 | bytes 5505024 | tf_op jit(solution)/shard_map/convert_element_type | solution.py:255
  127.4 0.0 copy-done.2
  127.4 0.8 multiply_convert_fusion
Async XLA Ops:
  0.6 123.0 %copy-start.1 = (bf16[512,896]{1,0:T(8,128)(2,1)S(1)}, bf16[512,896]{1,0:T(8,128)(2,1)}, u32[]{:S(2)}) copy-start(bf16[512,896]{1,0:T(8,128)(2,1)} %refs_3_.1) | copy-start | bytes 2752516
  0.6 123.0 %copy-start = (bf16[512,896]{1,0:T(8,128)(2,1)S(1)}, bf16[512,896]{1,0:T(8,128)(2,1)}, u32[]{:S(2)}) copy-start(bf16[512,896]{1,0:T(8,128)(2,1)} %refs_2_.1) | copy-start | bytes 2752516
  123.6 3.7 %copy-start.2 = (f32[256,896]{1,0:T(8,128)S(1)}, f32[256,896]{1,0:T(8,128)}, u32[]{:S(2)}) copy-start(f32[256,896]{1,0:T(8,128)} %get-tuple-element.6) | copy-start | bytes 2752516
